TPU v7x, 32 devices: a whole 2x2x4 slice. The times are simulated.
32 devices in a mesh: rep: 2 (over y), tile: 16 (over z, x, core).
Axes of the slice: x: 2, y: 2, z: 4, core: 2. Of those that a mesh axis runs over, the one named last changes fastest.
Arguments:
- inputs: bfloat16 [32, 32, 32, 320], P(('rep', 'tile')), parts along dimension 0, may hold values from -6 to 6
- out_grad: bfloat16 [32, 32, 32, 320], P(('rep', 'tile')), parts along dimension 0, may hold values from -6 to 6
- weight: bfloat16 [921600], P('tile'), may hold values from -0.109375 to 0.109375
- neighbours: int32 [16, 8], replicated, may hold values from 0 to 15, as said below
- orients: int32 [16, 8], replicated, may hold values from 0 to 3
Outputs:
- input_grad: bfloat16 [32, 32, 32, 320], P(('rep', 'tile')), parts along dimension 0
- weight_grad: float32 [1843200], P(('rep', 'tile')), parts along dimension 0
There are 2 independent parts, one for each index of `rep`. A program takes and returns all parts, laid end to end along the dimension named above; an argument that names none is the same for every part. Nothing has to cross between parts.
Inputs may be any that keep to these rules, and one draw needn't show every extreme that they name: The tiles form 16 // 16 faces of 4 x 4 tiles, each face at 16 consecutive indices. A tile's eight neighbours are eight different tiles, none of them the tile itself.
All inputs are finite; a program needn't handle non-finite values.
Results may differ from a plain program's by a relative error of at most 0.001.
Values may be sent and summed in bfloat16 or wider, within the bound.
No kernel may reach another device: no remote copies, remote signals or barrier semaphores. Data moves between devices by JAX's collectives and lax.ppermute only.
A program may use at most 64 MiB of HBM per device.

v0:
```python
import math

import jax
import jax.numpy as jnp
from jax import lax
from jax.sharding import PartitionSpec as P


def turn_once(borders, corners):
    new_borders = jnp.stack([borders[3], borders[2], borders[0][::-1], borders[1][::-1]])
    new_corners = jnp.stack([corners[1], corners[3], corners[0], corners[2]])
    return (new_borders, new_corners)


def all_turns(borders, corners):
    all_borders = [borders]
    all_corners = [corners]
    for count in range(3):
        next_borders, next_corners = turn_once(all_borders[-1], all_corners[-1])
        all_borders.append(next_borders)
        all_corners.append(next_corners)
    return (all_borders, all_corners)


def turned(borders, corners, turns):
    all_borders, all_corners = all_turns(borders, corners)
    return (jnp.stack(all_borders)[turns], jnp.stack(all_corners)[turns])


def taps_product(window, matrix):
    return lax.dot_general(
        window, matrix, (((1,), (1,)), ((), ())), preferred_element_type=jnp.float32
    )


def taps_grad(flat_in, window):
    return lax.dot_general(
        flat_in, window, (((0,), (0,)), ((), ())), preferred_element_type=jnp.float32
    )


def full_conv(padded, flat_in, kernel, side, width):
    total = jnp.zeros((side * side, width), jnp.float32)
    grads = []
    for row_tap in range(3):
        for col_tap in range(3):
            window = padded[
                2 - row_tap : 2 - row_tap + side, 2 - col_tap : 2 - col_tap + side, :
            ].reshape(side * side, width)
            total = total + taps_product(window, kernel[row_tap, col_tap])
            grads.append(taps_grad(flat_in, window))
    return (total.reshape(side, side, width), jnp.stack(grads).reshape(3, 3, width, width))


def per_device(inputs, out_grad, weight, neighbours, orients):
    side = inputs.shape[1]
    width = inputs.shape[3]
    tiles_all = lax.axis_size("tile") * inputs.shape[0]
    own_grad = out_grad[0]
    own_in = inputs[0]
    flat_in = own_in.reshape(side * side, width)
    kernel = lax.all_gather(weight, "tile", axis=0, tiled=True).reshape(3, 3, width, width)
    my_index = lax.axis_index("tile")
    my_nbrs = lax.dynamic_index_in_dim(neighbours, my_index, 0, keepdims=False)
    my_turns = lax.dynamic_index_in_dim(orients, my_index, 0, keepdims=False)
    borders = jnp.stack([own_grad[0], own_grad[-1], own_grad[:, 0], own_grad[:, -1]])[None]
    corners = jnp.stack([own_grad[0, 0], own_grad[0, -1], own_grad[-1, 0], own_grad[-1, -1]])[None]
    edge_pick = [1, 0, 3, 2]
    corner_pick = [3, 2, 1, 0]
    start_edges = jnp.zeros((4, side, width), jnp.bfloat16)
    start_corners = jnp.zeros((4, width), jnp.bfloat16)
    rim_edges = start_edges
    rim_corners = start_corners
    piece_borders = lax.all_gather(borders, "tile", axis=0, tiled=True)
    piece_corners = lax.all_gather(corners, "tile", axis=0, tiled=True)
    count = piece_borders.shape[0]
    new_edges = []
    new_corners = []
    for direction in range(8):
        local = my_nbrs[direction]
        inside = jnp.logical_and(local >= 0, local < count)
        place = jnp.clip(local, 0, count - 1)
        got_b, got_c = turned(piece_borders[place], piece_corners[place], my_turns[direction])
        if direction < 4:
            new_edges.append(jnp.where(inside, got_b[edge_pick[direction]], rim_edges[direction]))
        else:
            new_corners.append(
                jnp.where(inside, got_c[corner_pick[direction - 4]], rim_corners[direction - 4])
            )
    rim_edges = jnp.stack(new_edges)
    rim_corners = jnp.stack(new_corners)
    top_row = jnp.concatenate([rim_corners[0][None], rim_edges[0], rim_corners[1][None]], axis=0)
    bottom_row = jnp.concatenate([rim_corners[2][None], rim_edges[1], rim_corners[3][None]], axis=0)
    middle = jnp.concatenate([rim_edges[2][:, None], own_grad, rim_edges[3][:, None]], axis=1)
    extended = jnp.concatenate([top_row[None], middle, bottom_row[None]], axis=0)
    result, grads = full_conv(extended, flat_in, kernel, side, width)
    summed = lax.psum_scatter(
        grads.reshape(9 * width * width), "tile", scatter_dimension=0, tiled=True
    )
    scale = 1.0 / math.sqrt(tiles_all * side * side)
    input_grad = result.astype(jnp.bfloat16).reshape(1, side, side, width)
    return (input_grad, summed * scale)


def solution(mesh):
    in_specs = (
        P(("rep", "tile"), None, None, None),
        P(("rep", "tile"), None, None, None),
        P("tile"),
        P(),
        P(),
    )
    out_specs = (P(("rep", "tile"), None, None, None), P(("rep", "tile")))
    return jax.shard_map(
        per_device, mesh=mesh, in_specs=in_specs, out_specs=out_specs, check_vma=False
    )
```

profile of v0, /device:TPU:0, one launch (start us, length us, event | category | flops | bytes accessed | tf_op | source)
XLA Modules:
  0.0 220.9 jit_solution(9280278403318607073)
XLA Ops:
  8.0 1.1 fusion.59
  9.9 1.7 reshape.324
  39.6 23.2 %all-gather.2 = bf16[16,4,320]{2,1,0:T(4,128)(2,1)S(1)} all-gather(bf16[1,4,320]{2,1,0:T(4,128)(2,1)S(1)} %maximum_bitcast_fusion.14), channel_id=3, replica_groups=mesh['rep'=2,'tile'=16] {'tile'}, dimensions={0}, use_global_device_ids=true | all-gather | bytes 43520 | tf_op jit(solution)/shard_map/all_gather | solution.py:75
  67.8 1.3 dynamic-slice.1
  70.3 1.1 dynamic-slice_bitcast_fusion.13
  71.4 1.1 constant_dynamic-slice_fusion.30
  77.3 1.5 fusion.9
  78.8 1.3 fusion.8
  80.1 1.3 fusion.7
  81.5 1.3 fusion.6
  82.8 1.3 fusion.5
  84.2 1.3 fusion.4
  86.1 1.5 fusion.3
  87.6 1.4 fusion.2
  89.0 1.4 fusion.1
  90.3 6.0 %copy.36 = f32[9,320,320]{2,1,0:T(8,128)} copy(f32[9,320,320]{1,2,0:T(8,128)} %fusion.1) | data formatting | bytes 7372800 | tf_op jit(solution)/shard_map/stack | solution.py:52
  96.3 5.8 %reshape_reshape.3 = f32[921600]{0:T(1024)} reshape(f32[9,320,320]{2,1,0:T(8,128)} %copy.36) | data formatting | bytes 7372800 | tf_op jit(solution)/shard_map/reshape;reshape | solution.py:98
  102.6 27.1 %reduce = bf16[16,57600]{1,0:T(8,128)(2,1)S(1)} reduce(bf16[16,1,57600]{2,1,0:T(2,128)(2,1)} %all-gather.9.cloned.1.call-done, bf16[]{:T(256)} %constant.72), dimensions={1}, to_apply=%all-gather.3.reduce_sub_computation | reduce | bytes 3686402 | tf_op jit(solution)/shard_map/all_gather | solution.py:62
  129.7 4.0 %reshape.311 = bf16[3,3,320,320]{3,2,1,0:T(8,128)(2,1)} reshape(bf16[16,57600]{1,0:T(8,128)(2,1)S(1)} %reduce) | data formatting | bytes 3686400 | tf_op jit(solution)/shard_map/reshape | solution.py:62
  133.7 1.9 fusion.11
  135.7 1.8 convolution_add_fusion.7
  144.3 1.2 copy.34
  145.4 67.1 %all-reduce.3.cloned.1.call-done = f32[921600]{0:T(1024)} async-done(((f32[921600]{0:T(1024)}), f32[921600]{0:T(1024)}) %all-reduce.3.cloned.1.call-update) | async-done | bytes 3686416
  212.6 1.8 dynamic-slice_multiply_fusion
  (99 shorter events, 17.2 us)
Async XLA Ops:
  7.2 70.1 %copy-start = (bf16[1,32,32,320]{3,2,1,0:T(8,128)(2,1)S(1)}, bf16[1,32,32,320]{3,2,1,0:T(8,128)(2,1)}, u32[]{:S(2)}) copy-start(bf16[1,32,32,320]{3,2,1,0:T(8,128)(2,1)} %param.5) | copy-start | bytes 1966084
  7.2 63.1 %all-gather.7.cloned.1.call-start = ((), (), s32[]{:S(2)}) async-start(), calls=%async_computation | async-start | bytes 1671168 | tf_op jit(solution)/shard_map/all_gather | solution.py:74
  9.9 92.8 %all-gather.9.cloned.1.call-start = ((), (), s32[]{:S(2)}) async-start(), calls=%async_computation.1 | async-start | bytes 3916800 | tf_op jit(solution)/shard_map/all_gather | solution.py:62
  11.7 200.9 %all-reduce.3.cloned.1.call-start = ((), (), s32[]{:S(2)}) async-start(), calls=%async_computation.2 | async-start | bytes 7372800
  74.1 1.1 copy-start.1
  75.9 5.6 %copy-start.12 = (bf16[32,32,320]{2,1,0:T(8,128)(2,1)}, bf16[32,32,320]{2,1,0:T(8,128)(2,1)S(1)}, u32[]{:S(2)}) copy-start(bf16[32,32,320]{2,1,0:T(8,128)(2,1)S(1)} %get-tuple-element.49) | copy-start | bytes 1966084
  75.9 8.2 %copy-start.10 = (bf16[32,32,320]{2,1,0:T(8,128)(2,1)}, bf16[32,32,320]{2,1,0:T(8,128)(2,1)S(1)}, u32[]{:S(2)}) copy-start(bf16[32,32,320]{2,1,0:T(8,128)(2,1)S(1)} %get-tuple-element.48) | copy-start | bytes 1966084
  77.2 2.9 %copy-start.5 = (bf16[32,32,320]{2,1,0:T(8,128)(2,1)}, bf16[32,32,320]{2,1,0:T(8,128)(2,1)S(1)}, u32[]{:S(2)}) copy-start(bf16[32,32,320]{2,1,0:T(8,128)(2,1)S(1)} %get-tuple-element.44) | copy-start | bytes 1966084
  77.3 2.9 %copy-start.16 = (bf16[32,32,320]{2,1,0:T(8,128)(2,1)}, bf16[32,32,320]{2,1,0:T(8,128)(2,1)S(1)}, u32[]{:S(2)}) copy-start(bf16[32,32,320]{2,1,0:T(8,128)(2,1)S(1)} %get-tuple-element.45) | copy-start | bytes 1966084
  77.3 2.9 %copy-start.3 = (bf16[32,32,320]{2,1,0:T(8,128)(2,1)}, bf16[32,32,320]{2,1,0:T(8,128)(2,1)S(1)}, u32[]{:S(2)}) copy-start(bf16[32,32,320]{2,1,0:T(8,128)(2,1)S(1)} %get-tuple-element.43) | copy-start | bytes 1966084
  86.0 2.9 %copy-start.6 = (bf16[32,32,320]{2,1,0:T(8,128)(2,1)}, bf16[32,32,320]{2,1,0:T(8,128)(2,1)S(1)}, u32[]{:S(2)}) copy-start(bf16[32,32,320]{2,1,0:T(8,128)(2,1)S(1)} %get-tuple-element.41) | copy-start | bytes 1966084
  86.0 2.9 %copy-start.8 = (bf16[32,32,320]{2,1,0:T(8,128)(2,1)}, bf16[32,32,320]{2,1,0:T(8,128)(2,1)S(1)}, u32[]{:S(2)}) copy-start(bf16[32,32,320]{2,1,0:T(8,128)(2,1)S(1)} %get-tuple-element.42) | copy-start | bytes 1966084
  86.1 2.9 %copy-start.14 = (bf16[32,32,320]{2,1,0:T(8,128)(2,1)}, bf16[32,32,320]{2,1,0:T(8,128)(2,1)S(1)}, u32[]{:S(2)}) copy-start(bf16[32,32,320]{2,1,0:T(8,128)(2,1)S(1)} %get-tuple-element.40) | copy-start | bytes 1966084
  133.7 2.0 copy-start.2
  135.7 1.8 copy-start.4
  137.5 1.1 copy-start.13
  139.2 1.1 copy-start.11
  140.3 1.1 copy-start.9
  141.5 1.1 copy-start.7
  142.6 1.1 copy-start.15
Sparse Core Ops, SparseCore 0:
  10.9 42.3 all-gather.6
  56.1 46.4 all-gather.8
  106.3 106.2 all-reduce.2
where the time goes:
time: 222 us; the launch traced here: 221 us
  waiting for transfers between devices  67.7 us (30%)
  between operations  45.1 us (20%)
  local copies, waits for them, and re-layouts  33.2 us (15%)
  other arithmetic  31.7 us (14%)
  blocking collectives  23.2 us (10%)
  matrix products  19.8 us (9%)
    unnamed x4, waiting for transfers between devices  67.2 us
    all_gather x1, other arithmetic, per_device(): lax.all_gather(weight, 'tile', axis=0, tiled=True)  27.1 us
    all_gather x1, blocking collectives, per_device(): piece_corners = lax.all_gather(corners, 'tile', axis=0, tiled=True)  23.2 us
    dot_general x9, matrix products, taps_grad(): lax.dot_general(flat_in, window, (((0,), (0,)), ((), ())), preferred_elem...  12.5 us
    dot_general x9, matrix products, taps_product(): lax.dot_general(window, matrix, (((1,), (1,)), ((), ())), preferred_eleme...  7.37 us
    unnamed x37, local copies, waits for them, and re-layouts  6.52 us
    another operation x1, local copies, waits for them, and re-layouts, full_conv(): jnp.stack(grads).reshape(3, 3, width, width)  5.98 us
    another operation x1, local copies, waits for them, and re-layouts, per_device(): grads.reshape(9 * width * width)  5.79 us
  transfers between devices with their start and end apart: 3, of which 2 were waited for; matrix products, arithmetic and copies ran while one was open for 35% of the time, Pallas kernels for 0%

commit v1 on v0

v1 whole, which is shorter than its diff:
```python
import functools
import math

import jax
import jax.numpy as jnp
from jax import lax
from jax.experimental import pallas as pl
from jax.experimental.pallas import tpu as pltpu
from jax.sharding import PartitionSpec as P

LANES = 128
GROUP = 96
VMEM = pl.BlockSpec(memory_space=pltpu.VMEM)
SMEM = pl.BlockSpec(memory_space=pltpu.SMEM)
STRIP_OF = (
    (2, 4, 1, 7),
    (0, 6, 3, 5),
    (6, 3, 5, 0),
    (4, 1, 7, 2),
    (3, 2, 0, 1),
    (2, 0, 1, 3),
    (1, 3, 2, 0),
    (0, 1, 3, 2),
)


def strip_code(direction):
    return sum(strip << (4 * turn) for turn, strip in enumerate(STRIP_OF[direction]))


def params(megabytes):
    return pltpu.CompilerParams(vmem_limit_bytes=megabytes << 20)


def pack_borders(side, count, me_ref, nbr_ref, turn_ref, grad_ref, slots_ref, strips_ref):
    pixels = side * side
    row = lax.broadcasted_iota(jnp.int32, (8 * side, 1), 0)
    strip = row // side
    step = row % side
    along = jnp.where(strip % 2 == 1, side - 1 - step, step)
    edge = strip // 2
    target = jnp.where(
        edge == 0,
        along,
        jnp.where(
            edge == 1,
            (side - 1) * side + along,
            jnp.where(edge == 2, along * side, along * side + side - 1),
        ),
    )
    column = lax.broadcasted_iota(jnp.int32, (8 * side, pixels), 1)
    pick = jnp.where(column == target, 1.0, 0.0).astype(jnp.bfloat16)
    picked = jnp.dot(pick, grad_ref[...], preferred_element_type=jnp.float32)
    strips_ref[...] = picked.astype(jnp.bfloat16).reshape(strips_ref.shape)
    me = me_ref[0]

    def fill(dest, carry):
        which = jnp.int32(0)
        for direction in range(8):
            turn = turn_ref[dest * 8 + direction]
            found = (strip_code(direction) >> (4 * turn)) & 15
            which = jnp.where(nbr_ref[dest * 8 + direction] == me, found, which)
        slots_ref[dest] = strips_ref[which]
        return carry

    lax.fori_loop(0, count, fill, 0)


def exponent_of(peak):
    return jnp.maximum(jnp.ceil(jnp.log2(jnp.maximum(peak, 1e-30))), -90.0)


def coded(block):
    power = exponent_of(jnp.max(jnp.abs(block), axis=0, keepdims=True))
    steps = jnp.round(block * (jnp.exp2(15.0 - power) * 0.999)).astype(jnp.int32)
    return steps, power.astype(jnp.int32)


def write_coded(out_ref, block, rows):
    steps, power = coded(block)
    row = lax.broadcasted_iota(jnp.int32, block.shape, 0)
    out_ref[...] = jnp.where(row == rows, power, steps).astype(jnp.int16)


def read_coded(steps, rows):
    whole = steps.astype(jnp.int32)
    power = whole[rows : rows + 1].astype(jnp.float32)
    row = lax.broadcasted_iota(jnp.int32, whole.shape, 0)
    value = whole.astype(jnp.float32) * (jnp.exp2(power - 15.0) * (1.0 / 0.999))
    return jnp.where(row == rows, 0.0, value)


def plain_weight_term(
    side, width,
    me_ref, nbr_ref, in_ref, grad_ref, slots_ref,
    left_ref, mid_ref, right_ref, acc_ref,
    in_t_ref,
):
    me = me_ref[0]
    pixels = side * side
    lanes = left_ref.shape[1]
    spare = lanes - width
    own = grad_ref[...].astype(jnp.float32)
    own = jnp.concatenate([own, jnp.zeros((pixels, spare), jnp.float32)], axis=1)
    rims = []
    for direction in range(8):
        piece = slots_ref[nbr_ref[me * 8 + direction]].astype(jnp.float32)
        rims.append(jnp.concatenate([piece, jnp.zeros((side, spare), jnp.float32)], axis=1))
    north, south, west, east = rims[:4]
    nw, ne, sw, se = [rim[0:1] for rim in rims[4:]]
    mid_ref[0:side] = north.astype(jnp.bfloat16)
    mid_ref[side : side + pixels] = own.astype(jnp.bfloat16)
    mid_ref[side + pixels :] = south.astype(jnp.bfloat16)
    place = lax.broadcasted_iota(jnp.int32, (side, side, lanes), 1)
    strip_place = lax.broadcasted_iota(jnp.int32, (side, lanes), 0)
    tall = (side, side, lanes)
    moved = pltpu.roll(own, 1, 0).reshape(tall)
    moved = jnp.where(place == 0, west.reshape(side, 1, lanes), moved)
    left_ref[side : side + pixels] = moved.reshape(pixels, lanes).astype(jnp.bfloat16)
    moved = pltpu.roll(own, pixels - 1, 0).reshape(tall)
    moved = jnp.where(place == side - 1, east.reshape(side, 1, lanes), moved)
    right_ref[side : side + pixels] = moved.reshape(pixels, lanes).astype(jnp.bfloat16)
    for start, rim, first, last in ((0, north, nw, ne), (side + pixels, south, sw, se)):
        moved = jnp.where(strip_place == 0, first, pltpu.roll(rim, 1, 0))
        left_ref[start : start + side] = moved.astype(jnp.bfloat16)
        moved = jnp.where(strip_place == side - 1, last, pltpu.roll(rim, side - 1, 0))
        right_ref[start : start + side] = moved.astype(jnp.bfloat16)
    in_t_ref[...] = in_ref[...].T
    shifted = (right_ref, mid_ref, left_ref)
    for row_tap in range(3):
        for col_tap in range(3):
            window = shifted[col_tap][(2 - row_tap) * side : (2 - row_tap) * side + pixels]
            tap = 3 * row_tap + col_tap
            term = jnp.dot(in_t_ref[...], window, preferred_element_type=jnp.float32)
            for part in range(3):
                acc_ref[part, tap * width : (tap + 1) * width] = term[
                    :, part * LANES : (part + 1) * LANES
                ]


def weight_term(
    side, width, chips, pairs,
    me_ref, nbr_ref, in_ref, grad_ref, slots_ref,
    left_ref, mid_ref, right_ref, keep_ref, send_ref,
    in_t_ref, acc_ref, pack_ref,
):
    plain_weight_term(
        side, width,
        me_ref, nbr_ref, in_ref, grad_ref, slots_ref,
        left_ref, mid_ref, right_ref, acc_ref,
        in_t_ref,
    )
    half = LANES // 2
    low = lax.broadcasted_iota(jnp.int32, (pairs, LANES), 1) < half
    for shard in range(2 * chips):
        base = shard * 2 * pairs
        even = pl.ds(base, pairs, stride=2)
        odd = pl.ds(base + 1, pairs, stride=2)
        e0, e1, e2 = [acc_ref[part, even] for part in range(3)]
        o0, o1, o2 = [pltpu.roll(acc_ref[part, odd], half, 1) for part in range(3)]
        groups = (e0, e1, jnp.where(low, e2, o0), jnp.where(low, o0, o1), jnp.where(low, o1, o2))
        for group, block in enumerate(groups):
            pack_ref[shard, group * GROUP : group * GROUP + pairs] = block
            pack_ref[shard, group * GROUP + pairs : (group + 1) * GROUP] = jnp.zeros(
                (GROUP - pairs, LANES), jnp.float32
            )
    core = me_ref[0] % 2
    for chip in range(chips):
        keep_ref[chip] = pack_ref[2 * chip + core]
        write_coded(send_ref.at[chip], pack_ref[2 * chip + 1 - core], pairs)


def pair_sum(pairs, chips, me_ref, keep_ref, got_ref, own_ref, *send_refs):
    chip = me_ref[0] // 2
    for offset in range(chips):
        dest = chip ^ offset
        total = keep_ref[dest] + read_coded(got_ref[dest], pairs)
        if offset == 0:
            own_ref[...] = total
        else:
            write_coded(send_refs[offset - 1], total, pairs)


def final_sum(pairs, scale, own_ref, *refs):
    got_refs, out_ref = refs[:-1], refs[-1]
    total = own_ref[...]
    for got_ref in got_refs:
        total = total + read_coded(got_ref[...], pairs)
    total = total * scale
    for group in range(5):
        out_ref[pl.ds(group, pairs, stride=5), :] = total[group * GROUP : group * GROUP + pairs]


def input_term(side, width, left_ref, mid_ref, right_ref, kernel_ref, out_ref):
    shifted = (right_ref, mid_ref, left_ref)
    chunk = side * side // 4
    for part in range(4):
        total = jnp.zeros((chunk, width), jnp.float32)
        for row_tap in range(3):
            for col_tap in range(3):
                start = (2 - row_tap) * side + part * chunk
                total = total + lax.dot_general(
                    shifted[col_tap][start : start + chunk, 0:width],
                    kernel_ref[3 * row_tap + col_tap],
                    (((1,), (1,)), ((), ())),
                    preferred_element_type=jnp.float32,
                )
        out_ref[part * chunk : (part + 1) * chunk] = total.astype(jnp.bfloat16)


def gather_kernel(weight, count, me):
    chips = count // 2
    piece = weight.reshape(1, -1, LANES)
    held = piece
    size = 1
    steps = []
    while size < chips:
        steps.append(size)
        size *= 2
    for step in reversed(steps):
        got = lax.ppermute(held, "tile", [(i, i ^ (2 * step)) for i in range(count)])
        held = jnp.concatenate([held, got], axis=0)
    other = lax.ppermute(held, "tile", [(i, i ^ 1) for i in range(count)])
    offsets = [0]
    for step in reversed(steps):
        offsets = offsets + [o ^ step for o in offsets]
    core = me % 2
    chip = me // 2
    first = jnp.where(core == 0, held, other)
    second = jnp.where(core == 0, other, held)
    both = jnp.stack([first, second], axis=1)
    place = jnp.asarray([offsets.index(o) for o in range(chips)], jnp.int32)
    order = place[jnp.arange(chips, dtype=jnp.int32) ^ chip]
    return both[order]


def fast_weight_grad(
    side, width, count, scale, tall, transposed, me_array, nbrs, flat_in, grad, slots
):
    chips = count // 2
    pairs = 9 * width * width // (2 * width * count)
    message = (5 * GROUP, LANES)
    left, mid, right, keep, send = pl.pallas_call(
        functools.partial(weight_term, side, width, chips, pairs),
        out_shape=(
            tall, tall, tall,
            jax.ShapeDtypeStruct((chips,) + message, jnp.float32),
            jax.ShapeDtypeStruct((chips,) + message, jnp.int16),
        ),
        in_specs=[SMEM, SMEM, VMEM, VMEM, VMEM],
        out_specs=(VMEM,) * 5,
        scratch_shapes=[
            transposed,
            pltpu.VMEM((3, 9 * width, LANES), jnp.float32),
            pltpu.VMEM((count,) + message, jnp.float32),
        ],
        compiler_params=params(56),
        name="weight_term",
    )(me_array, nbrs, flat_in, grad, slots)

    got = lax.ppermute(send, "tile", [(i, i ^ 1) for i in range(count)])
    own, *sends = pl.pallas_call(
        functools.partial(pair_sum, pairs, chips),
        out_shape=(jax.ShapeDtypeStruct(message, jnp.float32),)
        + (jax.ShapeDtypeStruct(message, jnp.int16),) * (chips - 1),
        in_specs=[SMEM, VMEM, VMEM],
        out_specs=(VMEM,) * chips,
        compiler_params=params(32),
        name="pair_sum",
    )(me_array, keep, got)
    gots = [
        lax.ppermute(sends[offset - 1], "tile", [(i, i ^ (2 * offset)) for i in range(count)])
        for offset in range(1, chips)
    ]
    weight_grad = pl.pallas_call(
        functools.partial(final_sum, pairs, scale),
        out_shape=jax.ShapeDtypeStruct((5 * pairs, LANES), jnp.float32),
        in_specs=[VMEM] * chips,
        out_specs=VMEM,
        compiler_params=params(32),
        name="final_sum",
    )(own, *gots)
    return left, mid, right, weight_grad.reshape(-1)


def per_device(inputs, out_grad, weight, neighbours, orients):
    side, width = inputs.shape[1], inputs.shape[3]
    pixels = side * side
    count = lax.axis_size("tile")
    chips = count // 2
    lanes = 3 * LANES
    me = lax.axis_index("tile")
    me_array = me.reshape(1)
    nbrs = neighbours.reshape(-1)
    turns = orients.reshape(-1)
    grad = out_grad.reshape(pixels, width)
    flat_in = inputs.reshape(pixels, width)

    slots = pl.pallas_call(
        functools.partial(pack_borders, side, count),
        out_shape=jax.ShapeDtypeStruct((count, side, width), jnp.bfloat16),
        in_specs=[SMEM, SMEM, SMEM, VMEM],
        out_specs=VMEM,
        scratch_shapes=[pltpu.VMEM((8, side, width), jnp.bfloat16)],
        compiler_params=params(32),
        name="pack_borders",
    )(me_array, nbrs, turns, grad)
    slots = lax.all_to_all(slots, "tile", 0, 0, tiled=True)

    scale = 1.0 / math.sqrt(count * inputs.shape[0] * pixels)
    tall = jax.ShapeDtypeStruct((pixels + 2 * side, lanes), jnp.bfloat16)
    transposed = pltpu.VMEM((width, pixels), jnp.bfloat16)
    if 9 * width * width % (2 * width * count):
        kernel = lax.all_gather(weight, "tile", axis=0, tiled=True).reshape(9, width, width)
        left, mid, right, parts = pl.pallas_call(
            functools.partial(plain_weight_term, side, width),
            out_shape=(tall,) * 3 + (jax.ShapeDtypeStruct((3, 9 * width, LANES), jnp.float32),),
            in_specs=[SMEM, SMEM, VMEM, VMEM, VMEM],
            out_specs=(VMEM,) * 4,
            scratch_shapes=[transposed],
            compiler_params=params(56),
            name="plain_weight_term",
        )(me_array, nbrs, flat_in, grad, slots)
        whole = jnp.concatenate(list(parts), axis=1)[:, :width].reshape(-1)
        summed = lax.psum_scatter(whole, "tile", scatter_dimension=0, tiled=True)
        weight_grad = summed * scale
    else:
        kernel = gather_kernel(weight, count, me).reshape(9, width, width)
        left, mid, right, weight_grad = fast_weight_grad(
            side, width, count, scale, tall, transposed, me_array, nbrs, flat_in, grad, slots
        )

    input_grad = pl.pallas_call(
        functools.partial(input_term, side, width),
        out_shape=jax.ShapeDtypeStruct((pixels, width), jnp.bfloat16),
        in_specs=[VMEM] * 4,
        out_specs=VMEM,
        compiler_params=params(32),
        cost_estimate=pl.CostEstimate(
            flops=18 * pixels * width * width, bytes_accessed=6 << 20, transcendentals=0
        ),
        name="input_term",
    )(left, mid, right, kernel)
    return (input_grad.reshape(inputs.shape), weight_grad)


def solution(mesh):
    in_specs = (
        P(("rep", "tile"), None, None, None),
        P(("rep", "tile"), None, None, None),
        P("tile"),
        P(),
        P(),
    )
    out_specs = (P(("rep", "tile"), None, None, None), P(("rep", "tile")))
    return jax.shard_map(
        per_device, mesh=mesh, in_specs=in_specs, out_specs=out_specs, check_vma=False
    )
```

time: 222 us -> 114 us (0.51)
  between operations: 45.1 us -> 0.89 us
  waiting for transfers between devices: 67.7 us -> 38.9 us
  starting transfers between devices: 0.12 us -> 26.6 us
  other arithmetic: 31.7 us -> 7.23 us
  blocking collectives: 23.2 us -> 0 us
  matrix products: 19.8 us -> 0 us
  Pallas kernels: 0 us -> 17.3 us
  local copies, waits for them, and re-layouts: 33.2 us -> 22.5 us
    unnamed x4 -> x0, waiting for transfers between devices: 67.2 us -> none
    ppermute x0 -> x12, waiting for transfers between devices: none -> 38.9 us  [the longest x3 26.2 us: gather_kernel(): got = lax.ppermute(held, 'tile', [(i, i ^ 2 * step) for i in range(count)])]
    all_gather x1 -> x0, other arithmetic: 27.1 us -> none  [per_device(): lax.all_gather(weight, 'tile', axis=0, tiled=True)]
    all_gather x1 -> x0, blocking collectives: 23.2 us -> none  [per_device(): piece_corners = lax.all_gather(corners, 'tile', axis=0, tiled=True)]
    dot_general x18 -> x0, matrix products: 19.8 us -> none  [the longest x9 12.5 us: taps_grad(): lax.dot_general(flat_in, window, (((0,), (0,)), ((), ())), preferred_elem...]
    ppermute x0 -> x12, starting transfers between devices: none -> 19.3 us  [the longest x7 14.8 us: fast_weight_grad(): lax.ppermute(sends[offset - 1], 'tile', [(i, i ^ 2 * offset) for i in ran...]
    pallas_call x0 -> x5, Pallas kernels: none -> 17.3 us  [the longest x1 7.66 us: fast_weight_grad(): pl.pallas_call(functools.partial(weight_term, side, width, chips, pairs),...]
    another operation x3 -> x2, local copies, waits for them, and re-layouts: 12.5 us -> 2.85 us  [gather_kernel(): both = jnp.stack([first, second], axis=1)]
  transfers between devices with their start and end apart: 3 -> 13, of which waited for: 2 -> 6; matrix products, arithmetic and copies ran while one was open for 35% -> 2% of each run, Pallas kernels for 0% -> 9%
where the time goes in v1:
time: 114 us
  waiting for transfers between devices  38.9 us (34%)
  starting transfers between devices  26.6 us (23%)
  local copies, waits for them, and re-layouts  22.5 us (20%)
  Pallas kernels  17.3 us (15%)
  other arithmetic  7.23 us (6%)
    ppermute x3, waiting for transfers between devices, gather_kernel(): got = lax.ppermute(held, 'tile', [(i, i ^ 2 * step) for i in range(count)])  26.2 us
    ppermute x7, starting transfers between devices, fast_weight_grad(): lax.ppermute(sends[offset - 1], 'tile', [(i, i ^ 2 * offset) for i in ran...  14.8 us
    ppermute x7, waiting for transfers between devices, fast_weight_grad(): lax.ppermute(sends[offset - 1], 'tile', [(i, i ^ 2 * offset) for i in ran...  12.7 us
    pallas_call x1, Pallas kernels, fast_weight_grad(): pl.pallas_call(functools.partial(weight_term, side, width, chips, pairs),...  7.66 us
    all_to_all x1, starting transfers between devices, per_device(): slots = lax.all_to_all(slots, 'tile', 0, 0, tiled=True)  7.36 us
    gather x2, local copies, waits for them, and re-layouts, gather_kernel(): return both[order]  7.26 us
    another operation x2, other arithmetic, gather_kernel(): both = jnp.stack([first, second], axis=1)  7.03 us
    unnamed x38, local copies, waits for them, and re-layouts  7.01 us
  transfers between devices with their start and end apart: 13, of which 6 were waited for; matrix products, arithmetic and copies ran while one was open for 2% of the time, Pallas kernels for 9%

profile of v1, /device:TPU:0, one launch (start us, length us, event | category | flops | bytes accessed | tf_op | source)
XLA Modules:
  0.0 113.5 jit_solution(14586310988947945506)
XLA Ops:
  3.5 2.1 %pack_borders.1 = bf16[16,32,320]{2,1,0:T(8,128)(2,1)} custom-call(s32[1]{0:T(128)} %bitcast.me_ref, s32[128]{0:T(128)S(1)} %reshape.61.nbr_ref, s32[128]{0:T(128)S(1)} %reshape.64.turn_ref, bf16[1024,320]{1,0:T(8,128)(2,1)S(1)} %bitcast.17), custom_call_target="tpu_custom_call" | custom-call | tf_op jit(solution)/shard_map/pack_borders/pallas_call | solution.py:299
  5.6 7.4 %all-to-all-start = ((bf16[16,32,320]{2,1,0:T(8,128)(2,1)}), bf16[16,32,320]{2,1,0:T(8,128)(2,1)S(1)}, u32[]{:S(2)}, u32[]{:S(2)}) async-start(bf16[16,32,320]{2,1,0:T(8,128)(2,1)} %pack_borders.1), calls=%async_computation | async-start | bytes 786432 | tf_op jit(solution)/shard_map/all_to_all | solution.py:308
  13.0 2.9 %collective-permute-start = (bf16[1,450,128]{2,1,0:T(8,128)(2,1)S(1)}, bf16[1,450,128]{2,1,0:T(8,128)(2,1)S(1)}, u32[]{:S(2)}, u32[]{:S(2)}) collective-permute-start(bf16[1,450,128]{2,1,0:T(8,128)(2,1)S(1)} %bitcast.18), channel_id=1, source_target_pairs={{0,8},{1,9},{2,10},{3,11},{4,12},{5,13},{6,14},{7,15},{8,0},{9,1},... | collective-permute-start | bytes 345608 | tf_op jit(solution)/shard_map/ppermute | solution.py:221
  15.9 14.6 %collective-permute-done = bf16[1,450,128]{2,1,0:T(8,128)(2,1)S(1)} collective-permute-done((bf16[1,450,128]{2,1,0:T(8,128)(2,1)S(1)}, bf16[1,450,128]{2,1,0:T(8,128)(2,1)S(1)}, u32[]{:S(2)}, u32[]{:S(2)}) %collective-permute-start) | collective-permute-done | bytes 115232 | tf_op jit(solution)/shard_map/ppermute | solution.py:221
  31.3 7.7 %weight_term.1 = (bf16[1088,384]{1,0:T(8,128)(2,1)}, bf16[1088,384]{1,0:T(8,128)(2,1)}, bf16[1088,384]{1,0:T(8,128)(2,1)}, f32[8,480,128]{2,1,0:T(8,128)}, s16[8,480,128]{2,1,0:T(8,128)(2,1)}) custom-call(s32[1]{0:T(128)} %bitcast.me_ref, s32[128]{0:T(128)} %copy-done.2, bf16[1024,320]{1,0:T(8,128)(2,1)} %bitcast.23, bf16[1024,320]{1,0:T(8,128)(2,1)} %bitcast.16, ...), custom_call_target="tpu_custom_call" | custom-call | tf_op jit(solution)/shard_map/weight_term/pallas_call | solution.py:243
  39.0 1.5 %collective-permute-start.2 = (bf16[4,450,128]{2,1,0:T(8,128)(2,1)S(1)}, bf16[4,450,128]{2,1,0:T(8,128)(2,1)S(1)}, u32[]{:S(2)}, u32[]{:S(2)}) collective-permute-start(bf16[4,450,128]{2,1,0:T(8,128)(2,1)S(1)} %pad_maximum_fusion.2), channel_id=1, source_target_pairs={{0,2},{1,3},{2,0},{3,1},{4,6},{5,7},{6,4},{7,5},{8,10},{9,11},{10,... | collective-permute-start | bytes 1382408 | tf_op jit(solution)/shard_map/ppermute | solution.py:221
  40.6 11.6 %collective-permute-done.2 = bf16[4,450,128]{2,1,0:T(8,128)(2,1)S(1)} collective-permute-done((bf16[4,450,128]{2,1,0:T(8,128)(2,1)S(1)}, bf16[4,450,128]{2,1,0:T(8,128)(2,1)S(1)}, u32[]{:S(2)}, u32[]{:S(2)}) %collective-permute-start.2) | collective-permute-done | bytes 460832 | tf_op jit(solution)/shard_map/ppermute | solution.py:221
  53.4 1.2 %pair_sum.1 = (f32[480,128]{1,0:T(8,128)S(1)}, s16[480,128]{1,0:T(8,128)(2,1)}, s16[480,128]{1,0:T(8,128)(2,1)S(1)}, s16[480,128]{1,0:T(8,128)(2,1)S(1)}, s16[48...) custom-call(s32[1]{0:T(128)} %bitcast.me_ref, ...), custom_call_target="tpu_custom_call" | custom-call | tf_op jit(solution)/shard_map/pair_sum/pallas_call | solution.py:262
  55.9 1.5 %collective-permute-start.10 = (s16[480,128]{1,0:T(8,128)(2,1)}, s16[480,128]{1,0:T(8,128)(2,1)S(1)}, u32[]{:S(2)}, u32[]{:S(2)}) collective-permute-start(s16[480,128]{1,0:T(8,128)(2,1)} %get-tuple-element.26), channel_id=1, source_target_pairs={{0,12},{1,13},{2,14},{3,15},{4,8},{5,9},{6,10},{7,11},{8,4},{9,5},... | collective-permute-start | bytes 368648 | tf_op jit(solution)/shard_map/ppermute | solution.py:272
  57.4 3.3 %collective-permute-start.11 = (s16[480,128]{1,0:T(8,128)(2,1)}, s16[480,128]{1,0:T(8,128)(2,1)S(1)}, u32[]{:S(2)}, u32[]{:S(2)}) collective-permute-start(s16[480,128]{1,0:T(8,128)(2,1)} %get-tuple-element.27), channel_id=1, source_target_pairs={{0,14},{1,15},{2,12},{3,13},{4,10},{5,11},{6,8},{7,9},{8,6},{9,7},... | collective-permute-start | bytes 368648 | tf_op jit(solution)/shard_map/ppermute | solution.py:272
  62.2 2.0 %collective-permute-done.10.refs_5_ = s16[480,128]{1,0:T(8,128)(2,1)S(1)} collective-permute-done((s16[480,128]{1,0:T(8,128)(2,1)}, s16[480,128]{1,0:T(8,128)(2,1)S(1)}, u32[]{:S(2)}, u32[]{:S(2)}) %collective-permute-start.10) | collective-permute-done | bytes 122912 | tf_op jit(solution)/shard_map/ppermute | solution.py:272
  64.2 6.2 %collective-permute-start.7 = (s16[480,128]{1,0:T(8,128)(2,1)}, s16[480,128]{1,0:T(8,128)(2,1)S(1)}, u32[]{:S(2)}, u32[]{:S(2)}) collective-permute-start(s16[480,128]{1,0:T(8,128)(2,1)} %copy-done.6), channel_id=1, source_target_pairs={{0,6},{1,7},{2,4},{3,5},{4,2},{5,3},{6,0},{7,1},{8,14},{9,15},{10,... | collective-permute-start | bytes 368648 | tf_op jit(solution)/shard_map/ppermute | solution.py:272
  70.4 2.3 %collective-permute-start.8 = (s16[480,128]{1,0:T(8,128)(2,1)S(1)}, s16[480,128]{1,0:T(8,128)(2,1)S(1)}, u32[]{:S(2)}, u32[]{:S(2)}) collective-permute-start(s16[480,128]{1,0:T(8,128)(2,1)S(1)} %get-tuple-element.24), channel_id=1, source_target_pairs={{0,8},{1,9},{2,10},{3,11},{4,12},{5,13},{6,14},{7,15},{8,0},{9,1},... | collective-permute-start | bytes 368648 | tf_op jit(solution)/shard_map/ppermute | solution.py:272
  73.4 1.4 %collective-permute-done.7.refs_2_ = s16[480,128]{1,0:T(8,128)(2,1)S(1)} collective-permute-done((s16[480,128]{1,0:T(8,128)(2,1)}, s16[480,128]{1,0:T(8,128)(2,1)S(1)}, u32[]{:S(2)}, u32[]{:S(2)}) %collective-permute-start.7) | collective-permute-done | bytes 122912 | tf_op jit(solution)/shard_map/ppermute | solution.py:272
  74.8 7.5 %collective-permute-done.8.refs_3_ = s16[480,128]{1,0:T(8,128)(2,1)S(1)} collective-permute-done((s16[480,128]{1,0:T(8,128)(2,1)S(1)}, s16[480,128]{1,0:T(8,128)(2,1)S(1)}, u32[]{:S(2)}, u32[]{:S(2)}) %collective-permute-start.8) | collective-permute-done | bytes 122912 | tf_op jit(solution)/shard_map/ppermute | solution.py:272
  82.3 1.8 %collective-permute-done.9.refs_4_ = s16[480,128]{1,0:T(8,128)(2,1)S(1)} collective-permute-done((s16[480,128]{1,0:T(8,128)(2,1)S(1)}, s16[480,128]{1,0:T(8,128)(2,1)S(1)}, u32[]{:S(2)}, u32[]{:S(2)}) %collective-permute-start.9) | collective-permute-done | bytes 122912 | tf_op jit(solution)/shard_map/ppermute | solution.py:272
  85.1 1.4 %select_bitcast_fusion.1 = (bf16[8,1,450,128]{3,2,0,1:T(8,128)(2,1)S(1)}, bf16[8,1,450,128]{3,2,0,1:T(8,128)(2,1)S(1)}) fusion(pred[]{:T(512)S(6)} %eq.6, bf16[8,450,128]{2,0,1:T(8,128)(2,1)} %collective-permute-done.3, bf16[4,450,128]{2,1,0:T(8,128)(2,1)S(1)} %copy-done.16, bf16[2,450,128]{2,1,0:T(8,128)(2,1)S(1)} %copy-done.10, ...), kind=kLoop, calls=%fused_computation.5 | loop fusion | flops 2304000 | bytes 3686401 | tf_op jit(solution)/shard_map/stack | solution.py:231
  86.5 1.4 %copy.37 = bf16[8,1,450,128]{3,1,2,0:T(2,128)(2,1)S(1)} copy(bf16[8,1,450,128]{3,2,0,1:T(8,128)(2,1)S(1)} %get-tuple-element.28) | data formatting | bytes 1843200 | tf_op jit(solution)/shard_map/stack | solution.py:231
  87.9 1.4 %copy.38 = bf16[8,1,450,128]{3,1,2,0:T(2,128)(2,1)S(1)} copy(bf16[8,1,450,128]{3,2,0,1:T(8,128)(2,1)S(1)} %get-tuple-element.29) | data formatting | bytes 1843200 | tf_op jit(solution)/shard_map/stack | solution.py:231
  89.4 5.6 %pad_maximum_fusion = bf16[8,2,450,128]{3,1,2,0:T(2,128)(2,1)} fusion(bf16[8,1,450,128]{3,1,2,0:T(2,128)(2,1)S(1)} %copy.38, bf16[8,1,450,128]{3,1,2,0:T(2,128)(2,1)S(1)} %copy.37), kind=kLoop, calls=%fused_computation.2 | loop fusion | flops 3686400 | bytes 3686400 | tf_op jit(solution)/shard_map/stack | solution.py:231
  95.0 5.8 %gather_fusion.1 = bf16[8,2,450,128]{3,1,2,0:T(2,128)(2,1)S(1)} fusion(bf16[8,2,450,128]{3,1,2,0:T(2,128)(2,1)} %pad_maximum_fusion, s32[1024]{0:T(1024)S(1)} %pad_clamp_fusion), kind=kCustom, calls=%fused_computation.1 | custom fusion | bytes 3686432 | tf_op jit(solution)/shard_map/gather | solution.py:234
  100.8 1.5 %copy.39 = bf16[8,2,450,128]{3,2,1,0:T(8,128)(2,1)} copy(bf16[8,2,450,128]{3,1,2,0:T(2,128)(2,1)S(1)} %gather_fusion.1) | data formatting | bytes 3686400 | tf_op jit(solution)/shard_map/gather | solution.py:234
  102.3 3.6 %reshape.66.kernel_ref = bf16[9,320,320]{2,1,0:T(8,128)(2,1)S(1)} reshape(bf16[8,2,450,128]{3,2,1,0:T(8,128)(2,1)} %copy.39) | data formatting | bytes 3686400 | tf_op jit(solution)/shard_map/reshape | solution.py:328
  108.1 5.4 %input_term.1 = bf16[1024,320]{1,0:T(8,128)(2,1)} custom-call(bf16[1088,384]{1,0:T(8,128)(2,1)S(1)} %copy-done.3, bf16[1088,384]{1,0:T(8,128)(2,1)S(1)} %copy-done.4, bf16[1088,384]{1,0:T(8,128)(2,1)S(1)} %copy-done.5, bf16[9,320,320]{2,1,0:T(8,128)(2,1)S(1)} %reshape.66.kernel_ref), custom_call_target="tpu_custom_call" | custom-call | flops 1887436800 | bytes 6291456 | tf_op jit(solution)/shard_map/input_term/pallas_call | solution.py:333
  (63 shorter events, 11.5 us)
Async XLA Ops:
  1.5 29.1 %copy-start.2 = (s32[128]{0:T(128)}, s32[128]{0:T(128)S(1)}, u32[]{:S(2)}) copy-start(s32[128]{0:T(128)S(1)} %reshape.61.nbr_ref) | copy-start | bytes 1540
  3.5 9.5 %copy-start.11 = (bf16[57600]{0:T(1024)(128)(2,1)S(1)}, bf16[57600]{0:T(1024)(128)(2,1)}, u32[]{:S(2)}) copy-start(bf16[57600]{0:T(1024)(128)(2,1)} %param.8) | copy-start | bytes 345604
  5.6 24.9 %all-to-all-start = ((bf16[16,32,320]{2,1,0:T(8,128)(2,1)}), bf16[16,32,320]{2,1,0:T(8,128)(2,1)S(1)}, u32[]{:S(2)}, u32[]{:S(2)}) async-start(bf16[16,32,320]{2,1,0:T(8,128)(2,1)} %pack_borders.1), calls=%async_computation | async-start | bytes 786432 | tf_op jit(solution)/shard_map/all_to_all | solution.py:308
  13.0 17.4 %collective-permute-start = (bf16[1,450,128]{2,1,0:T(8,128)(2,1)S(1)}, bf16[1,450,128]{2,1,0:T(8,128)(2,1)S(1)}, u32[]{:S(2)}, u32[]{:S(2)}) collective-permute-start(bf16[1,450,128]{2,1,0:T(8,128)(2,1)S(1)} %bitcast.18), channel_id=1, source_target_pairs={{0,8},{1,9},{2,10},{3,11},{4,12},{5,13},{6,14},{7,15},{8,0},{9,1},... | collective-permute-start | bytes 345608 | tf_op jit(solution)/shard_map/ppermute | solution.py:221
  30.4 21.9 %copy-start.13 = (bf16[1,450,128]{2,1,0:T(8,128)(2,1)}, bf16[1,450,128]{2,1,0:T(8,128)(2,1)S(1)}, u32[]{:S(2)}) copy-start(bf16[1,450,128]{2,1,0:T(8,128)(2,1)S(1)} %collective-permute-done) | copy-start | bytes 345604
  30.5 8.5 %collective-permute-start.1 = (bf16[2,450,128]{2,1,0:T(8,128)(2,1)S(1)}, bf16[2,450,128]{2,1,0:T(8,128)(2,1)S(1)}, u32[]{:S(2)}, u32[]{:S(2)}) collective-permute-start(bf16[2,450,128]{2,1,0:T(8,128)(2,1)S(1)} %pad_maximum_fusion.3), channel_id=1, source_target_pairs={{0,4},{1,5},{2,6},{3,7},{4,0},{5,1},{6,2},{7,3},{8,12},{9,13},{10,... | collective-permute-start | bytes 691208 | tf_op jit(solution)/shard_map/ppermute | solution.py:221
  39.0 14.4 %collective-permute-start.4 = (s16[8,480,128]{2,1,0:T(8,128)(2,1)}, s16[8,480,128]{2,1,0:T(8,128)(2,1)S(1)}, u32[]{:S(2)}, u32[]{:S(2)}) collective-permute-start(s16[8,480,128]{2,1,0:T(8,128)(2,1)} %get-tuple-element.19), channel_id=1, source_target_pairs={{0,1},{1,0},{2,3},{3,2},{4,5},{5,4},{6,7},{7,6},{8,9},{9,8},{10,11... | collective-permute-start | bytes 2949128 | tf_op jit(solution)/shard_map/ppermute | solution.py:261
  39.0 14.4 %copy-start.9 = (bf16[2,450,128]{2,1,0:T(8,128)(2,1)}, bf16[2,450,128]{2,1,0:T(8,128)(2,1)S(1)}, u32[]{:S(2)}) copy-start(bf16[2,450,128]{2,1,0:T(8,128)(2,1)S(1)} %collective-permute-done.1) | copy-start | bytes 691204
  39.0 14.4 %copy-start.1 = (f32[8,480,128]{2,1,0:T(8,128)S(1)}, f32[8,480,128]{2,1,0:T(8,128)}, u32[]{:S(2)}) copy-start(f32[8,480,128]{2,1,0:T(8,128)} %get-tuple-element.18.keep_ref) | copy-start | bytes 5898244
  39.0 13.2 %collective-permute-start.2 = (bf16[4,450,128]{2,1,0:T(8,128)(2,1)S(1)}, bf16[4,450,128]{2,1,0:T(8,128)(2,1)S(1)}, u32[]{:S(2)}, u32[]{:S(2)}) collective-permute-start(bf16[4,450,128]{2,1,0:T(8,128)(2,1)S(1)} %pad_maximum_fusion.2), channel_id=1, source_target_pairs={{0,2},{1,3},{2,0},{3,1},{4,6},{5,7},{6,4},{7,5},{8,10},{9,11},{10,... | collective-permute-start | bytes 1382408 | tf_op jit(solution)/shard_map/ppermute | solution.py:221
  53.4 7.9 %copy-start.8 = (s32[8]{0:T(128)S(1)}, s32[8]{0:T(128)}, u32[]{:S(2)}) copy-start(s32[8]{0:T(128)} %constant.34.clone) | copy-start | bytes 100
  53.4 31.7 %collective-permute-start.3 = (bf16[8,450,128]{2,0,1:T(8,128)(2,1)}, bf16[8,450,128]{2,0,1:T(8,128)(2,1)}, u32[]{:S(2)}, u32[]{:S(2)}) collective-permute-start(bf16[8,450,128]{2,0,1:T(8,128)(2,1)} %copy.32), channel_id=1, source_target_pairs={{0,1},{1,0},{2,3},{3,2},{4,5},{5,4},{6,7},{7,6},{8,9},{9,8},{10,11... | collective-permute-start | bytes 2764808 | tf_op jit(solution)/shard_map/ppermute | solution.py:223
  55.9 29.2 %copy-start.10 = (bf16[2,450,128]{2,1,0:T(8,128)(2,1)S(1)}, bf16[2,450,128]{2,1,0:T(8,128)(2,1)}, u32[]{:S(2)}) copy-start(bf16[2,450,128]{2,1,0:T(8,128)(2,1)} %copy-done.9) | copy-start | bytes 691204
  55.9 29.2 %copy-start.12 = (bf16[57600]{0:T(1024)(128)(2,1)S(1)}, bf16[57600]{0:T(1024)(128)(2,1)}, u32[]{:S(2)}) copy-start(bf16[57600]{0:T(1024)(128)(2,1)} %param.8) | copy-start | bytes 345604
  55.9 29.2 %copy-start.14 = (bf16[1,450,128]{2,1,0:T(8,128)(2,1)S(1)}, bf16[1,450,128]{2,1,0:T(8,128)(2,1)}, u32[]{:S(2)}) copy-start(bf16[1,450,128]{2,1,0:T(8,128)(2,1)} %copy-done.13) | copy-start | bytes 345604
  55.9 29.2 %copy-start.16 = (bf16[4,450,128]{2,1,0:T(8,128)(2,1)S(1)}, bf16[4,450,128]{2,1,0:T(8,128)(2,1)}, u32[]{:S(2)}) copy-start(bf16[4,450,128]{2,1,0:T(8,128)(2,1)} %copy-done.15) | copy-start | bytes 1382404
  55.9 8.3 %collective-permute-start.10 = (s16[480,128]{1,0:T(8,128)(2,1)}, s16[480,128]{1,0:T(8,128)(2,1)S(1)}, u32[]{:S(2)}, u32[]{:S(2)}) collective-permute-start(s16[480,128]{1,0:T(8,128)(2,1)} %get-tuple-element.26), channel_id=1, source_target_pairs={{0,12},{1,13},{2,14},{3,15},{4,8},{5,9},{6,10},{7,11},{8,4},{9,5},... | collective-permute-start | bytes 368648 | tf_op jit(solution)/shard_map/ppermute | solution.py:272
  57.4 13.0 %collective-permute-start.11 = (s16[480,128]{1,0:T(8,128)(2,1)}, s16[480,128]{1,0:T(8,128)(2,1)S(1)}, u32[]{:S(2)}, u32[]{:S(2)}) collective-permute-start(s16[480,128]{1,0:T(8,128)(2,1)} %get-tuple-element.27), channel_id=1, source_target_pairs={{0,14},{1,15},{2,12},{3,13},{4,10},{5,11},{6,8},{7,9},{8,6},{9,7},... | collective-permute-start | bytes 368648 | tf_op jit(solution)/shard_map/ppermute | solution.py:272
  60.7 12.1 %collective-permute-start.5 = (s16[480,128]{1,0:T(8,128)(2,1)}, s16[480,128]{1,0:T(8,128)(2,1)S(1)}, u32[]{:S(2)}, u32[]{:S(2)}) collective-permute-start(s16[480,128]{1,0:T(8,128)(2,1)} %get-tuple-element.21), channel_id=1, source_target_pairs={{0,2},{1,3},{2,0},{3,1},{4,6},{5,7},{6,4},{7,5},{8,10},{9,11},{10,... | collective-permute-start | bytes 368648 | tf_op jit(solution)/shard_map/ppermute | solution.py:272
  61.9 11.5 %collective-permute-start.6 = (s16[480,128]{1,0:T(8,128)(2,1)}, s16[480,128]{1,0:T(8,128)(2,1)S(1)}, u32[]{:S(2)}, u32[]{:S(2)}) collective-permute-start(s16[480,128]{1,0:T(8,128)(2,1)} %copy-done.7), channel_id=1, source_target_pairs={{0,4},{1,5},{2,6},{3,7},{4,0},{5,1},{6,2},{7,3},{8,12},{9,13},{10,... | collective-permute-start | bytes 368648 | tf_op jit(solution)/shard_map/ppermute | solution.py:272
  64.2 10.6 %collective-permute-start.7 = (s16[480,128]{1,0:T(8,128)(2,1)}, s16[480,128]{1,0:T(8,128)(2,1)S(1)}, u32[]{:S(2)}, u32[]{:S(2)}) collective-permute-start(s16[480,128]{1,0:T(8,128)(2,1)} %copy-done.6), channel_id=1, source_target_pairs={{0,6},{1,7},{2,4},{3,5},{4,2},{5,3},{6,0},{7,1},{8,14},{9,15},{10,... | collective-permute-start | bytes 368648 | tf_op jit(solution)/shard_map/ppermute | solution.py:272
  70.4 11.9 %collective-permute-start.8 = (s16[480,128]{1,0:T(8,128)(2,1)S(1)}, s16[480,128]{1,0:T(8,128)(2,1)S(1)}, u32[]{:S(2)}, u32[]{:S(2)}) collective-permute-start(s16[480,128]{1,0:T(8,128)(2,1)S(1)} %get-tuple-element.24), channel_id=1, source_target_pairs={{0,8},{1,9},{2,10},{3,11},{4,12},{5,13},{6,14},{7,15},{8,0},{9,1},... | collective-permute-start | bytes 368648 | tf_op jit(solution)/shard_map/ppermute | solution.py:272
  72.8 11.3 %collective-permute-start.9 = (s16[480,128]{1,0:T(8,128)(2,1)S(1)}, s16[480,128]{1,0:T(8,128)(2,1)S(1)}, u32[]{:S(2)}, u32[]{:S(2)}) collective-permute-start(s16[480,128]{1,0:T(8,128)(2,1)S(1)} %get-tuple-element.25), channel_id=1, source_target_pairs={{0,10},{1,11},{2,8},{3,9},{4,14},{5,15},{6,12},{7,13},{8,2},{9,3},... | collective-permute-start | bytes 368648 | tf_op jit(solution)/shard_map/ppermute | solution.py:272
  102.3 3.6 %copy-start.3 = (bf16[1088,384]{1,0:T(8,128)(2,1)S(1)}, bf16[1088,384]{1,0:T(8,128)(2,1)}, u32[]{:S(2)}) copy-start(bf16[1088,384]{1,0:T(8,128)(2,1)} %get-tuple-element.15.left_ref) | copy-start | bytes 2506756
  (7 other events, 6.6 us)

commit v2 on v1

v2 whole, which is shorter than its diff:
```python
import functools
import math

import jax
import jax.numpy as jnp
from jax import lax
from jax.experimental import pallas as pl
from jax.experimental.pallas import tpu as pltpu
from jax.sharding import PartitionSpec as P

LANES = 128
GROUP = 96
VMEM = pl.BlockSpec(memory_space=pltpu.VMEM)
SMEM = pl.BlockSpec(memory_space=pltpu.SMEM)
STRIP_OF = (
    (2, 4, 1, 7),
    (0, 6, 3, 5),
    (6, 3, 5, 0),
    (4, 1, 7, 2),
    (3, 2, 0, 1),
    (2, 0, 1, 3),
    (1, 3, 2, 0),
    (0, 1, 3, 2),
)


def strip_code(direction):
    return sum(strip << (4 * turn) for turn, strip in enumerate(STRIP_OF[direction]))


def params(megabytes):
    return pltpu.CompilerParams(vmem_limit_bytes=megabytes << 20)


def low_half(rows):
    return lax.broadcasted_iota(jnp.int32, (rows, LANES), 1) < LANES // 2


def pick_pixels(rows, target, pixels, flat):
    column = lax.broadcasted_iota(jnp.int32, (rows, pixels), 1)
    pick = jnp.where(column == target, 1.0, 0.0).astype(jnp.bfloat16)
    return jnp.dot(pick, flat, preferred_element_type=jnp.float32)


def edge_pixels(side):
    row = lax.broadcasted_iota(jnp.int32, (4 * side, 1), 0)
    edge, along = row // side, row % side
    return jnp.where(
        edge == 0,
        along,
        jnp.where(
            edge == 1,
            (side - 1) * side + along,
            jnp.where(edge == 2, along * side, along * side + side - 1),
        ),
    )


def widened(block, width):
    return jnp.concatenate(
        [block, jnp.zeros((block.shape[0], 3 * LANES - width), block.dtype)], axis=1
    )


def pack_borders(side, count, me_ref, nbr_ref, turn_ref, grad_ref, slots_ref, strips_ref):
    pixels = side * side
    half = side // 2
    edges = pick_pixels(4 * side, edge_pixels(side), pixels, grad_ref[...])
    turned_row = lax.broadcasted_iota(jnp.int32, (4 * side, 4 * side), 0)
    turned_column = lax.broadcasted_iota(jnp.int32, (4 * side, 4 * side), 1)
    mirror = turned_row // side * (2 * side) + side - 1 - turned_row == turned_column
    mirror = jnp.where(mirror, 1.0, 0.0).astype(jnp.bfloat16)
    reverse = jnp.dot(mirror, edges.astype(jnp.bfloat16), preferred_element_type=jnp.float32)
    low = low_half(half)
    for flip, found in enumerate((edges, reverse)):
        found = widened(found, edges.shape[1])
        for edge in range(4):
            block = found[edge * side : (edge + 1) * side]
            last = block[:, 2 * LANES :]
            last = jnp.where(low, last[:half], pltpu.roll(last[half:], LANES // 2, 1))
            strips_ref[2 * edge + flip] = jnp.concatenate(
                [block[:, :LANES], block[:, LANES : 2 * LANES], last], axis=0
            ).astype(jnp.bfloat16)
    me = me_ref[0]

    def fill(dest, carry):
        which = jnp.int32(0)
        for direction in range(8):
            turn = turn_ref[dest, direction]
            found = (strip_code(direction) >> (4 * turn)) & 15
            which = jnp.where(nbr_ref[dest, direction] == me, found, which)
        slots_ref[dest] = strips_ref[which]
        return carry

    lax.fori_loop(0, count, fill, 0)


def rim_pieces(side, me_ref, nbr_ref, slots_ref):
    half = side // 2
    low = low_half(side)
    rims = []
    for direction in range(8):
        slot = slots_ref[nbr_ref[me_ref[0], direction]].astype(jnp.float32)
        last = slot[2 * side :]
        last = jnp.concatenate([last, pltpu.roll(last, LANES // 2, 1)], axis=0)
        last = jnp.where(low, last, 0.0)
        rims.append(jnp.concatenate([slot[:side], slot[side : 2 * side], last], axis=1))
    return rims


def row_shifts(side, rim, first, last):
    place = lax.broadcasted_iota(jnp.int32, rim.shape, 0)
    after = jnp.where(place == side - 1, last, pltpu.roll(rim, side - 1, 0))
    before = jnp.where(place == 0, first, pltpu.roll(rim, 1, 0))
    return (after, rim, before)


def fill_shifted(side, own, rims, refs):
    pixels, lanes = own.shape
    tall = (side, side, lanes)
    place = lax.broadcasted_iota(jnp.int32, tall, 1)
    after = pltpu.roll(own, pixels - 1, 0).reshape(tall)
    before = pltpu.roll(own, 1, 0).reshape(tall)
    if rims is None:
        after = jnp.where(place == side - 1, 0.0, after)
        before = jnp.where(place == 0, 0.0, before)
        outer = [[jnp.zeros((side, lanes), jnp.float32)] * 3] * 2
    else:
        north, south, west, east, nw, ne, sw, se = rims
        after = jnp.where(place == side - 1, east.reshape(side, 1, lanes), after)
        before = jnp.where(place == 0, west.reshape(side, 1, lanes), before)
        outer = [
            row_shifts(side, north, nw[0:1], ne[0:1]),
            row_shifts(side, south, sw[0:1], se[0:1]),
        ]
    for tap, block in enumerate((after.reshape(own.shape), own, before.reshape(own.shape))):
        refs[tap][0:side] = outer[0][tap].astype(jnp.bfloat16)
        refs[tap][side : side + pixels] = block.astype(jnp.bfloat16)
        refs[tap][side + pixels :] = outer[1][tap].astype(jnp.bfloat16)


def exponent_of(peak):
    return jnp.maximum(jnp.ceil(jnp.log2(jnp.maximum(peak, 1e-30))), -90.0)


def coded(block):
    power = exponent_of(jnp.max(jnp.abs(block), axis=0, keepdims=True))
    steps = jnp.round(block * (jnp.exp2(15.0 - power) * 0.999)).astype(jnp.int32)
    return steps, power.astype(jnp.int32)


def write_coded(out_ref, block, rows):
    steps, power = coded(block)
    row = lax.broadcasted_iota(jnp.int32, block.shape, 0)
    out_ref[...] = jnp.where(row == rows, power, steps).astype(jnp.int16)


def read_coded(steps, rows):
    whole = steps.astype(jnp.int32)
    power = whole[rows : rows + 1].astype(jnp.float32)
    row = lax.broadcasted_iota(jnp.int32, whole.shape, 0)
    value = whole.astype(jnp.float32) * (jnp.exp2(power - 15.0) * (1.0 / 0.999))
    return jnp.where(row == rows, 0.0, value)


def inner_term(side, width, in_ref, grad_ref, acc_ref, edge_ref, in_t_ref, *shifted):
    pixels = side * side
    own = widened(grad_ref[...].astype(jnp.float32), width)
    fill_shifted(side, own, None, shifted)
    edges = pick_pixels(4 * side, edge_pixels(side), pixels, in_ref[...])
    edge_ref[...] = edges.T.astype(jnp.bfloat16)
    in_t_ref[...] = in_ref[...].T
    for row_tap in range(3):
        for col_tap in range(3):
            window = shifted[col_tap][(2 - row_tap) * side : (2 - row_tap) * side + pixels]
            tap = 3 * row_tap + col_tap
            term = jnp.dot(in_t_ref[...], window, preferred_element_type=jnp.float32)
            for part in range(3):
                acc_ref[part, tap * width : (tap + 1) * width] = term[
                    :, part * LANES : (part + 1) * LANES
                ]


def add_rim(side, width, me_ref, nbr_ref, edge_ref, slots_ref, inner_ref, acc_ref):
    north, south, west, east, nw, ne, sw, se = rim_pieces(side, me_ref, nbr_ref, slots_ref)
    none = jnp.zeros_like(north)
    tops = row_shifts(side, north, nw[0:1], ne[0:1])
    bottoms = row_shifts(side, south, sw[0:1], se[0:1])
    lefts = row_shifts(side, west, 0.0, 0.0)
    rights = row_shifts(side, east, 0.0, 0.0)
    for row_tap in range(3):
        for col_tap in range(3):
            tap = 3 * row_tap + col_tap
            rows = slice(tap * width, (tap + 1) * width)
            if tap == 4:
                for part in range(3):
                    acc_ref[part, rows] = inner_ref[part, rows]
                continue
            outside = jnp.concatenate(
                [
                    tops[col_tap] if row_tap == 2 else none,
                    bottoms[col_tap] if row_tap == 0 else none,
                    lefts[row_tap] if col_tap == 2 else none,
                    rights[row_tap] if col_tap == 0 else none,
                ],
                axis=0,
            ).astype(jnp.bfloat16)
            term = jnp.dot(edge_ref[...], outside, preferred_element_type=jnp.float32)
            for part in range(3):
                acc_ref[part, rows] = (
                    inner_ref[part, rows] + term[:, part * LANES : (part + 1) * LANES]
                )


def rim_term(
    side, width, chips, pairs,
    me_ref, nbr_ref, edge_ref, slots_ref, inner_ref,
    keep_ref, send_ref,
    acc_ref, pack_ref,
):
    add_rim(side, width, me_ref, nbr_ref, edge_ref, slots_ref, inner_ref, acc_ref)
    half = LANES // 2
    low = low_half(pairs)
    for shard in range(2 * chips):
        base = shard * 2 * pairs
        even = pl.ds(base, pairs, stride=2)
        odd = pl.ds(base + 1, pairs, stride=2)
        e0, e1, e2 = [acc_ref[part, even] for part in range(3)]
        o0, o1, o2 = [pltpu.roll(acc_ref[part, odd], half, 1) for part in range(3)]
        groups = (e0, e1, jnp.where(low, e2, o0), jnp.where(low, o0, o1), jnp.where(low, o1, o2))
        for group, block in enumerate(groups):
            pack_ref[shard, group * GROUP : group * GROUP + pairs] = block
            pack_ref[shard, group * GROUP + pairs : (group + 1) * GROUP] = jnp.zeros(
                (GROUP - pairs, LANES), jnp.float32
            )
    core = me_ref[0] % 2
    for chip in range(chips):
        keep_ref[chip] = pack_ref[2 * chip + core]
        write_coded(send_ref.at[chip], pack_ref[2 * chip + 1 - core], pairs)


def pair_sum(pairs, chips, me_ref, keep_ref, got_ref, own_ref, *send_refs):
    chip = me_ref[0] // 2
    for offset in range(chips):
        dest = chip ^ offset
        total = keep_ref[dest] + read_coded(got_ref[dest], pairs)
        if offset == 0:
            own_ref[...] = total
        else:
            write_coded(send_refs[offset - 1], total, pairs)


def final_sum(pairs, scale, own_ref, *refs):
    got_refs, out_ref = refs[:-1], refs[-1]
    total = own_ref[...]
    for got_ref in got_refs:
        total = total + read_coded(got_ref[...], pairs)
    total = total * scale
    for group in range(5):
        out_ref[pl.ds(group, pairs, stride=5), :] = total[group * GROUP : group * GROUP + pairs]


def pack_kernel(pairs, kernel_ref, out_ref, rows_ref):
    half = LANES // 2
    low = low_half(pairs)
    rows_ref[...] = kernel_ref[...].astype(jnp.float32)
    parts = [rows_ref[pl.ds(group, pairs, stride=5), :] for group in range(5)]
    turned = [pltpu.roll(part, half, 1) for part in parts]
    groups = (
        parts[0],
        parts[1],
        jnp.where(low, turned[2], turned[3]),
        jnp.where(low, turned[3], turned[4]),
        jnp.where(low, parts[2], parts[4]),
    )
    for group, block in enumerate(groups):
        whole = jnp.concatenate([block, jnp.zeros((GROUP - pairs, LANES), jnp.float32)], axis=0)
        out_ref[0, group * GROUP : (group + 1) * GROUP] = whole.astype(jnp.bfloat16)


def unpack_kernel(pairs, places, me_ref, mine_ref, other_ref, rows_ref):
    chip = me_ref[0] // 2
    core = me_ref[0] % 2
    for offset, place in places.items():
        for source_ref, from_core in ((mine_ref, core), (other_ref, 1 - core)):
            shard = 2 * (chip ^ offset) + from_core
            base = shard * 2 * pairs
            even = pl.ds(base, pairs, stride=2)
            odd = pl.ds(base + 1, pairs, stride=2)
            e0, e1, o0, o1, last = [
                source_ref[place, group * GROUP : (group + 1) * GROUP].astype(jnp.float32)[:pairs]
                for group in range(5)
            ]
            rows_ref[0, even] = e0
            rows_ref[1, even] = e1
            rows_ref[2, even] = last
            rows_ref[0, odd] = o0
            rows_ref[1, odd] = o1
            rows_ref[2, odd] = pltpu.roll(last, LANES // 2, 1)


def input_sums(side, width, me_ref, nbr_ref, grad_ref, slots_ref, kernel_ref, out_ref, shifted):
    own = widened(grad_ref[...].astype(jnp.float32), width)
    fill_shifted(side, own, rim_pieces(side, me_ref, nbr_ref, slots_ref), shifted)
    chunk = side * side // 4
    for part in range(4):
        total = jnp.zeros((chunk, width), jnp.float32)
        for row_tap in range(3):
            for col_tap in range(3):
                start = (2 - row_tap) * side + part * chunk
                tap = 3 * row_tap + col_tap
                total = total + lax.dot_general(
                    shifted[col_tap][start : start + chunk],
                    kernel_ref[tap * width : (tap + 1) * width],
                    (((1,), (1,)), ((), ())),
                    preferred_element_type=jnp.float32,
                )
        out_ref[part * chunk : (part + 1) * chunk] = total.astype(jnp.bfloat16)


def plain_input_term(
    side, width, me_ref, nbr_ref, grad_ref, slots_ref, flat_ref, out_ref, kernel_ref, *shifted
):
    kernel_ref[...] = widened(flat_ref[...].astype(jnp.float32), width).astype(jnp.bfloat16)
    input_sums(side, width, me_ref, nbr_ref, grad_ref, slots_ref, kernel_ref, out_ref, shifted)


def input_term(
    side, width, pairs, places,
    me_ref, nbr_ref, grad_ref, slots_ref, mine_ref, other_ref,
    out_ref,
    kernel_ref, rows_ref, *shifted,
):
    unpack_kernel(pairs, places, me_ref, mine_ref, other_ref, rows_ref)
    for part in range(3):
        kernel_ref[:, part * LANES : (part + 1) * LANES] = rows_ref[part].astype(jnp.bfloat16)
    input_sums(side, width, me_ref, nbr_ref, grad_ref, slots_ref, kernel_ref, out_ref, shifted)


def after(value, *others):
    return lax.optimization_barrier((value,) + others)[0]


def gather_places(chips):
    places = [0]
    step = chips // 2
    while step:
        places = places + [offset ^ step for offset in places]
        step //= 2
    return {offset: place for place, offset in enumerate(places)}


def gather_step(held, count, step):
    got = lax.ppermute(held, "tile", [(i, i ^ (2 * step)) for i in range(count)])
    return jnp.concatenate([held, got], axis=0)


def per_device(inputs, out_grad, weight, neighbours, orients):
    side, width = inputs.shape[1], inputs.shape[3]
    pixels = side * side
    count = lax.axis_size("tile")
    chips = count // 2
    whole = 9 * width * width
    lanes = 3 * LANES
    me = lax.axis_index("tile").reshape(1)
    grad = out_grad.reshape(pixels, width)
    flat_in = inputs.reshape(pixels, width)
    scale = 1.0 / math.sqrt(count * inputs.shape[0] * pixels)
    slot = (5 * side // 2, LANES)
    shifted = [pltpu.VMEM((pixels + 2 * side, lanes), jnp.bfloat16)] * 3
    sums = (3, 9 * width, LANES)
    even = whole % (2 * width * count) == 0
    pairs = whole // (2 * width * count)
    message = (5 * GROUP, LANES)

    if even:
        packed = pl.pallas_call(
            functools.partial(pack_kernel, pairs),
            out_shape=jax.ShapeDtypeStruct((1,) + message, jnp.bfloat16),
            in_specs=[VMEM],
            out_specs=VMEM,
            scratch_shapes=[pltpu.VMEM((5 * pairs, LANES), jnp.float32)],
            name="pack_kernel",
        )(weight.reshape(-1, LANES))
        places = gather_places(chips)
        step = chips // 2
        held = gather_step(packed, count, step)
        ready_grad = after(grad, packed)
    else:
        flat_kernel = lax.all_gather(weight, "tile", axis=0, tiled=True).reshape(9 * width, width)
        ready_grad = grad

    slots = pl.pallas_call(
        functools.partial(pack_borders, side, count),
        out_shape=jax.ShapeDtypeStruct((count,) + slot, jnp.bfloat16),
        in_specs=[SMEM, SMEM, SMEM, VMEM],
        out_specs=VMEM,
        scratch_shapes=[pltpu.VMEM((8,) + slot, jnp.bfloat16)],
        compiler_params=params(32),
        name="pack_borders",
    )(me, neighbours, orients, ready_grad)
    ready_in = after(flat_in, slots)
    slots = lax.all_to_all(slots, "tile", 0, 0, tiled=True)

    inner, edges = pl.pallas_call(
        functools.partial(inner_term, side, width),
        out_shape=(
            jax.ShapeDtypeStruct(sums, jnp.float32),
            jax.ShapeDtypeStruct((width, 4 * side), jnp.bfloat16),
        ),
        in_specs=[VMEM, VMEM],
        out_specs=(VMEM, VMEM),
        scratch_shapes=[pltpu.VMEM((width, pixels), jnp.bfloat16)] + shifted,
        compiler_params=params(48),
        cost_estimate=pl.CostEstimate(
            flops=18 * pixels * width * width, bytes_accessed=6 << 20, transcendentals=0
        ),
        name="inner_term",
    )(ready_in, grad)

    if even:
        if step > 1:
            step //= 2
            held = gather_step(after(held, edges), count, step)
        keep, send = pl.pallas_call(
            functools.partial(rim_term, side, width, chips, pairs),
            out_shape=(
                jax.ShapeDtypeStruct((chips,) + message, jnp.float32),
                jax.ShapeDtypeStruct((chips,) + message, jnp.int16),
            ),
            in_specs=[SMEM, SMEM, VMEM, VMEM, VMEM],
            out_specs=(VMEM,) * 2,
            scratch_shapes=[
                pltpu.VMEM(sums, jnp.float32),
                pltpu.VMEM((count,) + message, jnp.float32),
            ],
            compiler_params=params(48),
            name="rim_term",
        )(me, neighbours, edges, slots, inner)
        while step > 1:
            step //= 2
            held = gather_step(after(held, send), count, step)
        own, gots = spread_sums(count, pairs, message, me, keep, send)
        other = lax.ppermute(after(held, own), "tile", [(i, i ^ 1) for i in range(count)])
        input_grad = pl.pallas_call(
            functools.partial(input_term, side, width, pairs, places),
            out_shape=jax.ShapeDtypeStruct((pixels, width), jnp.bfloat16),
            in_specs=[SMEM, SMEM] + [VMEM] * 4,
            out_specs=VMEM,
            scratch_shapes=[
                pltpu.VMEM((9 * width, lanes), jnp.bfloat16),
                pltpu.VMEM(sums, jnp.float32),
            ]
            + shifted,
            compiler_params=params(48),
            cost_estimate=pl.CostEstimate(
                flops=18 * pixels * width * width, bytes_accessed=6 << 20, transcendentals=0
            ),
            name="input_term",
        )(me, neighbours, grad, slots, held, other)
        weight_grad = pl.pallas_call(
            functools.partial(final_sum, pairs, scale),
            out_shape=jax.ShapeDtypeStruct((5 * pairs, LANES), jnp.float32),
            in_specs=[VMEM] * chips,
            out_specs=VMEM,
            compiler_params=params(32),
            name="final_sum",
        )(after(own, input_grad), *gots).reshape(-1)
    else:
        parts = pl.pallas_call(
            functools.partial(add_rim, side, width),
            out_shape=jax.ShapeDtypeStruct(sums, jnp.float32),
            in_specs=[SMEM, SMEM, VMEM, VMEM, VMEM],
            out_specs=VMEM,
            compiler_params=params(48),
            name="add_rim",
        )(me, neighbours, edges, slots, inner)
        flat_sums = jnp.concatenate(list(parts), axis=1)[:, :width].reshape(-1)
        weight_grad = scale * lax.psum_scatter(
            flat_sums, "tile", scatter_dimension=0, tiled=True
        )
        input_grad = pl.pallas_call(
            functools.partial(plain_input_term, side, width),
            out_shape=jax.ShapeDtypeStruct((pixels, width), jnp.bfloat16),
            in_specs=[SMEM, SMEM] + [VMEM] * 3,
            out_specs=VMEM,
            scratch_shapes=[pltpu.VMEM((9 * width, lanes), jnp.bfloat16)] + shifted,
            compiler_params=params(48),
            name="plain_input_term",
        )(me, neighbours, grad, slots, flat_kernel)
    return (input_grad.reshape(inputs.shape), weight_grad)


def spread_sums(count, pairs, message, me, keep, send):
    chips = count // 2
    got = lax.ppermute(send, "tile", [(i, i ^ 1) for i in range(count)])
    own, *sends = pl.pallas_call(
        functools.partial(pair_sum, pairs, chips),
        out_shape=(jax.ShapeDtypeStruct(message, jnp.float32),)
        + (jax.ShapeDtypeStruct(message, jnp.int16),) * (chips - 1),
        in_specs=[SMEM, VMEM, VMEM],
        out_specs=(VMEM,) * chips,
        compiler_params=params(32),
        name="pair_sum",
    )(me, keep, got)
    gots = [
        lax.ppermute(sends[offset - 1], "tile", [(i, i ^ (2 * offset)) for i in range(count)])
        for offset in range(1, chips)
    ]
    return own, gots


def solution(mesh):
    in_specs = (
        P(("rep", "tile"), None, None, None),
        P(("rep", "tile"), None, None, None),
        P("tile"),
        P(),
        P(),
    )
    out_specs = (P(("rep", "tile"), None, None, None), P(("rep", "tile")))
    return jax.shard_map(
        per_device, mesh=mesh, in_specs=in_specs, out_specs=out_specs, check_vma=False
    )
```

time: 114 us -> 79.4 us (0.70)
  local copies, waits for them, and re-layouts: 22.5 us -> 7.04 us
  waiting for transfers between devices: 38.9 us -> 25 us
  other arithmetic: 7.23 us -> 0.07 us
  Pallas kernels: 17.3 us -> 20.1 us
    ppermute x12, waiting for transfers between devices: 38.9 us -> 25 us  [the longest x3 19.1 us: gather_step(): got = lax.ppermute(held, 'tile', [(i, i ^ 2 * step) for i in range(count)])]
    gather x3 -> x0, local copies, waits for them, and re-layouts: 7.9 us -> none  [the longest x2 7.26 us: gather_kernel(): return both[order]]
    another operation x2 -> x0, other arithmetic: 7.03 us -> none  [gather_kernel(): both = jnp.stack([first, second], axis=1)]
    reshape x3 -> x0, local copies, waits for them, and re-layouts: 3.74 us -> none  [the longest x1 3.56 us: per_device(): kernel = gather_kernel(weight, count, me).reshape(9, width, width)]
    another operation x2 -> x0, local copies, waits for them, and re-layouts: 2.85 us -> none  [gather_kernel(): both = jnp.stack([first, second], axis=1)]
    pallas_call x4 -> x6, Pallas kernels: 15.2 us -> 17.7 us  [the longest x1 6.7 us: per_device(): pl.pallas_call(functools.partial(input_term, side, width, pairs, places),...]
    unnamed x38 -> x15, local copies, waits for them, and re-layouts: 7.01 us -> 6.98 us
  transfers between devices with their start and end apart: 13 -> 13, of which waited for: 6 -> 6; matrix products, arithmetic and copies ran while one was open for 2% -> 0% of each run, Pallas kernels for 9% -> 18%
where the time goes in v2:
time: 79.4 us; the launch traced here: 79 us
  starting transfers between devices  26.1 us (33%)
  waiting for transfers between devices  25 us (31%)
  Pallas kernels  20.1 us (25%)
  local copies, waits for them, and re-layouts  7.04 us (9%)
    ppermute x3, waiting for transfers between devices, gather_step(): got = lax.ppermute(held, 'tile', [(i, i ^ 2 * step) for i in range(count)])  19.1 us
    ppermute x7, starting transfers between devices, spread_sums(): lax.ppermute(sends[offset - 1], 'tile', [(i, i ^ 2 * offset) for i in ran...  14.2 us
    all_to_all x1, starting transfers between devices, per_device(): slots = lax.all_to_all(slots, 'tile', 0, 0, tiled=True)  7.35 us
    unnamed x15, local copies, waits for them, and re-layouts  6.98 us
    pallas_call x1, Pallas kernels, per_device(): pl.pallas_call(functools.partial(input_term, side, width, pairs, places),...  6.7 us
    ppermute x7, waiting for transfers between devices, spread_sums(): lax.ppermute(sends[offset - 1], 'tile', [(i, i ^ 2 * offset) for i in ran...  5.84 us
    ppermute x3, starting transfers between devices, gather_step(): got = lax.ppermute(held, 'tile', [(i, i ^ 2 * step) for i in range(count)])  4.43 us
    pallas_call x1, Pallas kernels, per_device(): pl.pallas_call(functools.partial(rim_term, side, width, chips, pairs), ou...  4.31 us
  transfers between devices with their start and end apart: 13, of which 6 were waited for; matrix products, arithmetic and copies ran while one was open for 0% of the time, Pallas kernels for 18%

profile of v2, /device:TPU:0, one launch (start us, length us, event | category | flops | bytes accessed | tf_op | source)
XLA Modules:
  0.0 79.0 jit_solution(11033640268159020621)
XLA Ops:
  0.6 1.7 %pack_kernel.1 = bf16[1,480,128]{2,1,0:T(8,128)(2,1)} custom-call(bf16[450,128]{1,0:T(8,128)(2,1)} %bitcast.11), custom_call_target="tpu_custom_call" | custom-call | tf_op jit(solution)/shard_map/pack_kernel/pallas_call | solution.py:377
  2.3 0.8 copy.10.nbr_ref
  3.8 1.1 %copy-done.1 = bf16[1,32,32,320]{3,2,1,0:T(8,128)(2,1)S(1)} copy-done((bf16[1,32,32,320]{3,2,1,0:T(8,128)(2,1)S(1)}, bf16[1,32,32,320]{3,2,1,0:T(8,128)(2,1)}, u32[]{:S(2)}) %copy-start.1) | copy-done | bytes 655384
  4.9 2.4 %pack_borders.1 = bf16[16,80,128]{2,1,0:T(8,128)(2,1)} custom-call(s32[1]{0:T(128)} %bitcast.me_ref, s32[16,8]{1,0:T(8,128)S(1)} %copy.10.nbr_ref, s32[16,8]{1,0:T(8,128)S(1)} %copy.8.turn_ref, bf16[1024,320]{1,0:T(8,128)(2,1)S(1)} %bitcast.6), custom_call_target="tpu_custom_call" | custom-call | tf_op jit(solution)/shard_map/pack_borders/pallas_call | solution.py:393
  7.4 7.4 %all-to-all-start = ((bf16[16,80,128]{2,1,0:T(8,128)(2,1)}), bf16[16,80,128]{2,1,0:T(8,128)(2,1)S(1)}, u32[]{:S(2)}, u32[]{:S(2)}) async-start(bf16[16,80,128]{2,1,0:T(8,128)(2,1)} %pack_borders.1), calls=%async_computation | async-start | bytes 655360 | tf_op jit(solution)/shard_map/all_to_all | solution.py:403
  14.7 2.8 %collective-permute-start = (bf16[1,480,128]{2,1,0:T(8,128)(2,1)}, bf16[1,480,128]{2,1,0:T(8,128)(2,1)S(1)}, u32[]{:S(2)}, u32[]{:S(2)}) collective-permute-start(bf16[1,480,128]{2,1,0:T(8,128)(2,1)} %pack_kernel.1), channel_id=1, source_target_pairs={{0,8},{1,9},{2,10},{3,11},{4,12},{5,13},{6,14},{7,15},{8,0},{9,1},... | collective-permute-start | bytes 368648 | tf_op jit(solution)/shard_map/ppermute | solution.py:354
  17.5 1.1 %copy-done.2 = bf16[1,32,32,320]{3,2,1,0:T(8,128)(2,1)S(1)} copy-done((bf16[1,32,32,320]{3,2,1,0:T(8,128)(2,1)S(1)}, bf16[1,32,32,320]{3,2,1,0:T(8,128)(2,1)}, u32[]{:S(2)}) %copy-start.2) | copy-done | bytes 655384
  18.7 1.1 %copy-done.4 = bf16[1,32,32,320]{3,2,1,0:T(8,128)(2,1)S(1)} copy-done((bf16[1,32,32,320]{3,2,1,0:T(8,128)(2,1)S(1)}, bf16[1,32,32,320]{3,2,1,0:T(8,128)(2,1)}, u32[]{:S(2)}) %copy-start.4) | copy-done | bytes 655384
  19.8 3.5 %inner_term.1 = (f32[3,2880,128]{2,1,0:T(8,128)S(1)}, bf16[320,128]{1,0:T(8,128)(2,1)S(1)}) custom-call(bf16[1024,320]{1,0:T(8,128)(2,1)S(1)} %bitcast.9, bf16[1024,320]{1,0:T(8,128)(2,1)S(1)} %bitcast.7), custom_call_target="tpu_custom_call" | custom-call | flops 1887436800 | bytes 6291456 | tf_op jit(solution)/shard_map/inner_term/pallas_call | solution.py:405
  23.3 2.0 %copy-done = f32[3,2880,128]{2,1,0:T(8,128)} copy-done((f32[3,2880,128]{2,1,0:T(8,128)}, f32[3,2880,128]{2,1,0:T(8,128)S(1)}, u32[]{:S(2)}) %copy-start) | copy-done | bytes 4423704
  25.3 5.7 %collective-permute-done = bf16[1,480,128]{2,1,0:T(8,128)(2,1)S(1)} collective-permute-done((bf16[1,480,128]{2,1,0:T(8,128)(2,1)}, bf16[1,480,128]{2,1,0:T(8,128)(2,1)S(1)}, u32[]{:S(2)}, u32[]{:S(2)}) %collective-permute-start) | collective-permute-done | bytes 122912 | tf_op jit(solution)/shard_map/ppermute | solution.py:354
  31.2 4.3 %rim_term.1 = (f32[8,480,128]{2,1,0:T(8,128)S(1)}, s16[8,480,128]{2,1,0:T(8,128)(2,1)S(1)}) custom-call(s32[1]{0:T(128)} %bitcast.me_ref, s32[16,8]{1,0:T(8,128)S(1)} %copy.10.nbr_ref, bf16[320,128]{1,0:T(8,128)(2,1)S(1)} %get-tuple-element.22.edge_ref, bf16[16,80,128]{2,1,0:T(8,128)(2,1)S(1)} %all-to-all-done.slots_ref, f32[3,2880,128]{2,1,0:T(8,128)} %copy-done), custom_call_target="tpu_custom_call" | custom-call | tf_op jit(solution)/shard_map/rim_term/pallas_call | solution.py:425
  35.6 3.1 %collective-permute-done.1 = bf16[2,480,128]{2,1,0:T(8,128)(2,1)S(1)} collective-permute-done((bf16[2,480,128]{2,1,0:T(8,128)(2,1)S(1)}, bf16[2,480,128]{2,1,0:T(8,128)(2,1)S(1)}, u32[]{:S(2)}, u32[]{:S(2)}) %collective-permute-start.1) | collective-permute-done | bytes 245792 | tf_op jit(solution)/shard_map/ppermute | solution.py:354
  38.7 1.5 %collective-permute-start.2 = (bf16[4,480,128]{2,1,0:T(8,128)(2,1)S(1)}, bf16[4,480,128]{2,1,0:T(8,128)(2,1)S(1)}, u32[]{:S(2)}, u32[]{:S(2)}) collective-permute-start(bf16[4,480,128]{2,1,0:T(8,128)(2,1)S(1)} %pad_maximum_fusion), channel_id=1, source_target_pairs={{0,2},{1,3},{2,0},{3,1},{4,6},{5,7},{6,4},{7,5},{8,10},{9,11},{10,... | collective-permute-start | bytes 1474568 | tf_op jit(solution)/shard_map/ppermute | solution.py:354
  40.2 10.4 %collective-permute-done.2 = bf16[4,480,128]{2,1,0:T(8,128)(2,1)S(1)} collective-permute-done((bf16[4,480,128]{2,1,0:T(8,128)(2,1)S(1)}, bf16[4,480,128]{2,1,0:T(8,128)(2,1)S(1)}, u32[]{:S(2)}, u32[]{:S(2)}) %collective-permute-start.2) | collective-permute-done | bytes 491552 | tf_op jit(solution)/shard_map/ppermute | solution.py:354
  51.3 1.6 %collective-permute-start.10 = (s16[480,128]{1,0:T(8,128)(2,1)S(1)}, s16[480,128]{1,0:T(8,128)(2,1)S(1)}, u32[]{:S(2)}, u32[]{:S(2)}) collective-permute-start(s16[480,128]{1,0:T(8,128)(2,1)S(1)} %get-tuple-element.36), channel_id=1, source_target_pairs={{0,12},{1,13},{2,14},{3,15},{4,8},{5,9},{6,10},{7,11},{8,4},{9,5},... | collective-permute-start | bytes 368648 | tf_op jit(solution)/shard_map/ppermute | solution.py:507
  52.9 3.2 %collective-permute-start.11 = (s16[480,128]{1,0:T(8,128)(2,1)S(1)}, s16[480,128]{1,0:T(8,128)(2,1)S(1)}, u32[]{:S(2)}, u32[]{:S(2)}) collective-permute-start(s16[480,128]{1,0:T(8,128)(2,1)S(1)} %get-tuple-element.37), channel_id=1, source_target_pairs={{0,14},{1,15},{2,12},{3,13},{4,10},{5,11},{6,8},{7,9},{8,6},{9,7},... | collective-permute-start | bytes 368648 | tf_op jit(solution)/shard_map/ppermute | solution.py:507
  56.7 2.5 %collective-permute-done.10.refs_5_ = s16[480,128]{1,0:T(8,128)(2,1)S(1)} collective-permute-done((s16[480,128]{1,0:T(8,128)(2,1)S(1)}, s16[480,128]{1,0:T(8,128)(2,1)S(1)}, u32[]{:S(2)}, u32[]{:S(2)}) %collective-permute-start.10) | collective-permute-done | bytes 122912 | tf_op jit(solution)/shard_map/ppermute | solution.py:507
  59.2 5.2 %collective-permute-start.7 = (s16[480,128]{1,0:T(8,128)(2,1)S(1)}, s16[480,128]{1,0:T(8,128)(2,1)S(1)}, u32[]{:S(2)}, u32[]{:S(2)}) collective-permute-start(s16[480,128]{1,0:T(8,128)(2,1)S(1)} %get-tuple-element.33), channel_id=1, source_target_pairs={{0,6},{1,7},{2,4},{3,5},{4,2},{5,3},{6,0},{7,1},{8,14},{9,15},{10,... | collective-permute-start | bytes 368648 | tf_op jit(solution)/shard_map/ppermute | solution.py:507
  64.4 3.6 %collective-permute-start.8 = (s16[480,128]{1,0:T(8,128)(2,1)S(1)}, s16[480,128]{1,0:T(8,128)(2,1)S(1)}, u32[]{:S(2)}, u32[]{:S(2)}) collective-permute-start(s16[480,128]{1,0:T(8,128)(2,1)S(1)} %get-tuple-element.34), channel_id=1, source_target_pairs={{0,8},{1,9},{2,10},{3,11},{4,12},{5,13},{6,14},{7,15},{8,0},{9,1},... | collective-permute-start | bytes 368648 | tf_op jit(solution)/shard_map/ppermute | solution.py:507
  68.0 6.7 %input_term.1 = bf16[1024,320]{1,0:T(8,128)(2,1)} custom-call(s32[1]{0:T(128)} %bitcast.me_ref, s32[16,8]{1,0:T(8,128)S(1)} %copy.10.nbr_ref, bf16[1024,320]{1,0:T(8,128)(2,1)S(1)} %bitcast.8, bf16[16,80,128]{2,1,0:T(8,128)(2,1)S(1)} %all-to-all-done.slots_ref, bf16[8,480,128]{2,1,0:T(8,128)(2,1)S(1)} %constant_dynamic-update-slice_fusion.mine_ref, ...), custom_call_target="tpu_custom_call" | custom-call | flops 1887436800 | bytes 6291456 | tf_op jit(solution)/shard_map/input_term/pallas_call | solution.py:445
  74.7 2.3 %collective-permute-done.8.refs_3_ = s16[480,128]{1,0:T(8,128)(2,1)S(1)} collective-permute-done((s16[480,128]{1,0:T(8,128)(2,1)S(1)}, s16[480,128]{1,0:T(8,128)(2,1)S(1)}, u32[]{:S(2)}, u32[]{:S(2)}) %collective-permute-start.8) | collective-permute-done | bytes 122912 | tf_op jit(solution)/shard_map/ppermute | solution.py:507
  77.1 1.0 %collective-permute-done.9.refs_4_ = s16[480,128]{1,0:T(8,128)(2,1)S(1)} collective-permute-done((s16[480,128]{1,0:T(8,128)(2,1)S(1)}, s16[480,128]{1,0:T(8,128)(2,1)S(1)}, u32[]{:S(2)}, u32[]{:S(2)}) %collective-permute-start.9) | collective-permute-done | bytes 122912 | tf_op jit(solution)/shard_map/ppermute | solution.py:507
  78.1 0.9 %final_sum.1 = f32[450,128]{1,0:T(8,128)} custom-call(f32[480,128]{1,0:T(8,128)S(1)} %get-tuple-element.30.own_ref, s16[480,128]{1,0:T(8,128)(2,1)S(1)} %collective-permute-done.5.refs_0_, s16[480,128]{1,0:T(8,128)(2,1)S(1)} %collective-permute-done.6.refs_1_, s16[480,128]{1,0:T(8,128)(2,1)S(1)} %collective-permute-done.7.refs_2_, ...), custom_call_target="tpu_custom_call" | custom-call | tf_op jit(solution)/shard_map/final_sum/pallas_call | solution.py:461
  (27 shorter events, 2.3 us)
Async XLA Ops:
  3.8 1.1 %copy-start.1 = (bf16[1,32,32,320]{3,2,1,0:T(8,128)(2,1)S(1)}, bf16[1,32,32,320]{3,2,1,0:T(8,128)(2,1)}, u32[]{:S(2)}) copy-start(bf16[1,32,32,320]{3,2,1,0:T(8,128)(2,1)} %param.6) | copy-start | bytes 1966084
  4.9 26.1 %copy-start.5 = (bf16[1,480,128]{2,1,0:T(8,128)(2,1)S(1)}, bf16[1,480,128]{2,1,0:T(8,128)(2,1)}, u32[]{:S(2)}) copy-start(bf16[1,480,128]{2,1,0:T(8,128)(2,1)} %pack_kernel.1) | copy-start | bytes 368644
  7.4 23.8 %all-to-all-start = ((bf16[16,80,128]{2,1,0:T(8,128)(2,1)}), bf16[16,80,128]{2,1,0:T(8,128)(2,1)S(1)}, u32[]{:S(2)}, u32[]{:S(2)}) async-start(bf16[16,80,128]{2,1,0:T(8,128)(2,1)} %pack_borders.1), calls=%async_computation | async-start | bytes 655360 | tf_op jit(solution)/shard_map/all_to_all | solution.py:403
  14.7 16.3 %collective-permute-start = (bf16[1,480,128]{2,1,0:T(8,128)(2,1)}, bf16[1,480,128]{2,1,0:T(8,128)(2,1)S(1)}, u32[]{:S(2)}, u32[]{:S(2)}) collective-permute-start(bf16[1,480,128]{2,1,0:T(8,128)(2,1)} %pack_kernel.1), channel_id=1, source_target_pairs={{0,8},{1,9},{2,10},{3,11},{4,12},{5,13},{6,14},{7,15},{8,0},{9,1},... | collective-permute-start | bytes 368648 | tf_op jit(solution)/shard_map/ppermute | solution.py:354
  17.5 1.1 %copy-start.2 = (bf16[1,32,32,320]{3,2,1,0:T(8,128)(2,1)S(1)}, bf16[1,32,32,320]{3,2,1,0:T(8,128)(2,1)}, u32[]{:S(2)}) copy-start(bf16[1,32,32,320]{3,2,1,0:T(8,128)(2,1)} %param.6) | copy-start | bytes 1966084
  18.7 1.1 %copy-start.4 = (bf16[1,32,32,320]{3,2,1,0:T(8,128)(2,1)S(1)}, bf16[1,32,32,320]{3,2,1,0:T(8,128)(2,1)}, u32[]{:S(2)}) copy-start(bf16[1,32,32,320]{3,2,1,0:T(8,128)(2,1)} %param.5) | copy-start | bytes 1966084
  23.3 2.0 %copy-start = (f32[3,2880,128]{2,1,0:T(8,128)}, f32[3,2880,128]{2,1,0:T(8,128)S(1)}, u32[]{:S(2)}) copy-start(f32[3,2880,128]{2,1,0:T(8,128)S(1)} %get-tuple-element.24.inner_ref) | copy-start | bytes 13271044
  31.1 7.6 %collective-permute-start.1 = (bf16[2,480,128]{2,1,0:T(8,128)(2,1)S(1)}, bf16[2,480,128]{2,1,0:T(8,128)(2,1)S(1)}, u32[]{:S(2)}, u32[]{:S(2)}) collective-permute-start(bf16[2,480,128]{2,1,0:T(8,128)(2,1)S(1)} %pad_maximum_fusion.1), channel_id=1, source_target_pairs={{0,4},{1,5},{2,6},{3,7},{4,0},{5,1},{6,2},{7,3},{8,12},{9,13},{10,... | collective-permute-start | bytes 737288 | tf_op jit(solution)/shard_map/ppermute | solution.py:354
  31.2 36.9 %copy-start.3 = (bf16[1,32,32,320]{3,2,1,0:T(8,128)(2,1)S(1)}, bf16[1,32,32,320]{3,2,1,0:T(8,128)(2,1)}, u32[]{:S(2)}) copy-start(bf16[1,32,32,320]{3,2,1,0:T(8,128)(2,1)} %param.6) | copy-start | bytes 1966084
  35.5 15.2 %collective-permute-start.3 = (s16[8,480,128]{2,1,0:T(8,128)(2,1)S(1)}, s16[8,480,128]{2,1,0:T(8,128)(2,1)S(1)}, u32[]{:S(2)}, u32[]{:S(2)}) collective-permute-start(s16[8,480,128]{2,1,0:T(8,128)(2,1)S(1)} %get-tuple-element.25), channel_id=1, source_target_pairs={{0,1},{1,0},{2,3},{3,2},{4,5},{5,4},{6,7},{7,6},{8,9},{9,8},{10,11... | collective-permute-start | bytes 2949128 | tf_op jit(solution)/shard_map/ppermute | solution.py:496
  38.7 11.9 %collective-permute-start.2 = (bf16[4,480,128]{2,1,0:T(8,128)(2,1)S(1)}, bf16[4,480,128]{2,1,0:T(8,128)(2,1)S(1)}, u32[]{:S(2)}, u32[]{:S(2)}) collective-permute-start(bf16[4,480,128]{2,1,0:T(8,128)(2,1)S(1)} %pad_maximum_fusion), channel_id=1, source_target_pairs={{0,2},{1,3},{2,0},{3,1},{4,6},{5,7},{6,4},{7,5},{8,10},{9,11},{10,... | collective-permute-start | bytes 1474568 | tf_op jit(solution)/shard_map/ppermute | solution.py:354
  51.3 16.7 %collective-permute-start.4 = (bf16[8,480,128]{2,1,0:T(8,128)(2,1)S(1)}, bf16[8,480,128]{2,1,0:T(8,128)(2,1)S(1)}, u32[]{:S(2)}, u32[]{:S(2)}) collective-permute-start(bf16[8,480,128]{2,1,0:T(8,128)(2,1)S(1)} %constant_dynamic-update-slice_fusion.mine_ref), channel_id=1, source_target_pairs={{0,1},{1,0},{2,3},{3,2},{4,5},{5,4},{6,7},{7,6},{8,9},{9,8},{10,11... | collective-permute-start | bytes 2949128 | tf_op jit(solution)/shard_map/ppermute | solution.py:444
  51.3 7.8 %collective-permute-start.10 = (s16[480,128]{1,0:T(8,128)(2,1)S(1)}, s16[480,128]{1,0:T(8,128)(2,1)S(1)}, u32[]{:S(2)}, u32[]{:S(2)}) collective-permute-start(s16[480,128]{1,0:T(8,128)(2,1)S(1)} %get-tuple-element.36), channel_id=1, source_target_pairs={{0,12},{1,13},{2,14},{3,15},{4,8},{5,9},{6,10},{7,11},{8,4},{9,5},... | collective-permute-start | bytes 368648 | tf_op jit(solution)/shard_map/ppermute | solution.py:507
  52.9 11.5 %collective-permute-start.11 = (s16[480,128]{1,0:T(8,128)(2,1)S(1)}, s16[480,128]{1,0:T(8,128)(2,1)S(1)}, u32[]{:S(2)}, u32[]{:S(2)}) collective-permute-start(s16[480,128]{1,0:T(8,128)(2,1)S(1)} %get-tuple-element.37), channel_id=1, source_target_pairs={{0,14},{1,15},{2,12},{3,13},{4,10},{5,11},{6,8},{7,9},{8,6},{9,7},... | collective-permute-start | bytes 368648 | tf_op jit(solution)/shard_map/ppermute | solution.py:507
  56.1 18.6 %collective-permute-start.5 = (s16[480,128]{1,0:T(8,128)(2,1)S(1)}, s16[480,128]{1,0:T(8,128)(2,1)S(1)}, u32[]{:S(2)}, u32[]{:S(2)}) collective-permute-start(s16[480,128]{1,0:T(8,128)(2,1)S(1)} %get-tuple-element.31), channel_id=1, source_target_pairs={{0,2},{1,3},{2,0},{3,1},{4,6},{5,7},{6,4},{7,5},{8,10},{9,11},{10,... | collective-permute-start | bytes 368648 | tf_op jit(solution)/shard_map/ppermute | solution.py:507
  56.7 18.0 %collective-permute-start.6 = (s16[480,128]{1,0:T(8,128)(2,1)S(1)}, s16[480,128]{1,0:T(8,128)(2,1)S(1)}, u32[]{:S(2)}, u32[]{:S(2)}) collective-permute-start(s16[480,128]{1,0:T(8,128)(2,1)S(1)} %get-tuple-element.32), channel_id=1, source_target_pairs={{0,4},{1,5},{2,6},{3,7},{4,0},{5,1},{6,2},{7,3},{8,12},{9,13},{10,... | collective-permute-start | bytes 368648 | tf_op jit(solution)/shard_map/ppermute | solution.py:507
  59.2 15.5 %collective-permute-start.7 = (s16[480,128]{1,0:T(8,128)(2,1)S(1)}, s16[480,128]{1,0:T(8,128)(2,1)S(1)}, u32[]{:S(2)}, u32[]{:S(2)}) collective-permute-start(s16[480,128]{1,0:T(8,128)(2,1)S(1)} %get-tuple-element.33), channel_id=1, source_target_pairs={{0,6},{1,7},{2,4},{3,5},{4,2},{5,3},{6,0},{7,1},{8,14},{9,15},{10,... | collective-permute-start | bytes 368648 | tf_op jit(solution)/shard_map/ppermute | solution.py:507
  64.4 12.7 %collective-permute-start.8 = (s16[480,128]{1,0:T(8,128)(2,1)S(1)}, s16[480,128]{1,0:T(8,128)(2,1)S(1)}, u32[]{:S(2)}, u32[]{:S(2)}) collective-permute-start(s16[480,128]{1,0:T(8,128)(2,1)S(1)} %get-tuple-element.34), channel_id=1, source_target_pairs={{0,8},{1,9},{2,10},{3,11},{4,12},{5,13},{6,14},{7,15},{8,0},{9,1},... | collective-permute-start | bytes 368648 | tf_op jit(solution)/shard_map/ppermute | solution.py:507
  68.0 10.1 %collective-permute-start.9 = (s16[480,128]{1,0:T(8,128)(2,1)S(1)}, s16[480,128]{1,0:T(8,128)(2,1)S(1)}, u32[]{:S(2)}, u32[]{:S(2)}) collective-permute-start(s16[480,128]{1,0:T(8,128)(2,1)S(1)} %get-tuple-element.35), channel_id=1, source_target_pairs={{0,10},{1,11},{2,8},{3,9},{4,14},{5,15},{6,12},{7,13},{8,2},{9,3},... | collective-permute-start | bytes 368648 | tf_op jit(solution)/shard_map/ppermute | solution.py:507

commit v3 on v2

--- a/solution.py
+++ b/solution.py
@@ -12,6 +12,7 @@
 GROUP = 96
 VMEM = pl.BlockSpec(memory_space=pltpu.VMEM)
 SMEM = pl.BlockSpec(memory_space=pltpu.SMEM)
+HBM = pl.BlockSpec(memory_space=pltpu.HBM)
 STRIP_OF = (
     (2, 4, 1, 7),
     (0, 6, 3, 5),
@@ -62,33 +63,69 @@
     )
 
 
-def pack_borders(side, count, me_ref, nbr_ref, turn_ref, grad_ref, slots_ref, strips_ref):
-    pixels = side * side
+def pack_borders(
+    side, count,
+    me_ref, nbr_in_ref, turn_in_ref, grad_in_ref,
+    slots_ref,
+    strips_ref, top_ref, bottom_ref, left_ref, right_ref, nbr_ref, turn_ref, sems,
+):
+    near = left_ref.shape[1]
     half = side // 2
-    edges = pick_pixels(4 * side, edge_pixels(side), pixels, grad_ref[...])
-    turned_row = lax.broadcasted_iota(jnp.int32, (4 * side, 4 * side), 0)
-    turned_column = lax.broadcasted_iota(jnp.int32, (4 * side, 4 * side), 1)
-    mirror = turned_row // side * (2 * side) + side - 1 - turned_row == turned_column
-    mirror = jnp.where(mirror, 1.0, 0.0).astype(jnp.bfloat16)
-    reverse = jnp.dot(mirror, edges.astype(jnp.bfloat16), preferred_element_type=jnp.float32)
+    copies = [
+        pltpu.make_async_copy(source, held, sems.at[place])
+        for place, (source, held) in enumerate(
+            (
+                (grad_in_ref.at[:, pl.ds(0, near)], left_ref),
+                (grad_in_ref.at[:, pl.ds(side - near, near)], right_ref),
+                (grad_in_ref.at[0], top_ref),
+                (grad_in_ref.at[side - 1], bottom_ref),
+                (nbr_in_ref, nbr_ref),
+                (turn_in_ref, turn_ref),
+            )
+        )
+    ]
+    for copy in copies:
+        copy.start()
+    row = lax.broadcasted_iota(jnp.int32, (8 * side, 1), 0)
+    edge = row // side % 4
+    along = jnp.where(row < 4 * side, row % side, side - 1 - row % side)
+    target = jnp.where(
+        edge < 2,
+        edge * side + along,
+        2 * side + jnp.where(edge == 2, along * near, (side + along) * near + near - 1),
+    )
+    known = 2 * side + 2 * side * near
+    column = lax.broadcasted_iota(jnp.int32, (8 * side, known), 1)
+    pick = jnp.where(column == target, 1.0, 0.0).astype(jnp.bfloat16)
     low = low_half(half)
-    for flip, found in enumerate((edges, reverse)):
-        found = widened(found, edges.shape[1])
-        for edge in range(4):
-            block = found[edge * side : (edge + 1) * side]
-            last = block[:, 2 * LANES :]
-            last = jnp.where(low, last[:half], pltpu.roll(last[half:], LANES // 2, 1))
-            strips_ref[2 * edge + flip] = jnp.concatenate(
-                [block[:, :LANES], block[:, LANES : 2 * LANES], last], axis=0
-            ).astype(jnp.bfloat16)
+    for copy in copies:
+        copy.wait()
+    width = top_ref.shape[1]
+    pixels = jnp.concatenate(
+        [
+            top_ref[...],
+            bottom_ref[...],
+            left_ref[...].reshape(side * near, width),
+            right_ref[...].reshape(side * near, width),
+        ],
+        axis=0,
+    )
+    found = widened(jnp.dot(pick, pixels, preferred_element_type=jnp.float32), width)
+    for strip in range(8):
+        block = found[strip * side : (strip + 1) * side]
+        last = block[:, 2 * LANES :]
+        last = jnp.where(low, last[:half], pltpu.roll(last[half:], LANES // 2, 1))
+        strips_ref[strip % 4 * 2 + strip // 4] = jnp.concatenate(
+            [block[:, :LANES], block[:, LANES : 2 * LANES], last], axis=0
+        ).astype(jnp.bfloat16)
     me = me_ref[0]
 
     def fill(dest, carry):
         which = jnp.int32(0)
         for direction in range(8):
-            turn = turn_ref[dest, direction]
+            turn = turn_ref[direction, dest]
             found = (strip_code(direction) >> (4 * turn)) & 15
-            which = jnp.where(nbr_ref[dest, direction] == me, found, which)
+            which = jnp.where(nbr_ref[direction, dest] == me, found, which)
         slots_ref[dest] = strips_ref[which]
         return carry
 
@@ -100,7 +137,7 @@
     low = low_half(side)
     rims = []
     for direction in range(8):
-        slot = slots_ref[nbr_ref[me_ref[0], direction]].astype(jnp.float32)
+        slot = slots_ref[nbr_ref[direction, me_ref[0]]].astype(jnp.float32)
         last = slot[2 * side :]
         last = jnp.concatenate([last, pltpu.roll(last, LANES // 2, 1)], axis=0)
         last = jnp.where(low, last, 0.0)
@@ -163,7 +200,7 @@
     return jnp.where(row == rows, 0.0, value)
 
 
-def inner_term(side, width, in_ref, grad_ref, acc_ref, edge_ref, in_t_ref, *shifted):
+def inner_term(side, width, packed_ref, in_ref, grad_ref, acc_ref, edge_ref, in_t_ref, *shifted):
     pixels = side * side
     own = widened(grad_ref[...].astype(jnp.float32), width)
     fill_shifted(side, own, None, shifted)
@@ -239,11 +276,21 @@
         write_coded(send_ref.at[chip], pack_ref[2 * chip + 1 - core], pairs)
 
 
-def pair_sum(pairs, chips, me_ref, keep_ref, got_ref, own_ref, *send_refs):
-    chip = me_ref[0] // 2
-    for offset in range(chips):
-        dest = chip ^ offset
-        total = keep_ref[dest] + read_coded(got_ref[dest], pairs)
+def pair_sum(pairs, chips, me_ref, keep_ref, got_ref, own_ref, send_ref):
+    across = me_ref[0] // 2 % 2
+    for row in range(chips // 2):
+        mine = 2 * row + across
+        own_ref[row] = keep_ref[mine] + read_coded(got_ref[mine], pairs)
+        theirs = 2 * row + 1 - across
+        write_coded(
+            send_ref.at[row], keep_ref[theirs] + read_coded(got_ref[theirs], pairs), pairs
+        )
+
+
+def cross_sum(pairs, rows, me_ref, keep_ref, got_ref, own_ref, *send_refs):
+    for offset in range(rows):
+        row = (me_ref[0] // 4) ^ offset
+        total = keep_ref[row] + read_coded(got_ref[row], pairs)
         if offset == 0:
             own_ref[...] = total
         else:
@@ -260,43 +307,28 @@
         out_ref[pl.ds(group, pairs, stride=5), :] = total[group * GROUP : group * GROUP + pairs]
 
 
-def pack_kernel(pairs, kernel_ref, out_ref, rows_ref):
+def unpack_kernel(pairs, chips, me_ref, mine_ref, other_ref, shard_ref, rows_ref):
+    chip = me_ref[0] // 2
+    core = me_ref[0] % 2
     half = LANES // 2
     low = low_half(pairs)
-    rows_ref[...] = kernel_ref[...].astype(jnp.float32)
-    parts = [rows_ref[pl.ds(group, pairs, stride=5), :] for group in range(5)]
-    turned = [pltpu.roll(part, half, 1) for part in parts]
-    groups = (
-        parts[0],
-        parts[1],
-        jnp.where(low, turned[2], turned[3]),
-        jnp.where(low, turned[3], turned[4]),
-        jnp.where(low, parts[2], parts[4]),
-    )
-    for group, block in enumerate(groups):
-        whole = jnp.concatenate([block, jnp.zeros((GROUP - pairs, LANES), jnp.float32)], axis=0)
-        out_ref[0, group * GROUP : (group + 1) * GROUP] = whole.astype(jnp.bfloat16)
-
-
-def unpack_kernel(pairs, places, me_ref, mine_ref, other_ref, rows_ref):
-    chip = me_ref[0] // 2
-    core = me_ref[0] % 2
-    for offset, place in places.items():
+    turn = 0
+    for offset in range(chips):
         for source_ref, from_core in ((mine_ref, core), (other_ref, 1 - core)):
             shard = 2 * (chip ^ offset) + from_core
             base = shard * 2 * pairs
             even = pl.ds(base, pairs, stride=2)
             odd = pl.ds(base + 1, pairs, stride=2)
-            e0, e1, o0, o1, last = [
-                source_ref[place, group * GROUP : (group + 1) * GROUP].astype(jnp.float32)[:pairs]
-                for group in range(5)
-            ]
-            rows_ref[0, even] = e0
-            rows_ref[1, even] = e1
-            rows_ref[2, even] = last
-            rows_ref[0, odd] = o0
-            rows_ref[1, odd] = o1
-            rows_ref[2, odd] = pltpu.roll(last, LANES // 2, 1)
+            shard_ref[turn] = source_ref[offset].astype(jnp.float32)[: 5 * pairs]
+            parts = [shard_ref[turn, pl.ds(group, pairs, stride=5), :] for group in range(5)]
+            turned = [pltpu.roll(part, half, 1) for part in parts[2:]]
+            rows_ref[0, even] = parts[0]
+            rows_ref[1, even] = parts[1]
+            rows_ref[2, even] = parts[2]
+            rows_ref[0, odd] = jnp.where(low, turned[0], turned[1])
+            rows_ref[1, odd] = jnp.where(low, turned[1], turned[2])
+            rows_ref[2, odd] = turned[2]
+            turn = 1 - turn
 
 
 def input_sums(side, width, me_ref, nbr_ref, grad_ref, slots_ref, kernel_ref, out_ref, shifted):
@@ -326,12 +358,12 @@
 
 
 def input_term(
-    side, width, pairs, places,
+    side, width, pairs, chips,
     me_ref, nbr_ref, grad_ref, slots_ref, mine_ref, other_ref,
     out_ref,
-    kernel_ref, rows_ref, *shifted,
+    kernel_ref, shard_ref, rows_ref, *shifted,
 ):
-    unpack_kernel(pairs, places, me_ref, mine_ref, other_ref, rows_ref)
+    unpack_kernel(pairs, chips, me_ref, mine_ref, other_ref, shard_ref, rows_ref)
     for part in range(3):
         kernel_ref[:, part * LANES : (part + 1) * LANES] = rows_ref[part].astype(jnp.bfloat16)
     input_sums(side, width, me_ref, nbr_ref, grad_ref, slots_ref, kernel_ref, out_ref, shifted)
@@ -341,18 +373,8 @@
     return lax.optimization_barrier((value,) + others)[0]
 
 
-def gather_places(chips):
-    places = [0]
-    step = chips // 2
-    while step:
-        places = places + [offset ^ step for offset in places]
-        step //= 2
-    return {offset: place for place, offset in enumerate(places)}
-
-
-def gather_step(held, count, step):
-    got = lax.ppermute(held, "tile", [(i, i ^ (2 * step)) for i in range(count)])
-    return jnp.concatenate([held, got], axis=0)
+def from_offset(value, count, offset):
+    return lax.ppermute(value, "tile", [(i, i ^ (2 * offset)) for i in range(count)])
 
 
 def per_device(inputs, out_grad, weight, neighbours, orients):
@@ -363,43 +385,43 @@
     whole = 9 * width * width
     lanes = 3 * LANES
     me = lax.axis_index("tile").reshape(1)
+    neighbours, orients = neighbours.T, orients.T
     grad = out_grad.reshape(pixels, width)
     flat_in = inputs.reshape(pixels, width)
     scale = 1.0 / math.sqrt(count * inputs.shape[0] * pixels)
     slot = (5 * side // 2, LANES)
     shifted = [pltpu.VMEM((pixels + 2 * side, lanes), jnp.bfloat16)] * 3
     sums = (3, 9 * width, LANES)
-    even = whole % (2 * width * count) == 0
+    even = count == 16 and whole % (2 * width * count) == 0
     pairs = whole // (2 * width * count)
     message = (5 * GROUP, LANES)
 
-    if even:
-        packed = pl.pallas_call(
-            functools.partial(pack_kernel, pairs),
-            out_shape=jax.ShapeDtypeStruct((1,) + message, jnp.bfloat16),
-            in_specs=[VMEM],
-            out_specs=VMEM,
-            scratch_shapes=[pltpu.VMEM((5 * pairs, LANES), jnp.float32)],
-            name="pack_kernel",
-        )(weight.reshape(-1, LANES))
-        places = gather_places(chips)
-        step = chips // 2
-        held = gather_step(packed, count, step)
-        ready_grad = after(grad, packed)
-    else:
+    if not even:
         flat_kernel = lax.all_gather(weight, "tile", axis=0, tiled=True).reshape(9 * width, width)
-        ready_grad = grad
 
     slots = pl.pallas_call(
         functools.partial(pack_borders, side, count),
         out_shape=jax.ShapeDtypeStruct((count,) + slot, jnp.bfloat16),
-        in_specs=[SMEM, SMEM, SMEM, VMEM],
+        in_specs=[SMEM, HBM, HBM, HBM],
         out_specs=VMEM,
-        scratch_shapes=[pltpu.VMEM((8,) + slot, jnp.bfloat16)],
-        compiler_params=params(32),
+        scratch_shapes=[
+            pltpu.VMEM((8,) + slot, jnp.bfloat16),
+            pltpu.VMEM((side, width), jnp.bfloat16),
+            pltpu.VMEM((side, width), jnp.bfloat16),
+            pltpu.VMEM((side, 8, width), jnp.bfloat16),
+            pltpu.VMEM((side, 8, width), jnp.bfloat16),
+            pltpu.SMEM(neighbours.shape, jnp.int32),
+            pltpu.SMEM(orients.shape, jnp.int32),
+            pltpu.SemaphoreType.DMA((6,)),
+        ],
+        compiler_params=params(60),
         name="pack_borders",
-    )(me, neighbours, orients, ready_grad)
-    ready_in = after(flat_in, slots)
+    )(me, neighbours, orients, out_grad[0])
+    packed = after(me, slots)
+    if even:
+        shard = after(weight, slots).reshape(1, -1, LANES)
+        shard = jnp.pad(shard, ((0, 0), (0, -shard.shape[1] % 16), (0, 0)))
+        held = jnp.concatenate([shard, from_offset(shard, count, 1)], axis=0)
     slots = lax.all_to_all(slots, "tile", 0, 0, tiled=True)
 
     inner, edges = pl.pallas_call(
@@ -408,20 +430,17 @@
             jax.ShapeDtypeStruct(sums, jnp.float32),
             jax.ShapeDtypeStruct((width, 4 * side), jnp.bfloat16),
         ),
-        in_specs=[VMEM, VMEM],
+        in_specs=[SMEM, VMEM, VMEM],
         out_specs=(VMEM, VMEM),
         scratch_shapes=[pltpu.VMEM((width, pixels), jnp.bfloat16)] + shifted,
-        compiler_params=params(48),
+        compiler_params=params(20),
         cost_estimate=pl.CostEstimate(
             flops=18 * pixels * width * width, bytes_accessed=6 << 20, transcendentals=0
         ),
         name="inner_term",
-    )(ready_in, grad)
+    )(packed, flat_in, grad)
 
     if even:
-        if step > 1:
-            step //= 2
-            held = gather_step(after(held, edges), count, step)
         keep, send = pl.pallas_call(
             functools.partial(rim_term, side, width, chips, pairs),
             out_shape=(
@@ -434,25 +453,28 @@
                 pltpu.VMEM(sums, jnp.float32),
                 pltpu.VMEM((count,) + message, jnp.float32),
             ],
-            compiler_params=params(48),
+            compiler_params=params(20),
             name="rim_term",
-        )(me, neighbours, edges, slots, inner)
-        while step > 1:
-            step //= 2
-            held = gather_step(after(held, send), count, step)
-        own, gots = spread_sums(count, pairs, message, me, keep, send)
+        )(after(me, held), neighbours, edges, slots, inner)
+        second = from_offset(held, count, 2)
+        third = from_offset(held, count, 4)
+        own, got, crossing = spread_sums(count, pairs, message, me, keep, send)
+        third = after(third, crossing, second)
+        last = after(from_offset(third, count, 2), own, got[2])
+        held = jnp.concatenate([held, second, third, last], axis=0)
         other = lax.ppermute(after(held, own), "tile", [(i, i ^ 1) for i in range(count)])
         input_grad = pl.pallas_call(
-            functools.partial(input_term, side, width, pairs, places),
+            functools.partial(input_term, side, width, pairs, chips),
             out_shape=jax.ShapeDtypeStruct((pixels, width), jnp.bfloat16),
             in_specs=[SMEM, SMEM] + [VMEM] * 4,
             out_specs=VMEM,
             scratch_shapes=[
                 pltpu.VMEM((9 * width, lanes), jnp.bfloat16),
+                pltpu.VMEM((2, 5 * pairs, LANES), jnp.float32),
                 pltpu.VMEM(sums, jnp.float32),
             ]
             + shifted,
-            compiler_params=params(48),
+            compiler_params=params(26),
             cost_estimate=pl.CostEstimate(
                 flops=18 * pixels * width * width, bytes_accessed=6 << 20, transcendentals=0
             ),
@@ -461,18 +483,18 @@
         weight_grad = pl.pallas_call(
             functools.partial(final_sum, pairs, scale),
             out_shape=jax.ShapeDtypeStruct((5 * pairs, LANES), jnp.float32),
-            in_specs=[VMEM] * chips,
+            in_specs=[VMEM] * (count // 4),
             out_specs=VMEM,
-            compiler_params=params(32),
+            compiler_params=params(8),
             name="final_sum",
-        )(after(own, input_grad), *gots).reshape(-1)
+        )(after(own, input_grad), *got).reshape(-1)
     else:
         parts = pl.pallas_call(
             functools.partial(add_rim, side, width),
             out_shape=jax.ShapeDtypeStruct(sums, jnp.float32),
             in_specs=[SMEM, SMEM, VMEM, VMEM, VMEM],
             out_specs=VMEM,
-            compiler_params=params(48),
+            compiler_params=params(20),
             name="add_rim",
         )(me, neighbours, edges, slots, inner)
         flat_sums = jnp.concatenate(list(parts), axis=1)[:, :width].reshape(-1)
@@ -485,29 +507,38 @@
             in_specs=[SMEM, SMEM] + [VMEM] * 3,
             out_specs=VMEM,
             scratch_shapes=[pltpu.VMEM((9 * width, lanes), jnp.bfloat16)] + shifted,
-            compiler_params=params(48),
+            compiler_params=params(26),
             name="plain_input_term",
         )(me, neighbours, grad, slots, flat_kernel)
     return (input_grad.reshape(inputs.shape), weight_grad)
 
 
 def spread_sums(count, pairs, message, me, keep, send):
-    chips = count // 2
+    rows = count // 4
+    several = jax.ShapeDtypeStruct((rows,) + message, jnp.float32)
+    coded_several = jax.ShapeDtypeStruct((rows,) + message, jnp.int16)
     got = lax.ppermute(send, "tile", [(i, i ^ 1) for i in range(count)])
-    own, *sends = pl.pallas_call(
-        functools.partial(pair_sum, pairs, chips),
-        out_shape=(jax.ShapeDtypeStruct(message, jnp.float32),)
-        + (jax.ShapeDtypeStruct(message, jnp.int16),) * (chips - 1),
+    keep, send = pl.pallas_call(
+        functools.partial(pair_sum, pairs, count // 2),
+        out_shape=(several, coded_several),
         in_specs=[SMEM, VMEM, VMEM],
-        out_specs=(VMEM,) * chips,
-        compiler_params=params(32),
+        out_specs=(VMEM,) * 2,
+        compiler_params=params(12),
         name="pair_sum",
     )(me, keep, got)
-    gots = [
-        lax.ppermute(sends[offset - 1], "tile", [(i, i ^ (2 * offset)) for i in range(count)])
-        for offset in range(1, chips)
-    ]
-    return own, gots
+    crossing = send
+    got = from_offset(send, count, 1)
+    own, *sends = pl.pallas_call(
+        functools.partial(cross_sum, pairs, rows),
+        out_shape=(jax.ShapeDtypeStruct(message, jnp.float32),)
+        + (jax.ShapeDtypeStruct(message, jnp.int16),) * (rows - 1),
+        in_specs=[SMEM, VMEM, VMEM],
+        out_specs=(VMEM,) * rows,
+        compiler_params=params(12),
+        name="cross_sum",
+    )(me, keep, got)
+    got = [from_offset(sends[offset - 1], count, 2 * offset) for offset in range(1, rows)]
+    return own, got, crossing
 
 
 def solution(mesh):

time: 79.4 us -> 65.3 us (0.82)
  starting transfers between devices: 26.1 us -> 19.2 us
  waiting for transfers between devices: 25 us -> 19.9 us
  Pallas kernels: 20.1 us -> 17.5 us
    ppermute x10 -> x8, waiting for transfers between devices: 25 us -> 17 us  [from_offset(): lax.ppermute(value, 'tile', [(i, i ^ 2 * offset) for i in range(count)])]
    ppermute x10 -> x8, starting transfers between devices: 18.6 us -> 11.6 us  [from_offset(): lax.ppermute(value, 'tile', [(i, i ^ 2 * offset) for i in range(count)])]
    ppermute x1, waiting for transfers between devices: 0.01 us -> 2.45 us  [spread_sums(): got = lax.ppermute(send, 'tile', [(i, i ^ 1) for i in range(count)])]
    pallas_call x1, Pallas kernels: 4.31 us -> 2.72 us  [per_device(): pl.pallas_call(functools.partial(rim_term, side, width, chips, pairs), ou...]
    pallas_call x3, Pallas kernels: 8.94 us -> 7.79 us  [the longest x1 6.97 us: per_device(): pl.pallas_call(functools.partial(input_term, side, width, pairs, chips),...]
    pad x0 -> x1, local copies, waits for them, and re-layouts: none -> 0.93 us  [per_device(): shard = jnp.pad(shard, ((0, 0), (0, -shard.shape[1] % 16), (0, 0)))]
  transfers between devices with their start and end apart: 13 -> 11, of which waited for: 6 -> 6; matrix products, arithmetic and copies ran while one was open for 0% -> 2% of each run, Pallas kernels for 18% -> 17%
where the time goes in v3:
time: 65.3 us; the launch traced here: 64.9 us
  waiting for transfers between devices  19.9 us (30%)
  starting transfers between devices  19.2 us (29%)
  Pallas kernels  17.5 us (27%)
  local copies, waits for them, and re-layouts  7.6 us (12%)
  between operations  0.76 us (1%)
    ppermute x8, waiting for transfers between devices, from_offset(): lax.ppermute(value, 'tile', [(i, i ^ 2 * offset) for i in range(count)])  17 us
    ppermute x8, starting transfers between devices, from_offset(): lax.ppermute(value, 'tile', [(i, i ^ 2 * offset) for i in range(count)])  11.6 us
    all_to_all x1, starting transfers between devices, per_device(): slots = lax.all_to_all(slots, 'tile', 0, 0, tiled=True)  7.37 us
    pallas_call x1, Pallas kernels, per_device(): pl.pallas_call(functools.partial(input_term, side, width, pairs, chips),...  6.97 us
    unnamed x15, local copies, waits for them, and re-layouts  6.63 us
    pallas_call x1, Pallas kernels, per_device(): pl.pallas_call(functools.partial(inner_term, side, width), out_shape=(jax...  3.48 us
    pallas_call x1, Pallas kernels, per_device(): pl.pallas_call(functools.partial(rim_term, side, width, chips, pairs), ou...  2.72 us
    pallas_call x1, Pallas kernels, per_device(): pl.pallas_call(functools.partial(pack_borders, side, count), out_shape=ja...  2.66 us
  transfers between devices with their start and end apart: 11, of which 6 were waited for; matrix products, arithmetic and copies ran while one was open for 2% of the time, Pallas kernels for 17%

profile of v3, /device:TPU:0, one launch (start us, length us, event | category | flops | bytes accessed | tf_op | source)
XLA Modules:
  0.0 64.9 jit_solution(9173047457005948383)
XLA Ops:
  0.6 2.7 %pack_borders.1 = bf16[16,80,128]{2,1,0:T(8,128)(2,1)} custom-call(s32[1]{0:T(128)} %bitcast.me_ref.packed_ref, s32[8,16]{1,0:T(8,128)} %bitcast.12, s32[8,16]{1,0:T(8,128)} %bitcast.18, bf16[32,32,320]{2,1,0:T(8,128)(2,1)} %bitcast.9), custom_call_target="tpu_custom_call" | custom-call | tf_op jit(solution)/shard_map/pack_borders/pallas_call | solution.py:402
  3.3 7.4 %all-to-all-start = ((bf16[16,80,128]{2,1,0:T(8,128)(2,1)}), bf16[16,80,128]{2,1,0:T(8,128)(2,1)S(1)}, u32[]{:S(2)}, u32[]{:S(2)}) async-start(bf16[16,80,128]{2,1,0:T(8,128)(2,1)} %pack_borders.1), calls=%async_computation | async-start | bytes 655360 | tf_op jit(solution)/shard_map/all_to_all | solution.py:425
  10.7 0.9 %fusion = (bf16[1,464,128]{2,1,0:T(8,128)(2,1)S(1)}, bf16[8,464,128]{2,1,0:T(8,128)(2,1)S(1)}) fusion(bf16[1,450,128]{2,1,0:T(8,128)(2,1)} %bitcast.17), kind=kLoop, calls=%fused_computation.6 | loop fusion | bytes 352768 | tf_op jit(solution)/shard_map/jit(_pad)/pad | solution.py:423
  11.6 2.0 %collective-permute-start = (bf16[1,464,128]{2,1,0:T(8,128)(2,1)S(1)}, bf16[1,464,128]{2,1,0:T(8,128)(2,1)S(1)}, u32[]{:S(2)}, u32[]{:S(2)}) collective-permute-start(bf16[1,464,128]{2,1,0:T(8,128)(2,1)S(1)} %get-tuple-element.36), channel_id=1, source_target_pairs={{0,2},{1,3},{2,0},{3,1},{4,6},{5,7},{6,4},{7,5},{8,10},{9,11},{10,... | collective-permute-start | bytes 356360 | tf_op jit(solution)/shard_map/ppermute | solution.py:377
  13.6 1.1 %copy-done.2 = bf16[1,32,32,320]{3,2,1,0:T(8,128)(2,1)S(1)} copy-done((bf16[1,32,32,320]{3,2,1,0:T(8,128)(2,1)S(1)}, bf16[1,32,32,320]{3,2,1,0:T(8,128)(2,1)}, u32[]{:S(2)}) %copy-start.2) | copy-done | bytes 655384
  14.8 1.1 %copy-done.5 = bf16[1,32,32,320]{3,2,1,0:T(8,128)(2,1)S(1)} copy-done((bf16[1,32,32,320]{3,2,1,0:T(8,128)(2,1)S(1)}, bf16[1,32,32,320]{3,2,1,0:T(8,128)(2,1)}, u32[]{:S(2)}) %copy-start.5) | copy-done | bytes 655384
  15.9 3.5 %inner_term.1 = (f32[3,2880,128]{2,1,0:T(8,128)S(1)}, bf16[320,128]{1,0:T(8,128)(2,1)S(1)}) custom-call(s32[1]{0:T(128)} %bitcast.me_ref.packed_ref, bf16[1024,320]{1,0:T(8,128)(2,1)S(1)} %bitcast.15, bf16[1024,320]{1,0:T(8,128)(2,1)S(1)} %bitcast.10), custom_call_target="tpu_custom_call" | custom-call | flops 1887436800 | bytes 6291456 | tf_op jit(solution)/shard_map/inner_term/pallas_call | solution.py:427
  19.4 2.0 %copy-done = f32[3,2880,128]{2,1,0:T(8,128)} copy-done((f32[3,2880,128]{2,1,0:T(8,128)}, f32[3,2880,128]{2,1,0:T(8,128)S(1)}, u32[]{:S(2)}) %copy-start) | copy-done | bytes 4423704
  21.4 0.4 all-to-all-done.slots_ref
  21.8 2.3 %copy-done.1 = f32[3,2880,128]{2,1,0:T(8,128)S(1)} copy-done((f32[3,2880,128]{2,1,0:T(8,128)S(1)}, f32[3,2880,128]{2,1,0:T(8,128)}, u32[]{:S(2)}) %copy-start.1) | copy-done | bytes 4423704
  24.1 2.7 %rim_term.1 = (f32[8,480,128]{2,1,0:T(8,128)S(1)}, s16[8,480,128]{2,1,0:T(8,128)(2,1)S(1)}) custom-call(s32[1]{0:T(128)} %bitcast.me_ref.packed_ref, s32[8,16]{1,0:T(8,128)S(1)} %bitcast.13, bf16[320,128]{1,0:T(8,128)(2,1)S(1)} %get-tuple-element.22.edge_ref, bf16[16,80,128]{2,1,0:T(8,128)(2,1)S(1)} %all-to-all-done.slots_ref, f32[3,2880,128]{2,1,0:T(8,128)S(1)} %copy-done.1), custom_call_target="tpu_custom_call" | custom-call | tf_op jit(solution)/shard_map/rim_term/pallas_call | solution.py:444
  27.0 2.5 %collective-permute-done.3.got_ref = s16[8,480,128]{2,1,0:T(8,128)(2,1)S(1)} collective-permute-done((s16[8,480,128]{2,1,0:T(8,128)(2,1)S(1)}, s16[8,480,128]{2,1,0:T(8,128)(2,1)S(1)}, u32[]{:S(2)}, u32[]{:S(2)}) %collective-permute-start.3) | collective-permute-done | bytes 983072 | tf_op jit(solution)/shard_map/ppermute | solution.py:520
  29.4 0.5 pair_sum.1
  29.9 0.5 collective-permute-start.5
  30.4 1.3 %collective-permute-start.1 = (bf16[2,464,128]{2,1,0:T(8,128)(2,1)S(1)}, bf16[2,464,128]{2,1,0:T(8,128)(2,1)S(1)}, u32[]{:S(2)}, u32[]{:S(2)}) collective-permute-start(bf16[2,464,128]{2,1,0:T(8,128)(2,1)S(1)} %pad_maximum_fusion), channel_id=1, source_target_pairs={{0,4},{1,5},{2,6},{3,7},{4,0},{5,1},{6,2},{7,3},{8,12},{9,13},{10,... | collective-permute-start | bytes 712712 | tf_op jit(solution)/shard_map/ppermute | solution.py:377
  31.7 2.4 %collective-permute-start.2 = (bf16[2,464,128]{2,1,0:T(8,128)(2,1)S(1)}, bf16[2,464,128]{2,1,0:T(8,128)(2,1)S(1)}, u32[]{:S(2)}, u32[]{:S(2)}) collective-permute-start(bf16[2,464,128]{2,1,0:T(8,128)(2,1)S(1)} %pad_maximum_fusion), channel_id=1, source_target_pairs={{0,8},{1,9},{2,10},{3,11},{4,12},{5,13},{6,14},{7,15},{8,0},{9,1},... | collective-permute-start | bytes 712712 | tf_op jit(solution)/shard_map/ppermute | solution.py:377
  34.1 9.0 %collective-permute-done.1 = bf16[2,464,128]{2,1,0:T(8,128)(2,1)S(1)} collective-permute-done((bf16[2,464,128]{2,1,0:T(8,128)(2,1)S(1)}, bf16[2,464,128]{2,1,0:T(8,128)(2,1)S(1)}, u32[]{:S(2)}, u32[]{:S(2)}) %collective-permute-start.1) | collective-permute-done | bytes 237600 | tf_op jit(solution)/shard_map/ppermute | solution.py:377
  43.1 1.9 %collective-permute-done.2 = bf16[2,464,128]{2,1,0:T(8,128)(2,1)S(1)} collective-permute-done((bf16[2,464,128]{2,1,0:T(8,128)(2,1)S(1)}, bf16[2,464,128]{2,1,0:T(8,128)(2,1)S(1)}, u32[]{:S(2)}, u32[]{:S(2)}) %collective-permute-start.2) | collective-permute-done | bytes 237600 | tf_op jit(solution)/shard_map/ppermute | solution.py:377
  45.7 2.2 %collective-permute-start.6 = (s16[480,128]{1,0:T(8,128)(2,1)S(1)}, s16[480,128]{1,0:T(8,128)(2,1)S(1)}, u32[]{:S(2)}, u32[]{:S(2)}) collective-permute-start(s16[480,128]{1,0:T(8,128)(2,1)S(1)} %get-tuple-element.30), channel_id=1, source_target_pairs={{0,12},{1,13},{2,14},{3,15},{4,8},{5,9},{6,10},{7,11},{8,4},{9,5},... | collective-permute-start | bytes 368648 | tf_op jit(solution)/shard_map/ppermute | solution.py:377
  47.9 4.5 %collective-permute-done.4 = bf16[2,464,128]{2,1,0:T(8,128)(2,1)S(1)} collective-permute-done((bf16[2,464,128]{2,1,0:T(8,128)(2,1)S(1)}, bf16[2,464,128]{2,1,0:T(8,128)(2,1)S(1)}, u32[]{:S(2)}, u32[]{:S(2)}) %collective-permute-start.4) | collective-permute-done | bytes 237600 | tf_op jit(solution)/shard_map/ppermute | solution.py:377
  52.4 1.6 %collective-permute-done.6.refs_2_ = s16[480,128]{1,0:T(8,128)(2,1)S(1)} collective-permute-done((s16[480,128]{1,0:T(8,128)(2,1)S(1)}, s16[480,128]{1,0:T(8,128)(2,1)S(1)}, u32[]{:S(2)}, u32[]{:S(2)}) %collective-permute-start.6) | collective-permute-done | bytes 122912 | tf_op jit(solution)/shard_map/ppermute | solution.py:377
  54.2 2.9 %collective-permute-start.9 = (s16[480,128]{1,0:T(8,128)(2,1)S(1)}, s16[480,128]{1,0:T(8,128)(2,1)S(1)}, u32[]{:S(2)}, u32[]{:S(2)}) collective-permute-start(s16[480,128]{1,0:T(8,128)(2,1)S(1)} %get-tuple-element.35), channel_id=1, source_target_pairs={{0,8},{1,9},{2,10},{3,11},{4,12},{5,13},{6,14},{7,15},{8,0},{9,1},... | collective-permute-start | bytes 368648 | tf_op jit(solution)/shard_map/ppermute | solution.py:377
  57.1 7.0 %input_term.1 = bf16[1024,320]{1,0:T(8,128)(2,1)} custom-call(s32[1]{0:T(128)} %bitcast.me_ref.packed_ref, s32[8,16]{1,0:T(8,128)S(1)} %bitcast.14, bf16[1024,320]{1,0:T(8,128)(2,1)S(1)} %bitcast.11, bf16[16,80,128]{2,1,0:T(8,128)(2,1)S(1)} %all-to-all-done.slots_ref, bf16[8,464,128]{2,1,0:T(8,128)(2,1)S(1)} %constant_dynamic-update-slice_fusion.mine_ref, ...), custom_call_target="tpu_custom_call" | custom-call | flops 1887436800 | bytes 6291456 | tf_op jit(solution)/shard_map/input_term/pallas_call | solution.py:466
  64.1 0.8 %final_sum.1 = f32[450,128]{1,0:T(8,128)} custom-call(f32[480,128]{1,0:T(8,128)S(1)} %get-tuple-element.33.own_ref, s16[480,128]{1,0:T(8,128)(2,1)S(1)} %collective-permute-done.8.refs_0_, s16[480,128]{1,0:T(8,128)(2,1)S(1)} %collective-permute-done.9.refs_1_, s16[480,128]{1,0:T(8,128)(2,1)S(1)} %collective-permute-done.6.refs_2_), custom_call_target="tpu_custom_call" | custom-call | tf_op jit(solution)/shard_map/final_sum/pallas_call | solution.py:483
  (23 shorter events, 1.1 us)
Async XLA Ops:
  3.3 18.5 %copy-start.4 = (s32[16,8]{0,1:T(8,128)S(1)}, s32[16,8]{0,1:T(8,128)}, u32[]{:S(2)}) copy-start(s32[16,8]{0,1:T(8,128)} %param.8) | copy-start | bytes 1540
  3.3 18.5 %all-to-all-start = ((bf16[16,80,128]{2,1,0:T(8,128)(2,1)}), bf16[16,80,128]{2,1,0:T(8,128)(2,1)S(1)}, u32[]{:S(2)}, u32[]{:S(2)}) async-start(bf16[16,80,128]{2,1,0:T(8,128)(2,1)} %pack_borders.1), calls=%async_computation | async-start | bytes 655360 | tf_op jit(solution)/shard_map/all_to_all | solution.py:425
  11.6 9.8 %collective-permute-start = (bf16[1,464,128]{2,1,0:T(8,128)(2,1)S(1)}, bf16[1,464,128]{2,1,0:T(8,128)(2,1)S(1)}, u32[]{:S(2)}, u32[]{:S(2)}) collective-permute-start(bf16[1,464,128]{2,1,0:T(8,128)(2,1)S(1)} %get-tuple-element.36), channel_id=1, source_target_pairs={{0,2},{1,3},{2,0},{3,1},{4,6},{5,7},{6,4},{7,5},{8,10},{9,11},{10,... | collective-permute-start | bytes 356360 | tf_op jit(solution)/shard_map/ppermute | solution.py:377
  13.6 1.1 %copy-start.2 = (bf16[1,32,32,320]{3,2,1,0:T(8,128)(2,1)S(1)}, bf16[1,32,32,320]{3,2,1,0:T(8,128)(2,1)}, u32[]{:S(2)}) copy-start(bf16[1,32,32,320]{3,2,1,0:T(8,128)(2,1)} %param.6) | copy-start | bytes 1966084
  14.8 1.1 %copy-start.5 = (bf16[1,32,32,320]{3,2,1,0:T(8,128)(2,1)S(1)}, bf16[1,32,32,320]{3,2,1,0:T(8,128)(2,1)}, u32[]{:S(2)}) copy-start(bf16[1,32,32,320]{3,2,1,0:T(8,128)(2,1)} %param.5) | copy-start | bytes 1966084
  19.4 2.0 %copy-start = (f32[3,2880,128]{2,1,0:T(8,128)}, f32[3,2880,128]{2,1,0:T(8,128)S(1)}, u32[]{:S(2)}) copy-start(f32[3,2880,128]{2,1,0:T(8,128)S(1)} %get-tuple-element.23.inner_ref) | copy-start | bytes 13271044
  21.8 2.3 %copy-start.1 = (f32[3,2880,128]{2,1,0:T(8,128)S(1)}, f32[3,2880,128]{2,1,0:T(8,128)}, u32[]{:S(2)}) copy-start(f32[3,2880,128]{2,1,0:T(8,128)} %copy-done) | copy-start | bytes 13271044
  24.0 33.1 %copy-start.3 = (bf16[1,32,32,320]{3,2,1,0:T(8,128)(2,1)S(1)}, bf16[1,32,32,320]{3,2,1,0:T(8,128)(2,1)}, u32[]{:S(2)}) copy-start(bf16[1,32,32,320]{3,2,1,0:T(8,128)(2,1)} %param.6) | copy-start | bytes 1966084
  26.8 2.6 %collective-permute-start.3 = (s16[8,480,128]{2,1,0:T(8,128)(2,1)S(1)}, s16[8,480,128]{2,1,0:T(8,128)(2,1)S(1)}, u32[]{:S(2)}, u32[]{:S(2)}) collective-permute-start(s16[8,480,128]{2,1,0:T(8,128)(2,1)S(1)} %get-tuple-element.25), channel_id=1, source_target_pairs={{0,1},{1,0},{2,3},{3,2},{4,5},{5,4},{6,7},{7,6},{8,9},{9,8},{10,11... | collective-permute-start | bytes 2949128 | tf_op jit(solution)/shard_map/ppermute | solution.py:520
  29.9 15.4 %collective-permute-start.5 = (s16[4,480,128]{2,1,0:T(8,128)(2,1)S(1)}, s16[4,480,128]{2,1,0:T(8,128)(2,1)S(1)}, u32[]{:S(2)}, u32[]{:S(2)}) collective-permute-start(s16[4,480,128]{2,1,0:T(8,128)(2,1)S(1)} %get-tuple-element.26), channel_id=1, source_target_pairs={{0,2},{1,3},{2,0},{3,1},{4,6},{5,7},{6,4},{7,5},{8,10},{9,11},{10,... | collective-permute-start | bytes 1474568 | tf_op jit(solution)/shard_map/ppermute | solution.py:377
  30.4 12.6 %collective-permute-start.1 = (bf16[2,464,128]{2,1,0:T(8,128)(2,1)S(1)}, bf16[2,464,128]{2,1,0:T(8,128)(2,1)S(1)}, u32[]{:S(2)}, u32[]{:S(2)}) collective-permute-start(bf16[2,464,128]{2,1,0:T(8,128)(2,1)S(1)} %pad_maximum_fusion), channel_id=1, source_target_pairs={{0,4},{1,5},{2,6},{3,7},{4,0},{5,1},{6,2},{7,3},{8,12},{9,13},{10,... | collective-permute-start | bytes 712712 | tf_op jit(solution)/shard_map/ppermute | solution.py:377
  31.7 13.3 %collective-permute-start.2 = (bf16[2,464,128]{2,1,0:T(8,128)(2,1)S(1)}, bf16[2,464,128]{2,1,0:T(8,128)(2,1)S(1)}, u32[]{:S(2)}, u32[]{:S(2)}) collective-permute-start(bf16[2,464,128]{2,1,0:T(8,128)(2,1)S(1)} %pad_maximum_fusion), channel_id=1, source_target_pairs={{0,8},{1,9},{2,10},{3,11},{4,12},{5,13},{6,14},{7,15},{8,0},{9,1},... | collective-permute-start | bytes 712712 | tf_op jit(solution)/shard_map/ppermute | solution.py:377
  45.0 7.4 %collective-permute-start.4 = (bf16[2,464,128]{2,1,0:T(8,128)(2,1)S(1)}, bf16[2,464,128]{2,1,0:T(8,128)(2,1)S(1)}, u32[]{:S(2)}, u32[]{:S(2)}) collective-permute-start(bf16[2,464,128]{2,1,0:T(8,128)(2,1)S(1)} %collective-permute-done.2), channel_id=1, source_target_pairs={{0,4},{1,5},{2,6},{3,7},{4,0},{5,1},{6,2},{7,3},{8,12},{9,13},{10,... | collective-permute-start | bytes 712712 | tf_op jit(solution)/shard_map/ppermute | solution.py:377
  45.7 8.3 %collective-permute-start.6 = (s16[480,128]{1,0:T(8,128)(2,1)S(1)}, s16[480,128]{1,0:T(8,128)(2,1)S(1)}, u32[]{:S(2)}, u32[]{:S(2)}) collective-permute-start(s16[480,128]{1,0:T(8,128)(2,1)S(1)} %get-tuple-element.30), channel_id=1, source_target_pairs={{0,12},{1,13},{2,14},{3,15},{4,8},{5,9},{6,10},{7,11},{8,4},{9,5},... | collective-permute-start | bytes 368648 | tf_op jit(solution)/shard_map/ppermute | solution.py:377
  54.1 3.1 %collective-permute-start.7 = (bf16[8,464,128]{2,1,0:T(8,128)(2,1)S(1)}, bf16[8,464,128]{2,1,0:T(8,128)(2,1)S(1)}, u32[]{:S(2)}, u32[]{:S(2)}) collective-permute-start(bf16[8,464,128]{2,1,0:T(8,128)(2,1)S(1)} %constant_dynamic-update-slice_fusion.mine_ref), channel_id=1, source_target_pairs={{0,1},{1,0},{2,3},{3,2},{4,5},{5,4},{6,7},{7,6},{8,9},{9,8},{10,11... | collective-permute-start | bytes 2850824 | tf_op jit(solution)/shard_map/ppermute | solution.py:465
  54.1 10.0 %collective-permute-start.8 = (s16[480,128]{1,0:T(8,128)(2,1)S(1)}, s16[480,128]{1,0:T(8,128)(2,1)S(1)}, u32[]{:S(2)}, u32[]{:S(2)}) collective-permute-start(s16[480,128]{1,0:T(8,128)(2,1)S(1)} %get-tuple-element.34), channel_id=1, source_target_pairs={{0,4},{1,5},{2,6},{3,7},{4,0},{5,1},{6,2},{7,3},{8,12},{9,13},{10,... | collective-permute-start | bytes 368648 | tf_op jit(solution)/shard_map/ppermute | solution.py:377
  54.2 9.9 %collective-permute-start.9 = (s16[480,128]{1,0:T(8,128)(2,1)S(1)}, s16[480,128]{1,0:T(8,128)(2,1)S(1)}, u32[]{:S(2)}, u32[]{:S(2)}) collective-permute-start(s16[480,128]{1,0:T(8,128)(2,1)S(1)} %get-tuple-element.35), channel_id=1, source_target_pairs={{0,8},{1,9},{2,10},{3,11},{4,12},{5,13},{6,14},{7,15},{8,0},{9,1},... | collective-permute-start | bytes 368648 | tf_op jit(solution)/shard_map/ppermute | solution.py:377

commit v4 on v3

--- a/solution.py
+++ b/solution.py
@@ -67,7 +67,7 @@
     side, count,
     me_ref, nbr_in_ref, turn_in_ref, grad_in_ref,
     slots_ref,
-    strips_ref, top_ref, bottom_ref, left_ref, right_ref, nbr_ref, turn_ref, sems,
+    strips_ref, top_ref, bottom_ref, left_ref, right_ref, nbr_ref, turn_ref, which_ref, sems,
 ):
     near = left_ref.shape[1]
     half = side // 2
@@ -98,7 +98,21 @@
     column = lax.broadcasted_iota(jnp.int32, (8 * side, known), 1)
     pick = jnp.where(column == target, 1.0, 0.0).astype(jnp.bfloat16)
     low = low_half(half)
-    for copy in copies:
+    me = me_ref[0]
+    for copy in copies[4:]:
+        copy.wait()
+
+    def choose(dest, carry):
+        which = jnp.int32(0)
+        for direction in range(8):
+            turn = turn_ref[direction, dest]
+            found = (strip_code(direction) >> (4 * turn)) & 15
+            which = jnp.where(nbr_ref[direction, dest] == me, found, which)
+        which_ref[dest] = which
+        return carry
+
+    lax.fori_loop(0, count, choose, 0, unroll=4)
+    for copy in copies[:4]:
         copy.wait()
     width = top_ref.shape[1]
     pixels = jnp.concatenate(
@@ -118,18 +132,12 @@
         strips_ref[strip % 4 * 2 + strip // 4] = jnp.concatenate(
             [block[:, :LANES], block[:, LANES : 2 * LANES], last], axis=0
         ).astype(jnp.bfloat16)
-    me = me_ref[0]
 
     def fill(dest, carry):
-        which = jnp.int32(0)
-        for direction in range(8):
-            turn = turn_ref[direction, dest]
-            found = (strip_code(direction) >> (4 * turn)) & 15
-            which = jnp.where(nbr_ref[direction, dest] == me, found, which)
-        slots_ref[dest] = strips_ref[which]
+        slots_ref[dest] = strips_ref[which_ref[dest]]
         return carry
 
-    lax.fori_loop(0, count, fill, 0)
+    lax.fori_loop(0, count, fill, 0, unroll=8)
 
 
 def rim_pieces(side, me_ref, nbr_ref, slots_ref):
@@ -152,7 +160,7 @@
     return (after, rim, before)
 
 
-def fill_shifted(side, own, rims, refs):
+def fill_shifted(side, own, rims, ref):
     pixels, lanes = own.shape
     tall = (side, side, lanes)
     place = lax.broadcasted_iota(jnp.int32, tall, 1)
@@ -171,9 +179,10 @@
             row_shifts(side, south, sw[0:1], se[0:1]),
         ]
     for tap, block in enumerate((after.reshape(own.shape), own, before.reshape(own.shape))):
-        refs[tap][0:side] = outer[0][tap].astype(jnp.bfloat16)
-        refs[tap][side : side + pixels] = block.astype(jnp.bfloat16)
-        refs[tap][side + pixels :] = outer[1][tap].astype(jnp.bfloat16)
+        place = slice(tap * lanes, (tap + 1) * lanes)
+        ref[0:side, place] = outer[0][tap].astype(jnp.bfloat16)
+        ref[side : side + pixels, place] = block.astype(jnp.bfloat16)
+        ref[side + pixels :, place] = outer[1][tap].astype(jnp.bfloat16)
 
 
 def exponent_of(peak):
@@ -200,7 +209,7 @@
     return jnp.where(row == rows, 0.0, value)
 
 
-def inner_term(side, width, packed_ref, in_ref, grad_ref, acc_ref, edge_ref, in_t_ref, *shifted):
+def inner_term(side, width, packed_ref, in_ref, grad_ref, acc_ref, edge_ref, in_t_ref, shifted):
     pixels = side * side
     own = widened(grad_ref[...].astype(jnp.float32), width)
     fill_shifted(side, own, None, shifted)
@@ -208,14 +217,13 @@
     edge_ref[...] = edges.T.astype(jnp.bfloat16)
     in_t_ref[...] = in_ref[...].T
     for row_tap in range(3):
+        window = shifted[(2 - row_tap) * side : (2 - row_tap) * side + pixels]
+        term = jnp.dot(in_t_ref[...], window, preferred_element_type=jnp.float32)
         for col_tap in range(3):
-            window = shifted[col_tap][(2 - row_tap) * side : (2 - row_tap) * side + pixels]
             tap = 3 * row_tap + col_tap
-            term = jnp.dot(in_t_ref[...], window, preferred_element_type=jnp.float32)
             for part in range(3):
-                acc_ref[part, tap * width : (tap + 1) * width] = term[
-                    :, part * LANES : (part + 1) * LANES
-                ]
+                place = (3 * col_tap + part) * LANES
+                acc_ref[part, tap * width : (tap + 1) * width] = term[:, place : place + LANES]
 
 
 def add_rim(side, width, me_ref, nbr_ref, edge_ref, slots_ref, inner_ref, acc_ref):
@@ -258,22 +266,29 @@
     add_rim(side, width, me_ref, nbr_ref, edge_ref, slots_ref, inner_ref, acc_ref)
     half = LANES // 2
     low = low_half(pairs)
-    for shard in range(2 * chips):
-        base = shard * 2 * pairs
-        even = pl.ds(base, pairs, stride=2)
-        odd = pl.ds(base + 1, pairs, stride=2)
-        e0, e1, e2 = [acc_ref[part, even] for part in range(3)]
-        o0, o1, o2 = [pltpu.roll(acc_ref[part, odd], half, 1) for part in range(3)]
-        groups = (e0, e1, jnp.where(low, e2, o0), jnp.where(low, o0, o1), jnp.where(low, o1, o2))
-        for group, block in enumerate(groups):
-            pack_ref[shard, group * GROUP : group * GROUP + pairs] = block
-            pack_ref[shard, group * GROUP + pairs : (group + 1) * GROUP] = jnp.zeros(
-                (GROUP - pairs, LANES), jnp.float32
+    core = me_ref[0] % 2
+    blank = jnp.zeros((GROUP - pairs, LANES), jnp.float32)
+    for chip in range(chips):
+        for shard, out_ref in (
+            (2 * chip + core, keep_ref.at[chip]),
+            (2 * chip + 1 - core, pack_ref.at[chip % 2]),
+        ):
+            base = shard * 2 * pairs
+            even = pl.ds(base, pairs, stride=2)
+            odd = pl.ds(base + 1, pairs, stride=2)
+            e0, e1, e2 = [acc_ref[part, even] for part in range(3)]
+            o0, o1, o2 = [pltpu.roll(acc_ref[part, odd], half, 1) for part in range(3)]
+            groups = (
+                e0,
+                e1,
+                jnp.where(low, e2, o0),
+                jnp.where(low, o0, o1),
+                jnp.where(low, o1, o2),
             )
-    core = me_ref[0] % 2
-    for chip in range(chips):
-        keep_ref[chip] = pack_ref[2 * chip + core]
-        write_coded(send_ref.at[chip], pack_ref[2 * chip + 1 - core], pairs)
+            for group, block in enumerate(groups):
+                out_ref[group * GROUP : group * GROUP + pairs] = block
+                out_ref[group * GROUP + pairs : (group + 1) * GROUP] = blank
+        write_coded(send_ref.at[chip], pack_ref[chip % 2], pairs)
 
 
 def pair_sum(pairs, chips, me_ref, keep_ref, got_ref, own_ref, send_ref):
@@ -334,26 +349,41 @@
 def input_sums(side, width, me_ref, nbr_ref, grad_ref, slots_ref, kernel_ref, out_ref, shifted):
     own = widened(grad_ref[...].astype(jnp.float32), width)
     fill_shifted(side, own, rim_pieces(side, me_ref, nbr_ref, slots_ref), shifted)
-    chunk = side * side // 4
-    for part in range(4):
-        total = jnp.zeros((chunk, width), jnp.float32)
-        for row_tap in range(3):
-            for col_tap in range(3):
-                start = (2 - row_tap) * side + part * chunk
-                tap = 3 * row_tap + col_tap
-                total = total + lax.dot_general(
-                    shifted[col_tap][start : start + chunk],
-                    kernel_ref[tap * width : (tap + 1) * width],
-                    (((1,), (1,)), ((), ())),
-                    preferred_element_type=jnp.float32,
-                )
-        out_ref[part * chunk : (part + 1) * chunk] = total.astype(jnp.bfloat16)
+    pixels = side * side
+    main = 2 * LANES
+    rest = width - main
+    total = jnp.zeros((pixels, main), jnp.float32)
+    for row_tap in range(3):
+        total = total + lax.dot_general(
+            shifted[(2 - row_tap) * side : (2 - row_tap) * side + pixels],
+            kernel_ref[row_tap * width : row_tap * width + main],
+            (((1,), (1,)), ((), ())),
+            preferred_element_type=jnp.float32,
+        )
+    out_ref[:, :main] = total.astype(jnp.bfloat16)
+    tails = lax.dot_general(
+        shifted[...],
+        jnp.concatenate(
+            [kernel_ref[tap * width + main : (tap + 1) * width] for tap in range(3)], axis=0
+        ),
+        (((1,), (1,)), ((), ())),
+        preferred_element_type=jnp.float32,
+    )
+    first = tails[2 * side : 2 * side + pixels, :rest]
+    second = tails[side : side + pixels, rest : 2 * rest]
+    third = tails[:pixels, 2 * rest :]
+    out_ref[:, main:] = (first + second + third).astype(jnp.bfloat16)
 
 
 def plain_input_term(
-    side, width, me_ref, nbr_ref, grad_ref, slots_ref, flat_ref, out_ref, kernel_ref, *shifted
+    side, width, me_ref, nbr_ref, grad_ref, slots_ref, flat_ref, out_ref, kernel_ref, shifted
 ):
-    kernel_ref[...] = widened(flat_ref[...].astype(jnp.float32), width).astype(jnp.bfloat16)
+    for tap in range(9):
+        rows = widened(flat_ref[tap * width : (tap + 1) * width].astype(jnp.float32), width)
+        place = tap % 3 * rows.shape[1]
+        kernel_ref[
+            tap // 3 * width : (tap // 3 + 1) * width, place : place + rows.shape[1]
+        ] = rows.astype(jnp.bfloat16)
     input_sums(side, width, me_ref, nbr_ref, grad_ref, slots_ref, kernel_ref, out_ref, shifted)
 
 
@@ -361,11 +391,15 @@
     side, width, pairs, chips,
     me_ref, nbr_ref, grad_ref, slots_ref, mine_ref, other_ref,
     out_ref,
-    kernel_ref, shard_ref, rows_ref, *shifted,
+    kernel_ref, shard_ref, rows_ref, shifted,
 ):
     unpack_kernel(pairs, chips, me_ref, mine_ref, other_ref, shard_ref, rows_ref)
-    for part in range(3):
-        kernel_ref[:, part * LANES : (part + 1) * LANES] = rows_ref[part].astype(jnp.bfloat16)
+    for tap in range(9):
+        for part in range(3):
+            place = (tap % 3 * 3 + part) * LANES
+            kernel_ref[
+                tap // 3 * width : (tap // 3 + 1) * width, place : place + LANES
+            ] = rows_ref[part, tap * width : (tap + 1) * width].astype(jnp.bfloat16)
     input_sums(side, width, me_ref, nbr_ref, grad_ref, slots_ref, kernel_ref, out_ref, shifted)
 
 
@@ -390,7 +424,7 @@
     flat_in = inputs.reshape(pixels, width)
     scale = 1.0 / math.sqrt(count * inputs.shape[0] * pixels)
     slot = (5 * side // 2, LANES)
-    shifted = [pltpu.VMEM((pixels + 2 * side, lanes), jnp.bfloat16)] * 3
+    shifted = [pltpu.VMEM((pixels + 2 * side, 3 * lanes), jnp.bfloat16)]
     sums = (3, 9 * width, LANES)
     even = count == 16 and whole % (2 * width * count) == 0
     pairs = whole // (2 * width * count)
@@ -412,6 +446,7 @@
             pltpu.VMEM((side, 8, width), jnp.bfloat16),
             pltpu.SMEM(neighbours.shape, jnp.int32),
             pltpu.SMEM(orients.shape, jnp.int32),
+            pltpu.SMEM((count,), jnp.int32),
             pltpu.SemaphoreType.DMA((6,)),
         ],
         compiler_params=params(60),
@@ -451,7 +486,7 @@
             out_specs=(VMEM,) * 2,
             scratch_shapes=[
                 pltpu.VMEM(sums, jnp.float32),
-                pltpu.VMEM((count,) + message, jnp.float32),
+                pltpu.VMEM((2,) + message, jnp.float32),
             ],
             compiler_params=params(20),
             name="rim_term",
@@ -469,7 +504,7 @@
             in_specs=[SMEM, SMEM] + [VMEM] * 4,
             out_specs=VMEM,
             scratch_shapes=[
-                pltpu.VMEM((9 * width, lanes), jnp.bfloat16),
+                pltpu.VMEM((3 * width, 3 * lanes), jnp.bfloat16),
                 pltpu.VMEM((2, 5 * pairs, LANES), jnp.float32),
                 pltpu.VMEM(sums, jnp.float32),
             ]
@@ -506,7 +541,7 @@
             out_shape=jax.ShapeDtypeStruct((pixels, width), jnp.bfloat16),
             in_specs=[SMEM, SMEM] + [VMEM] * 3,
             out_specs=VMEM,
-            scratch_shapes=[pltpu.VMEM((9 * width, lanes), jnp.bfloat16)] + shifted,
+            scratch_shapes=[pltpu.VMEM((3 * width, 3 * lanes), jnp.bfloat16)] + shifted,
             compiler_params=params(26),
             name="plain_input_term",
         )(me, neighbours, grad, slots, flat_kernel)

time: 65.3 us -> 64.4 us (0.986)
  waiting for transfers between devices: 19.9 us -> 22.9 us
  Pallas kernels: 17.5 us -> 15.2 us
  starting transfers between devices: 19.2 us -> 17.6 us
    ppermute x8, waiting for transfers between devices: 17 us -> 19.5 us  [from_offset(): lax.ppermute(value, 'tile', [(i, i ^ 2 * offset) for i in range(count)])]
    ppermute x8, starting transfers between devices: 11.6 us -> 9.96 us  [from_offset(): lax.ppermute(value, 'tile', [(i, i ^ 2 * offset) for i in range(count)])]
    pallas_call x1, Pallas kernels: 6.97 us -> 5.52 us  [per_device(): pl.pallas_call(functools.partial(input_term, side, width, pairs, chips),...]
  transfers between devices with their start and end apart: 11 -> 11, of which waited for: 6 -> 8; matrix products, arithmetic and copies ran while one was open for 2% -> 2% of each run, Pallas kernels for 17% -> 14%
where the time goes in v4:
time: 64.4 us; the launch traced here: 64.1 us
  waiting for transfers between devices  22.9 us (36%)
  starting transfers between devices  17.6 us (27%)
  Pallas kernels  15.2 us (24%)
  local copies, waits for them, and re-layouts  7.6 us (12%)
  between operations  0.76 us (1%)
    ppermute x8, waiting for transfers between devices, from_offset(): lax.ppermute(value, 'tile', [(i, i ^ 2 * offset) for i in range(count)])  19.5 us
    ppermute x8, starting transfers between devices, from_offset(): lax.ppermute(value, 'tile', [(i, i ^ 2 * offset) for i in range(count)])  9.96 us
    all_to_all x1, starting transfers between devices, per_device(): slots = lax.all_to_all(slots, 'tile', 0, 0, tiled=True)  7.37 us
    unnamed x15, local copies, waits for them, and re-layouts  6.63 us
    pallas_call x1, Pallas kernels, per_device(): pl.pallas_call(functools.partial(input_term, side, width, pairs, chips),...  5.52 us
    pallas_call x1, Pallas kernels, per_device(): pl.pallas_call(functools.partial(inner_term, side, width), out_shape=(jax...  3 us
    pallas_call x1, Pallas kernels, per_device(): pl.pallas_call(functools.partial(rim_term, side, width, chips, pairs), ou...  2.59 us
    pallas_call x1, Pallas kernels, per_device(): pl.pallas_call(functools.partial(pack_borders, side, count), out_shape=ja...  2.48 us
  transfers between devices with their start and end apart: 11, of which 8 were waited for; matrix products, arithmetic and copies ran while one was open for 2% of the time, Pallas kernels for 14%

profile of v4, /device:TPU:0, one launch (start us, length us, event | category | flops | bytes accessed | tf_op | source)
XLA Modules:
  0.0 64.1 jit_solution(3153957921162836215)
XLA Ops:
  0.6 2.5 %pack_borders.1 = bf16[16,80,128]{2,1,0:T(8,128)(2,1)} custom-call(s32[1]{0:T(128)} %bitcast.me_ref.packed_ref, s32[8,16]{1,0:T(8,128)} %bitcast.12, s32[8,16]{1,0:T(8,128)} %bitcast.18, bf16[32,32,320]{2,1,0:T(8,128)(2,1)} %bitcast.9), custom_call_target="tpu_custom_call" | custom-call | tf_op jit(solution)/shard_map/pack_borders/pallas_call | solution.py:436
  3.1 7.4 %all-to-all-start = ((bf16[16,80,128]{2,1,0:T(8,128)(2,1)}), bf16[16,80,128]{2,1,0:T(8,128)(2,1)S(1)}, u32[]{:S(2)}, u32[]{:S(2)}) async-start(bf16[16,80,128]{2,1,0:T(8,128)(2,1)} %pack_borders.1), calls=%async_computation | async-start | bytes 655360 | tf_op jit(solution)/shard_map/all_to_all | solution.py:460
  10.5 0.9 %fusion = (bf16[1,464,128]{2,1,0:T(8,128)(2,1)S(1)}, bf16[8,464,128]{2,1,0:T(8,128)(2,1)S(1)}) fusion(bf16[1,450,128]{2,1,0:T(8,128)(2,1)} %bitcast.17), kind=kLoop, calls=%fused_computation.6 | loop fusion | bytes 352768 | tf_op jit(solution)/shard_map/jit(_pad)/pad | solution.py:458
  11.4 2.0 %collective-permute-start = (bf16[1,464,128]{2,1,0:T(8,128)(2,1)S(1)}, bf16[1,464,128]{2,1,0:T(8,128)(2,1)S(1)}, u32[]{:S(2)}, u32[]{:S(2)}) collective-permute-start(bf16[1,464,128]{2,1,0:T(8,128)(2,1)S(1)} %get-tuple-element.36), channel_id=1, source_target_pairs={{0,2},{1,3},{2,0},{3,1},{4,6},{5,7},{6,4},{7,5},{8,10},{9,11},{10,... | collective-permute-start | bytes 356360 | tf_op jit(solution)/shard_map/ppermute | solution.py:411
  13.4 1.1 %copy-done.2 = bf16[1,32,32,320]{3,2,1,0:T(8,128)(2,1)S(1)} copy-done((bf16[1,32,32,320]{3,2,1,0:T(8,128)(2,1)S(1)}, bf16[1,32,32,320]{3,2,1,0:T(8,128)(2,1)}, u32[]{:S(2)}) %copy-start.2) | copy-done | bytes 655384
  14.6 1.1 %copy-done.5 = bf16[1,32,32,320]{3,2,1,0:T(8,128)(2,1)S(1)} copy-done((bf16[1,32,32,320]{3,2,1,0:T(8,128)(2,1)S(1)}, bf16[1,32,32,320]{3,2,1,0:T(8,128)(2,1)}, u32[]{:S(2)}) %copy-start.5) | copy-done | bytes 655384
  15.7 3.0 %inner_term.1 = (f32[3,2880,128]{2,1,0:T(8,128)S(1)}, bf16[320,128]{1,0:T(8,128)(2,1)S(1)}) custom-call(s32[1]{0:T(128)} %bitcast.me_ref.packed_ref, bf16[1024,320]{1,0:T(8,128)(2,1)S(1)} %bitcast.15, bf16[1024,320]{1,0:T(8,128)(2,1)S(1)} %bitcast.10), custom_call_target="tpu_custom_call" | custom-call | flops 1887436800 | bytes 6291456 | tf_op jit(solution)/shard_map/inner_term/pallas_call | solution.py:462
  18.7 2.0 %copy-done = f32[3,2880,128]{2,1,0:T(8,128)} copy-done((f32[3,2880,128]{2,1,0:T(8,128)}, f32[3,2880,128]{2,1,0:T(8,128)S(1)}, u32[]{:S(2)}) %copy-start) | copy-done | bytes 4423704
  20.8 0.8 %all-to-all-done.slots_ref = bf16[16,80,128]{2,1,0:T(8,128)(2,1)S(1)} async-done(((bf16[16,80,128]{2,1,0:T(8,128)(2,1)}), bf16[16,80,128]{2,1,0:T(8,128)(2,1)S(1)}, u32[]{:S(2)}, u32[]{:S(2)}) %all-to-all-start) | async-done | bytes 327712 | tf_op jit(solution)/shard_map/all_to_all | solution.py:460
  21.6 2.3 %copy-done.1 = f32[3,2880,128]{2,1,0:T(8,128)S(1)} copy-done((f32[3,2880,128]{2,1,0:T(8,128)S(1)}, f32[3,2880,128]{2,1,0:T(8,128)}, u32[]{:S(2)}) %copy-start.1) | copy-done | bytes 4423704
  23.9 2.6 %rim_term.1 = (f32[8,480,128]{2,1,0:T(8,128)S(1)}, s16[8,480,128]{2,1,0:T(8,128)(2,1)S(1)}) custom-call(s32[1]{0:T(128)} %bitcast.me_ref.packed_ref, s32[8,16]{1,0:T(8,128)S(1)} %bitcast.13, bf16[320,128]{1,0:T(8,128)(2,1)S(1)} %get-tuple-element.22.edge_ref, bf16[16,80,128]{2,1,0:T(8,128)(2,1)S(1)} %all-to-all-done.slots_ref, f32[3,2880,128]{2,1,0:T(8,128)S(1)} %copy-done.1), custom_call_target="tpu_custom_call" | custom-call | tf_op jit(solution)/shard_map/rim_term/pallas_call | solution.py:479
  26.6 2.5 %collective-permute-done.3.got_ref = s16[8,480,128]{2,1,0:T(8,128)(2,1)S(1)} collective-permute-done((s16[8,480,128]{2,1,0:T(8,128)(2,1)S(1)}, s16[8,480,128]{2,1,0:T(8,128)(2,1)S(1)}, u32[]{:S(2)}, u32[]{:S(2)}) %collective-permute-start.3) | collective-permute-done | bytes 983072 | tf_op jit(solution)/shard_map/ppermute | solution.py:555
  29.1 0.5 pair_sum.1
  30.1 1.1 %collective-permute-start.1 = (bf16[2,464,128]{2,1,0:T(8,128)(2,1)S(1)}, bf16[2,464,128]{2,1,0:T(8,128)(2,1)S(1)}, u32[]{:S(2)}, u32[]{:S(2)}) collective-permute-start(bf16[2,464,128]{2,1,0:T(8,128)(2,1)S(1)} %pad_maximum_fusion), channel_id=1, source_target_pairs={{0,4},{1,5},{2,6},{3,7},{4,0},{5,1},{6,2},{7,3},{8,12},{9,13},{10,... | collective-permute-start | bytes 712712 | tf_op jit(solution)/shard_map/ppermute | solution.py:411
  31.2 2.1 %collective-permute-start.2 = (bf16[2,464,128]{2,1,0:T(8,128)(2,1)S(1)}, bf16[2,464,128]{2,1,0:T(8,128)(2,1)S(1)}, u32[]{:S(2)}, u32[]{:S(2)}) collective-permute-start(bf16[2,464,128]{2,1,0:T(8,128)(2,1)S(1)} %pad_maximum_fusion), channel_id=1, source_target_pairs={{0,8},{1,9},{2,10},{3,11},{4,12},{5,13},{6,14},{7,15},{8,0},{9,1},... | collective-permute-start | bytes 712712 | tf_op jit(solution)/shard_map/ppermute | solution.py:411
  33.3 9.0 %collective-permute-done.1 = bf16[2,464,128]{2,1,0:T(8,128)(2,1)S(1)} collective-permute-done((bf16[2,464,128]{2,1,0:T(8,128)(2,1)S(1)}, bf16[2,464,128]{2,1,0:T(8,128)(2,1)S(1)}, u32[]{:S(2)}, u32[]{:S(2)}) %collective-permute-start.1) | collective-permute-done | bytes 237600 | tf_op jit(solution)/shard_map/ppermute | solution.py:411
  42.3 2.4 %collective-permute-done.2 = bf16[2,464,128]{2,1,0:T(8,128)(2,1)S(1)} collective-permute-done((bf16[2,464,128]{2,1,0:T(8,128)(2,1)S(1)}, bf16[2,464,128]{2,1,0:T(8,128)(2,1)S(1)}, u32[]{:S(2)}, u32[]{:S(2)}) %collective-permute-start.2) | collective-permute-done | bytes 237600 | tf_op jit(solution)/shard_map/ppermute | solution.py:411
  45.0 2.0 %collective-permute-start.6 = (s16[480,128]{1,0:T(8,128)(2,1)S(1)}, s16[480,128]{1,0:T(8,128)(2,1)S(1)}, u32[]{:S(2)}, u32[]{:S(2)}) collective-permute-start(s16[480,128]{1,0:T(8,128)(2,1)S(1)} %get-tuple-element.30), channel_id=1, source_target_pairs={{0,12},{1,13},{2,14},{3,15},{4,8},{5,9},{6,10},{7,11},{8,4},{9,5},... | collective-permute-start | bytes 368648 | tf_op jit(solution)/shard_map/ppermute | solution.py:411
  47.1 5.0 %collective-permute-done.4 = bf16[2,464,128]{2,1,0:T(8,128)(2,1)S(1)} collective-permute-done((bf16[2,464,128]{2,1,0:T(8,128)(2,1)S(1)}, bf16[2,464,128]{2,1,0:T(8,128)(2,1)S(1)}, u32[]{:S(2)}, u32[]{:S(2)}) %collective-permute-start.4) | collective-permute-done | bytes 237600 | tf_op jit(solution)/shard_map/ppermute | solution.py:411
  52.1 1.7 %collective-permute-done.6.refs_2_ = s16[480,128]{1,0:T(8,128)(2,1)S(1)} collective-permute-done((s16[480,128]{1,0:T(8,128)(2,1)S(1)}, s16[480,128]{1,0:T(8,128)(2,1)S(1)}, u32[]{:S(2)}, u32[]{:S(2)}) %collective-permute-start.6) | collective-permute-done | bytes 122912 | tf_op jit(solution)/shard_map/ppermute | solution.py:411
  54.0 2.3 %collective-permute-start.9 = (s16[480,128]{1,0:T(8,128)(2,1)S(1)}, s16[480,128]{1,0:T(8,128)(2,1)S(1)}, u32[]{:S(2)}, u32[]{:S(2)}) collective-permute-start(s16[480,128]{1,0:T(8,128)(2,1)S(1)} %get-tuple-element.35), channel_id=1, source_target_pairs={{0,8},{1,9},{2,10},{3,11},{4,12},{5,13},{6,14},{7,15},{8,0},{9,1},... | collective-permute-start | bytes 368648 | tf_op jit(solution)/shard_map/ppermute | solution.py:411
  56.5 5.5 %input_term.1 = bf16[1024,320]{1,0:T(8,128)(2,1)} custom-call(s32[1]{0:T(128)} %bitcast.me_ref.packed_ref, s32[8,16]{1,0:T(8,128)S(1)} %bitcast.14, bf16[1024,320]{1,0:T(8,128)(2,1)S(1)} %bitcast.11, bf16[16,80,128]{2,1,0:T(8,128)(2,1)S(1)} %all-to-all-done.slots_ref, bf16[8,464,128]{2,1,0:T(8,128)(2,1)S(1)} %constant_dynamic-update-slice_fusion.mine_ref, ...), custom_call_target="tpu_custom_call" | custom-call | flops 1887436800 | bytes 6291456 | tf_op jit(solution)/shard_map/input_term/pallas_call | solution.py:501
  62.0 1.3 %collective-permute-done.9.refs_1_ = s16[480,128]{1,0:T(8,128)(2,1)S(1)} collective-permute-done((s16[480,128]{1,0:T(8,128)(2,1)S(1)}, s16[480,128]{1,0:T(8,128)(2,1)S(1)}, u32[]{:S(2)}, u32[]{:S(2)}) %collective-permute-start.9) | collective-permute-done | bytes 122912 | tf_op jit(solution)/shard_map/ppermute | solution.py:411
  63.3 0.8 %final_sum.1 = f32[450,128]{1,0:T(8,128)} custom-call(f32[480,128]{1,0:T(8,128)S(1)} %get-tuple-element.33.own_ref, s16[480,128]{1,0:T(8,128)(2,1)S(1)} %collective-permute-done.8.refs_0_, s16[480,128]{1,0:T(8,128)(2,1)S(1)} %collective-permute-done.9.refs_1_, s16[480,128]{1,0:T(8,128)(2,1)S(1)} %collective-permute-done.6.refs_2_), custom_call_target="tpu_custom_call" | custom-call | tf_op jit(solution)/shard_map/final_sum/pallas_call | solution.py:518
  (23 shorter events, 1.4 us)
Async XLA Ops:
  3.1 18.5 %copy-start.4 = (s32[16,8]{0,1:T(8,128)S(1)}, s32[16,8]{0,1:T(8,128)}, u32[]{:S(2)}) copy-start(s32[16,8]{0,1:T(8,128)} %param.8) | copy-start | bytes 1540
  3.1 18.5 %all-to-all-start = ((bf16[16,80,128]{2,1,0:T(8,128)(2,1)}), bf16[16,80,128]{2,1,0:T(8,128)(2,1)S(1)}, u32[]{:S(2)}, u32[]{:S(2)}) async-start(bf16[16,80,128]{2,1,0:T(8,128)(2,1)} %pack_borders.1), calls=%async_computation | async-start | bytes 655360 | tf_op jit(solution)/shard_map/all_to_all | solution.py:460
  11.4 9.3 %collective-permute-start = (bf16[1,464,128]{2,1,0:T(8,128)(2,1)S(1)}, bf16[1,464,128]{2,1,0:T(8,128)(2,1)S(1)}, u32[]{:S(2)}, u32[]{:S(2)}) collective-permute-start(bf16[1,464,128]{2,1,0:T(8,128)(2,1)S(1)} %get-tuple-element.36), channel_id=1, source_target_pairs={{0,2},{1,3},{2,0},{3,1},{4,6},{5,7},{6,4},{7,5},{8,10},{9,11},{10,... | collective-permute-start | bytes 356360 | tf_op jit(solution)/shard_map/ppermute | solution.py:411
  13.4 1.1 %copy-start.2 = (bf16[1,32,32,320]{3,2,1,0:T(8,128)(2,1)S(1)}, bf16[1,32,32,320]{3,2,1,0:T(8,128)(2,1)}, u32[]{:S(2)}) copy-start(bf16[1,32,32,320]{3,2,1,0:T(8,128)(2,1)} %param.6) | copy-start | bytes 1966084
  14.6 1.1 %copy-start.5 = (bf16[1,32,32,320]{3,2,1,0:T(8,128)(2,1)S(1)}, bf16[1,32,32,320]{3,2,1,0:T(8,128)(2,1)}, u32[]{:S(2)}) copy-start(bf16[1,32,32,320]{3,2,1,0:T(8,128)(2,1)} %param.5) | copy-start | bytes 1966084
  18.7 2.0 %copy-start = (f32[3,2880,128]{2,1,0:T(8,128)}, f32[3,2880,128]{2,1,0:T(8,128)S(1)}, u32[]{:S(2)}) copy-start(f32[3,2880,128]{2,1,0:T(8,128)S(1)} %get-tuple-element.23.inner_ref) | copy-start | bytes 13271044
  21.6 2.3 %copy-start.1 = (f32[3,2880,128]{2,1,0:T(8,128)S(1)}, f32[3,2880,128]{2,1,0:T(8,128)}, u32[]{:S(2)}) copy-start(f32[3,2880,128]{2,1,0:T(8,128)} %copy-done) | copy-start | bytes 13271044
  23.9 32.6 %copy-start.3 = (bf16[1,32,32,320]{3,2,1,0:T(8,128)(2,1)S(1)}, bf16[1,32,32,320]{3,2,1,0:T(8,128)(2,1)}, u32[]{:S(2)}) copy-start(bf16[1,32,32,320]{3,2,1,0:T(8,128)(2,1)} %param.6) | copy-start | bytes 1966084
  26.5 2.6 %collective-permute-start.3 = (s16[8,480,128]{2,1,0:T(8,128)(2,1)S(1)}, s16[8,480,128]{2,1,0:T(8,128)(2,1)S(1)}, u32[]{:S(2)}, u32[]{:S(2)}) collective-permute-start(s16[8,480,128]{2,1,0:T(8,128)(2,1)S(1)} %get-tuple-element.25), channel_id=1, source_target_pairs={{0,1},{1,0},{2,3},{3,2},{4,5},{5,4},{6,7},{7,6},{8,9},{9,8},{10,11... | collective-permute-start | bytes 2949128 | tf_op jit(solution)/shard_map/ppermute | solution.py:555
  29.6 15.1 %collective-permute-start.5 = (s16[4,480,128]{2,1,0:T(8,128)(2,1)S(1)}, s16[4,480,128]{2,1,0:T(8,128)(2,1)S(1)}, u32[]{:S(2)}, u32[]{:S(2)}) collective-permute-start(s16[4,480,128]{2,1,0:T(8,128)(2,1)S(1)} %get-tuple-element.26), channel_id=1, source_target_pairs={{0,2},{1,3},{2,0},{3,1},{4,6},{5,7},{6,4},{7,5},{8,10},{9,11},{10,... | collective-permute-start | bytes 1474568 | tf_op jit(solution)/shard_map/ppermute | solution.py:411
  30.1 12.2 %collective-permute-start.1 = (bf16[2,464,128]{2,1,0:T(8,128)(2,1)S(1)}, bf16[2,464,128]{2,1,0:T(8,128)(2,1)S(1)}, u32[]{:S(2)}, u32[]{:S(2)}) collective-permute-start(bf16[2,464,128]{2,1,0:T(8,128)(2,1)S(1)} %pad_maximum_fusion), channel_id=1, source_target_pairs={{0,4},{1,5},{2,6},{3,7},{4,0},{5,1},{6,2},{7,3},{8,12},{9,13},{10,... | collective-permute-start | bytes 712712 | tf_op jit(solution)/shard_map/ppermute | solution.py:411
  31.2 13.5 %collective-permute-start.2 = (bf16[2,464,128]{2,1,0:T(8,128)(2,1)S(1)}, bf16[2,464,128]{2,1,0:T(8,128)(2,1)S(1)}, u32[]{:S(2)}, u32[]{:S(2)}) collective-permute-start(bf16[2,464,128]{2,1,0:T(8,128)(2,1)S(1)} %pad_maximum_fusion), channel_id=1, source_target_pairs={{0,8},{1,9},{2,10},{3,11},{4,12},{5,13},{6,14},{7,15},{8,0},{9,1},... | collective-permute-start | bytes 712712 | tf_op jit(solution)/shard_map/ppermute | solution.py:411
  44.7 7.4 %collective-permute-start.4 = (bf16[2,464,128]{2,1,0:T(8,128)(2,1)S(1)}, bf16[2,464,128]{2,1,0:T(8,128)(2,1)S(1)}, u32[]{:S(2)}, u32[]{:S(2)}) collective-permute-start(bf16[2,464,128]{2,1,0:T(8,128)(2,1)S(1)} %collective-permute-done.2), channel_id=1, source_target_pairs={{0,4},{1,5},{2,6},{3,7},{4,0},{5,1},{6,2},{7,3},{8,12},{9,13},{10,... | collective-permute-start | bytes 712712 | tf_op jit(solution)/shard_map/ppermute | solution.py:411
  45.0 8.8 %collective-permute-start.6 = (s16[480,128]{1,0:T(8,128)(2,1)S(1)}, s16[480,128]{1,0:T(8,128)(2,1)S(1)}, u32[]{:S(2)}, u32[]{:S(2)}) collective-permute-start(s16[480,128]{1,0:T(8,128)(2,1)S(1)} %get-tuple-element.30), channel_id=1, source_target_pairs={{0,12},{1,13},{2,14},{3,15},{4,8},{5,9},{6,10},{7,11},{8,4},{9,5},... | collective-permute-start | bytes 368648 | tf_op jit(solution)/shard_map/ppermute | solution.py:411
  53.9 2.6 %collective-permute-start.7 = (bf16[8,464,128]{2,1,0:T(8,128)(2,1)S(1)}, bf16[8,464,128]{2,1,0:T(8,128)(2,1)S(1)}, u32[]{:S(2)}, u32[]{:S(2)}) collective-permute-start(bf16[8,464,128]{2,1,0:T(8,128)(2,1)S(1)} %constant_dynamic-update-slice_fusion.mine_ref), channel_id=1, source_target_pairs={{0,1},{1,0},{2,3},{3,2},{4,5},{5,4},{6,7},{7,6},{8,9},{9,8},{10,11... | collective-permute-start | bytes 2850824 | tf_op jit(solution)/shard_map/ppermute | solution.py:500
  54.0 8.0 %collective-permute-start.8 = (s16[480,128]{1,0:T(8,128)(2,1)S(1)}, s16[480,128]{1,0:T(8,128)(2,1)S(1)}, u32[]{:S(2)}, u32[]{:S(2)}) collective-permute-start(s16[480,128]{1,0:T(8,128)(2,1)S(1)} %get-tuple-element.34), channel_id=1, source_target_pairs={{0,4},{1,5},{2,6},{3,7},{4,0},{5,1},{6,2},{7,3},{8,12},{9,13},{10,... | collective-permute-start | bytes 368648 | tf_op jit(solution)/shard_map/ppermute | solution.py:411
  54.0 9.2 %collective-permute-start.9 = (s16[480,128]{1,0:T(8,128)(2,1)S(1)}, s16[480,128]{1,0:T(8,128)(2,1)S(1)}, u32[]{:S(2)}, u32[]{:S(2)}) collective-permute-start(s16[480,128]{1,0:T(8,128)(2,1)S(1)} %get-tuple-element.35), channel_id=1, source_target_pairs={{0,8},{1,9},{2,10},{3,11},{4,12},{5,13},{6,14},{7,15},{8,0},{9,1},... | collective-permute-start | bytes 368648 | tf_op jit(solution)/shard_map/ppermute | solution.py:411

commit v5 on v4

--- a/solution.py
+++ b/solution.py
@@ -313,13 +313,14 @@
 
 
 def final_sum(pairs, scale, own_ref, *refs):
-    got_refs, out_ref = refs[:-1], refs[-1]
+    got_refs, out_ref, rows_ref = refs[:-2], refs[-2], refs[-1]
     total = own_ref[...]
     for got_ref in got_refs:
         total = total + read_coded(got_ref[...], pairs)
     total = total * scale
     for group in range(5):
-        out_ref[pl.ds(group, pairs, stride=5), :] = total[group * GROUP : group * GROUP + pairs]
+        rows_ref[pl.ds(group, GROUP, stride=5), :] = total[group * GROUP : (group + 1) * GROUP]
+    out_ref[...] = rows_ref[: out_ref.shape[0]]
 
 
 def unpack_kernel(pairs, chips, me_ref, mine_ref, other_ref, shard_ref, rows_ref):
@@ -334,7 +335,7 @@
             base = shard * 2 * pairs
             even = pl.ds(base, pairs, stride=2)
             odd = pl.ds(base + 1, pairs, stride=2)
-            shard_ref[turn] = source_ref[offset].astype(jnp.float32)[: 5 * pairs]
+            shard_ref[turn, : source_ref.shape[1]] = source_ref[offset].astype(jnp.float32)
             parts = [shard_ref[turn, pl.ds(group, pairs, stride=5), :] for group in range(5)]
             turned = [pltpu.roll(part, half, 1) for part in parts[2:]]
             rows_ref[0, even] = parts[0]
@@ -426,6 +427,7 @@
     slot = (5 * side // 2, LANES)
     shifted = [pltpu.VMEM((pixels + 2 * side, 3 * lanes), jnp.bfloat16)]
     sums = (3, 9 * width, LANES)
+    padded_sums = (3, 9 * width + 16, LANES)
     even = count == 16 and whole % (2 * width * count) == 0
     pairs = whole // (2 * width * count)
     message = (5 * GROUP, LANES)
@@ -485,7 +487,7 @@
             in_specs=[SMEM, SMEM, VMEM, VMEM, VMEM],
             out_specs=(VMEM,) * 2,
             scratch_shapes=[
-                pltpu.VMEM(sums, jnp.float32),
+                pltpu.VMEM(padded_sums, jnp.float32),
                 pltpu.VMEM((2,) + message, jnp.float32),
             ],
             compiler_params=params(20),
@@ -505,8 +507,8 @@
             out_specs=VMEM,
             scratch_shapes=[
                 pltpu.VMEM((3 * width, 3 * lanes), jnp.bfloat16),
-                pltpu.VMEM((2, 5 * pairs, LANES), jnp.float32),
-                pltpu.VMEM(sums, jnp.float32),
+                pltpu.VMEM((2, 5 * GROUP, LANES), jnp.float32),
+                pltpu.VMEM(padded_sums, jnp.float32),
             ]
             + shifted,
             compiler_params=params(26),
@@ -520,6 +522,7 @@
             out_shape=jax.ShapeDtypeStruct((5 * pairs, LANES), jnp.float32),
             in_specs=[VMEM] * (count // 4),
             out_specs=VMEM,
+            scratch_shapes=[pltpu.VMEM(message, jnp.float32)],
             compiler_params=params(8),
             name="final_sum",
         )(after(own, input_grad), *got).reshape(-1)

time: 64.4 us -> 64.5 us (level)
  no operation moved by 1% of the time
where the time goes in v5:
time: 64.5 us; the launch traced here: 64.1 us
  waiting for transfers between devices  22.9 us (36%)
  starting transfers between devices  17.6 us (27%)
  Pallas kernels  15.3 us (24%)
  local copies, waits for them, and re-layouts  7.6 us (12%)
  between operations  0.76 us (1%)
    ppermute x8, waiting for transfers between devices, from_offset(): lax.ppermute(value, 'tile', [(i, i ^ 2 * offset) for i in range(count)])  19.5 us
    ppermute x8, starting transfers between devices, from_offset(): lax.ppermute(value, 'tile', [(i, i ^ 2 * offset) for i in range(count)])  9.97 us
    all_to_all x1, starting transfers between devices, per_device(): slots = lax.all_to_all(slots, 'tile', 0, 0, tiled=True)  7.37 us
    unnamed x15, local copies, waits for them, and re-layouts  6.63 us
    pallas_call x1, Pallas kernels, per_device(): pl.pallas_call(functools.partial(input_term, side, width, pairs, chips),...  5.51 us
    pallas_call x1, Pallas kernels, per_device(): pl.pallas_call(functools.partial(inner_term, side, width), out_shape=(jax...  3 us
    pallas_call x1, Pallas kernels, per_device(): pl.pallas_call(functools.partial(rim_term, side, width, chips, pairs), ou...  2.59 us
    pallas_call x1, Pallas kernels, per_device(): pl.pallas_call(functools.partial(pack_borders, side, count), out_shape=ja...  2.48 us
  transfers between devices with their start and end apart: 11, of which 8 were waited for; matrix products, arithmetic and copies ran while one was open for 2% of the time, Pallas kernels for 14%

profile of v5, /device:TPU:0, one launch (start us, length us, event | category | flops | bytes accessed | tf_op | source)
XLA Modules:
  0.0 64.1 jit_solution(13693519901375141332)
XLA Ops:
  0.6 2.5 %pack_borders.1 = bf16[16,80,128]{2,1,0:T(8,128)(2,1)} custom-call(s32[1]{0:T(128)} %bitcast.me_ref.packed_ref, s32[8,16]{1,0:T(8,128)} %bitcast.12, s32[8,16]{1,0:T(8,128)} %bitcast.18, bf16[32,32,320]{2,1,0:T(8,128)(2,1)} %bitcast.9), custom_call_target="tpu_custom_call" | custom-call | tf_op jit(solution)/shard_map/pack_borders/pallas_call | solution.py:438
  3.1 7.4 %all-to-all-start = ((bf16[16,80,128]{2,1,0:T(8,128)(2,1)}), bf16[16,80,128]{2,1,0:T(8,128)(2,1)S(1)}, u32[]{:S(2)}, u32[]{:S(2)}) async-start(bf16[16,80,128]{2,1,0:T(8,128)(2,1)} %pack_borders.1), calls=%async_computation | async-start | bytes 655360 | tf_op jit(solution)/shard_map/all_to_all | solution.py:462
  10.5 0.9 %fusion = (bf16[1,464,128]{2,1,0:T(8,128)(2,1)S(1)}, bf16[8,464,128]{2,1,0:T(8,128)(2,1)S(1)}) fusion(bf16[1,450,128]{2,1,0:T(8,128)(2,1)} %bitcast.17), kind=kLoop, calls=%fused_computation.6 | loop fusion | bytes 352768 | tf_op jit(solution)/shard_map/jit(_pad)/pad | solution.py:460
  11.4 2.0 %collective-permute-start = (bf16[1,464,128]{2,1,0:T(8,128)(2,1)S(1)}, bf16[1,464,128]{2,1,0:T(8,128)(2,1)S(1)}, u32[]{:S(2)}, u32[]{:S(2)}) collective-permute-start(bf16[1,464,128]{2,1,0:T(8,128)(2,1)S(1)} %get-tuple-element.36), channel_id=1, source_target_pairs={{0,2},{1,3},{2,0},{3,1},{4,6},{5,7},{6,4},{7,5},{8,10},{9,11},{10,... | collective-permute-start | bytes 356360 | tf_op jit(solution)/shard_map/ppermute | solution.py:412
  13.4 1.1 %copy-done.2 = bf16[1,32,32,320]{3,2,1,0:T(8,128)(2,1)S(1)} copy-done((bf16[1,32,32,320]{3,2,1,0:T(8,128)(2,1)S(1)}, bf16[1,32,32,320]{3,2,1,0:T(8,128)(2,1)}, u32[]{:S(2)}) %copy-start.2) | copy-done | bytes 655384
  14.6 1.1 %copy-done.5 = bf16[1,32,32,320]{3,2,1,0:T(8,128)(2,1)S(1)} copy-done((bf16[1,32,32,320]{3,2,1,0:T(8,128)(2,1)S(1)}, bf16[1,32,32,320]{3,2,1,0:T(8,128)(2,1)}, u32[]{:S(2)}) %copy-start.5) | copy-done | bytes 655384
  15.7 3.0 %inner_term.1 = (f32[3,2880,128]{2,1,0:T(8,128)S(1)}, bf16[320,128]{1,0:T(8,128)(2,1)S(1)}) custom-call(s32[1]{0:T(128)} %bitcast.me_ref.packed_ref, bf16[1024,320]{1,0:T(8,128)(2,1)S(1)} %bitcast.15, bf16[1024,320]{1,0:T(8,128)(2,1)S(1)} %bitcast.10), custom_call_target="tpu_custom_call" | custom-call | flops 1887436800 | bytes 6291456 | tf_op jit(solution)/shard_map/inner_term/pallas_call | solution.py:464
  18.7 2.0 %copy-done = f32[3,2880,128]{2,1,0:T(8,128)} copy-done((f32[3,2880,128]{2,1,0:T(8,128)}, f32[3,2880,128]{2,1,0:T(8,128)S(1)}, u32[]{:S(2)}) %copy-start) | copy-done | bytes 4423704
  20.8 0.8 %all-to-all-done.slots_ref = bf16[16,80,128]{2,1,0:T(8,128)(2,1)S(1)} async-done(((bf16[16,80,128]{2,1,0:T(8,128)(2,1)}), bf16[16,80,128]{2,1,0:T(8,128)(2,1)S(1)}, u32[]{:S(2)}, u32[]{:S(2)}) %all-to-all-start) | async-done | bytes 327712 | tf_op jit(solution)/shard_map/all_to_all | solution.py:462
  21.6 2.3 %copy-done.1 = f32[3,2880,128]{2,1,0:T(8,128)S(1)} copy-done((f32[3,2880,128]{2,1,0:T(8,128)S(1)}, f32[3,2880,128]{2,1,0:T(8,128)}, u32[]{:S(2)}) %copy-start.1) | copy-done | bytes 4423704
  23.9 2.6 %rim_term.1 = (f32[8,480,128]{2,1,0:T(8,128)S(1)}, s16[8,480,128]{2,1,0:T(8,128)(2,1)S(1)}) custom-call(s32[1]{0:T(128)} %bitcast.me_ref.packed_ref, s32[8,16]{1,0:T(8,128)S(1)} %bitcast.13, bf16[320,128]{1,0:T(8,128)(2,1)S(1)} %get-tuple-element.22.edge_ref, bf16[16,80,128]{2,1,0:T(8,128)(2,1)S(1)} %all-to-all-done.slots_ref, f32[3,2880,128]{2,1,0:T(8,128)S(1)} %copy-done.1), custom_call_target="tpu_custom_call" | custom-call | tf_op jit(solution)/shard_map/rim_term/pallas_call | solution.py:481
  26.6 2.5 %collective-permute-done.3.got_ref = s16[8,480,128]{2,1,0:T(8,128)(2,1)S(1)} collective-permute-done((s16[8,480,128]{2,1,0:T(8,128)(2,1)S(1)}, s16[8,480,128]{2,1,0:T(8,128)(2,1)S(1)}, u32[]{:S(2)}, u32[]{:S(2)}) %collective-permute-start.3) | collective-permute-done | bytes 983072 | tf_op jit(solution)/shard_map/ppermute | solution.py:558
  29.1 0.5 pair_sum.1
  30.1 1.1 %collective-permute-start.1 = (bf16[2,464,128]{2,1,0:T(8,128)(2,1)S(1)}, bf16[2,464,128]{2,1,0:T(8,128)(2,1)S(1)}, u32[]{:S(2)}, u32[]{:S(2)}) collective-permute-start(bf16[2,464,128]{2,1,0:T(8,128)(2,1)S(1)} %pad_maximum_fusion), channel_id=1, source_target_pairs={{0,4},{1,5},{2,6},{3,7},{4,0},{5,1},{6,2},{7,3},{8,12},{9,13},{10,... | collective-permute-start | bytes 712712 | tf_op jit(solution)/shard_map/ppermute | solution.py:412
  31.2 2.1 %collective-permute-start.2 = (bf16[2,464,128]{2,1,0:T(8,128)(2,1)S(1)}, bf16[2,464,128]{2,1,0:T(8,128)(2,1)S(1)}, u32[]{:S(2)}, u32[]{:S(2)}) collective-permute-start(bf16[2,464,128]{2,1,0:T(8,128)(2,1)S(1)} %pad_maximum_fusion), channel_id=1, source_target_pairs={{0,8},{1,9},{2,10},{3,11},{4,12},{5,13},{6,14},{7,15},{8,0},{9,1},... | collective-permute-start | bytes 712712 | tf_op jit(solution)/shard_map/ppermute | solution.py:412
  33.3 9.0 %collective-permute-done.1 = bf16[2,464,128]{2,1,0:T(8,128)(2,1)S(1)} collective-permute-done((bf16[2,464,128]{2,1,0:T(8,128)(2,1)S(1)}, bf16[2,464,128]{2,1,0:T(8,128)(2,1)S(1)}, u32[]{:S(2)}, u32[]{:S(2)}) %collective-permute-start.1) | collective-permute-done | bytes 237600 | tf_op jit(solution)/shard_map/ppermute | solution.py:412
  42.3 2.4 %collective-permute-done.2 = bf16[2,464,128]{2,1,0:T(8,128)(2,1)S(1)} collective-permute-done((bf16[2,464,128]{2,1,0:T(8,128)(2,1)S(1)}, bf16[2,464,128]{2,1,0:T(8,128)(2,1)S(1)}, u32[]{:S(2)}, u32[]{:S(2)}) %collective-permute-start.2) | collective-permute-done | bytes 237600 | tf_op jit(solution)/shard_map/ppermute | solution.py:412
  45.0 2.0 %collective-permute-start.6 = (s16[480,128]{1,0:T(8,128)(2,1)S(1)}, s16[480,128]{1,0:T(8,128)(2,1)S(1)}, u32[]{:S(2)}, u32[]{:S(2)}) collective-permute-start(s16[480,128]{1,0:T(8,128)(2,1)S(1)} %get-tuple-element.30), channel_id=1, source_target_pairs={{0,12},{1,13},{2,14},{3,15},{4,8},{5,9},{6,10},{7,11},{8,4},{9,5},... | collective-permute-start | bytes 368648 | tf_op jit(solution)/shard_map/ppermute | solution.py:412
  47.1 5.0 %collective-permute-done.4 = bf16[2,464,128]{2,1,0:T(8,128)(2,1)S(1)} collective-permute-done((bf16[2,464,128]{2,1,0:T(8,128)(2,1)S(1)}, bf16[2,464,128]{2,1,0:T(8,128)(2,1)S(1)}, u32[]{:S(2)}, u32[]{:S(2)}) %collective-permute-start.4) | collective-permute-done | bytes 237600 | tf_op jit(solution)/shard_map/ppermute | solution.py:412
  52.1 1.7 %collective-permute-done.6.refs_2_ = s16[480,128]{1,0:T(8,128)(2,1)S(1)} collective-permute-done((s16[480,128]{1,0:T(8,128)(2,1)S(1)}, s16[480,128]{1,0:T(8,128)(2,1)S(1)}, u32[]{:S(2)}, u32[]{:S(2)}) %collective-permute-start.6) | collective-permute-done | bytes 122912 | tf_op jit(solution)/shard_map/ppermute | solution.py:412
  54.0 2.3 %collective-permute-start.9 = (s16[480,128]{1,0:T(8,128)(2,1)S(1)}, s16[480,128]{1,0:T(8,128)(2,1)S(1)}, u32[]{:S(2)}, u32[]{:S(2)}) collective-permute-start(s16[480,128]{1,0:T(8,128)(2,1)S(1)} %get-tuple-element.35), channel_id=1, source_target_pairs={{0,8},{1,9},{2,10},{3,11},{4,12},{5,13},{6,14},{7,15},{8,0},{9,1},... | collective-permute-start | bytes 368648 | tf_op jit(solution)/shard_map/ppermute | solution.py:412
  56.5 5.5 %input_term.1 = bf16[1024,320]{1,0:T(8,128)(2,1)} custom-call(s32[1]{0:T(128)} %bitcast.me_ref.packed_ref, s32[8,16]{1,0:T(8,128)S(1)} %bitcast.14, bf16[1024,320]{1,0:T(8,128)(2,1)S(1)} %bitcast.11, bf16[16,80,128]{2,1,0:T(8,128)(2,1)S(1)} %all-to-all-done.slots_ref, bf16[8,464,128]{2,1,0:T(8,128)(2,1)S(1)} %constant_dynamic-update-slice_fusion.mine_ref, ...), custom_call_target="tpu_custom_call" | custom-call | flops 1887436800 | bytes 6291456 | tf_op jit(solution)/shard_map/input_term/pallas_call | solution.py:503
  62.0 1.3 %collective-permute-done.9.refs_1_ = s16[480,128]{1,0:T(8,128)(2,1)S(1)} collective-permute-done((s16[480,128]{1,0:T(8,128)(2,1)S(1)}, s16[480,128]{1,0:T(8,128)(2,1)S(1)}, u32[]{:S(2)}, u32[]{:S(2)}) %collective-permute-start.9) | collective-permute-done | bytes 122912 | tf_op jit(solution)/shard_map/ppermute | solution.py:412
  63.3 0.9 %final_sum.1 = f32[450,128]{1,0:T(8,128)} custom-call(f32[480,128]{1,0:T(8,128)S(1)} %get-tuple-element.33.own_ref, s16[480,128]{1,0:T(8,128)(2,1)S(1)} %collective-permute-done.8.refs_0_, s16[480,128]{1,0:T(8,128)(2,1)S(1)} %collective-permute-done.9.refs_1_, s16[480,128]{1,0:T(8,128)(2,1)S(1)} %collective-permute-done.6.refs_2_), custom_call_target="tpu_custom_call" | custom-call | tf_op jit(solution)/shard_map/final_sum/pallas_call | solution.py:520
  (23 shorter events, 1.4 us)
Async XLA Ops:
  3.1 18.5 %copy-start.4 = (s32[16,8]{0,1:T(8,128)S(1)}, s32[16,8]{0,1:T(8,128)}, u32[]{:S(2)}) copy-start(s32[16,8]{0,1:T(8,128)} %param.8) | copy-start | bytes 1540
  3.1 18.5 %all-to-all-start = ((bf16[16,80,128]{2,1,0:T(8,128)(2,1)}), bf16[16,80,128]{2,1,0:T(8,128)(2,1)S(1)}, u32[]{:S(2)}, u32[]{:S(2)}) async-start(bf16[16,80,128]{2,1,0:T(8,128)(2,1)} %pack_borders.1), calls=%async_computation | async-start | bytes 655360 | tf_op jit(solution)/shard_map/all_to_all | solution.py:462
  11.4 9.3 %collective-permute-start = (bf16[1,464,128]{2,1,0:T(8,128)(2,1)S(1)}, bf16[1,464,128]{2,1,0:T(8,128)(2,1)S(1)}, u32[]{:S(2)}, u32[]{:S(2)}) collective-permute-start(bf16[1,464,128]{2,1,0:T(8,128)(2,1)S(1)} %get-tuple-element.36), channel_id=1, source_target_pairs={{0,2},{1,3},{2,0},{3,1},{4,6},{5,7},{6,4},{7,5},{8,10},{9,11},{10,... | collective-permute-start | bytes 356360 | tf_op jit(solution)/shard_map/ppermute | solution.py:412
  13.4 1.1 %copy-start.2 = (bf16[1,32,32,320]{3,2,1,0:T(8,128)(2,1)S(1)}, bf16[1,32,32,320]{3,2,1,0:T(8,128)(2,1)}, u32[]{:S(2)}) copy-start(bf16[1,32,32,320]{3,2,1,0:T(8,128)(2,1)} %param.6) | copy-start | bytes 1966084
  14.6 1.1 %copy-start.5 = (bf16[1,32,32,320]{3,2,1,0:T(8,128)(2,1)S(1)}, bf16[1,32,32,320]{3,2,1,0:T(8,128)(2,1)}, u32[]{:S(2)}) copy-start(bf16[1,32,32,320]{3,2,1,0:T(8,128)(2,1)} %param.5) | copy-start | bytes 1966084
  18.7 2.0 %copy-start = (f32[3,2880,128]{2,1,0:T(8,128)}, f32[3,2880,128]{2,1,0:T(8,128)S(1)}, u32[]{:S(2)}) copy-start(f32[3,2880,128]{2,1,0:T(8,128)S(1)} %get-tuple-element.23.inner_ref) | copy-start | bytes 13271044
  21.6 2.3 %copy-start.1 = (f32[3,2880,128]{2,1,0:T(8,128)S(1)}, f32[3,2880,128]{2,1,0:T(8,128)}, u32[]{:S(2)}) copy-start(f32[3,2880,128]{2,1,0:T(8,128)} %copy-done) | copy-start | bytes 13271044
  23.9 32.6 %copy-start.3 = (bf16[1,32,32,320]{3,2,1,0:T(8,128)(2,1)S(1)}, bf16[1,32,32,320]{3,2,1,0:T(8,128)(2,1)}, u32[]{:S(2)}) copy-start(bf16[1,32,32,320]{3,2,1,0:T(8,128)(2,1)} %param.6) | copy-start | bytes 1966084
  26.5 2.6 %collective-permute-start.3 = (s16[8,480,128]{2,1,0:T(8,128)(2,1)S(1)}, s16[8,480,128]{2,1,0:T(8,128)(2,1)S(1)}, u32[]{:S(2)}, u32[]{:S(2)}) collective-permute-start(s16[8,480,128]{2,1,0:T(8,128)(2,1)S(1)} %get-tuple-element.25), channel_id=1, source_target_pairs={{0,1},{1,0},{2,3},{3,2},{4,5},{5,4},{6,7},{7,6},{8,9},{9,8},{10,11... | collective-permute-start | bytes 2949128 | tf_op jit(solution)/shard_map/ppermute | solution.py:558
  29.6 15.1 %collective-permute-start.5 = (s16[4,480,128]{2,1,0:T(8,128)(2,1)S(1)}, s16[4,480,128]{2,1,0:T(8,128)(2,1)S(1)}, u32[]{:S(2)}, u32[]{:S(2)}) collective-permute-start(s16[4,480,128]{2,1,0:T(8,128)(2,1)S(1)} %get-tuple-element.26), channel_id=1, source_target_pairs={{0,2},{1,3},{2,0},{3,1},{4,6},{5,7},{6,4},{7,5},{8,10},{9,11},{10,... | collective-permute-start | bytes 1474568 | tf_op jit(solution)/shard_map/ppermute | solution.py:412
  30.1 12.2 %collective-permute-start.1 = (bf16[2,464,128]{2,1,0:T(8,128)(2,1)S(1)}, bf16[2,464,128]{2,1,0:T(8,128)(2,1)S(1)}, u32[]{:S(2)}, u32[]{:S(2)}) collective-permute-start(bf16[2,464,128]{2,1,0:T(8,128)(2,1)S(1)} %pad_maximum_fusion), channel_id=1, source_target_pairs={{0,4},{1,5},{2,6},{3,7},{4,0},{5,1},{6,2},{7,3},{8,12},{9,13},{10,... | collective-permute-start | bytes 712712 | tf_op jit(solution)/shard_map/ppermute | solution.py:412
  31.2 13.5 %collective-permute-start.2 = (bf16[2,464,128]{2,1,0:T(8,128)(2,1)S(1)}, bf16[2,464,128]{2,1,0:T(8,128)(2,1)S(1)}, u32[]{:S(2)}, u32[]{:S(2)}) collective-permute-start(bf16[2,464,128]{2,1,0:T(8,128)(2,1)S(1)} %pad_maximum_fusion), channel_id=1, source_target_pairs={{0,8},{1,9},{2,10},{3,11},{4,12},{5,13},{6,14},{7,15},{8,0},{9,1},... | collective-permute-start | bytes 712712 | tf_op jit(solution)/shard_map/ppermute | solution.py:412
  44.7 7.4 %collective-permute-start.4 = (bf16[2,464,128]{2,1,0:T(8,128)(2,1)S(1)}, bf16[2,464,128]{2,1,0:T(8,128)(2,1)S(1)}, u32[]{:S(2)}, u32[]{:S(2)}) collective-permute-start(bf16[2,464,128]{2,1,0:T(8,128)(2,1)S(1)} %collective-permute-done.2), channel_id=1, source_target_pairs={{0,4},{1,5},{2,6},{3,7},{4,0},{5,1},{6,2},{7,3},{8,12},{9,13},{10,... | collective-permute-start | bytes 712712 | tf_op jit(solution)/shard_map/ppermute | solution.py:412
  45.0 8.8 %collective-permute-start.6 = (s16[480,128]{1,0:T(8,128)(2,1)S(1)}, s16[480,128]{1,0:T(8,128)(2,1)S(1)}, u32[]{:S(2)}, u32[]{:S(2)}) collective-permute-start(s16[480,128]{1,0:T(8,128)(2,1)S(1)} %get-tuple-element.30), channel_id=1, source_target_pairs={{0,12},{1,13},{2,14},{3,15},{4,8},{5,9},{6,10},{7,11},{8,4},{9,5},... | collective-permute-start | bytes 368648 | tf_op jit(solution)/shard_map/ppermute | solution.py:412
  53.9 2.6 %collective-permute-start.7 = (bf16[8,464,128]{2,1,0:T(8,128)(2,1)S(1)}, bf16[8,464,128]{2,1,0:T(8,128)(2,1)S(1)}, u32[]{:S(2)}, u32[]{:S(2)}) collective-permute-start(bf16[8,464,128]{2,1,0:T(8,128)(2,1)S(1)} %constant_dynamic-update-slice_fusion.mine_ref), channel_id=1, source_target_pairs={{0,1},{1,0},{2,3},{3,2},{4,5},{5,4},{6,7},{7,6},{8,9},{9,8},{10,11... | collective-permute-start | bytes 2850824 | tf_op jit(solution)/shard_map/ppermute | solution.py:502
  54.0 8.0 %collective-permute-start.8 = (s16[480,128]{1,0:T(8,128)(2,1)S(1)}, s16[480,128]{1,0:T(8,128)(2,1)S(1)}, u32[]{:S(2)}, u32[]{:S(2)}) collective-permute-start(s16[480,128]{1,0:T(8,128)(2,1)S(1)} %get-tuple-element.34), channel_id=1, source_target_pairs={{0,4},{1,5},{2,6},{3,7},{4,0},{5,1},{6,2},{7,3},{8,12},{9,13},{10,... | collective-permute-start | bytes 368648 | tf_op jit(solution)/shard_map/ppermute | solution.py:412
  54.0 9.2 %collective-permute-start.9 = (s16[480,128]{1,0:T(8,128)(2,1)S(1)}, s16[480,128]{1,0:T(8,128)(2,1)S(1)}, u32[]{:S(2)}, u32[]{:S(2)}) collective-permute-start(s16[480,128]{1,0:T(8,128)(2,1)S(1)} %get-tuple-element.35), channel_id=1, source_target_pairs={{0,8},{1,9},{2,10},{3,11},{4,12},{5,13},{6,14},{7,15},{8,0},{9,1},... | collective-permute-start | bytes 368648 | tf_op jit(solution)/shard_map/ppermute | solution.py:412
